TPU v7x, 32 devices: a whole 2x2x4 slice. The times are simulated.
32 devices in a mesh: dp: 8 (over y, x, core), tensor: 4 (over z).
Axes of the slice: x: 2, y: 2, z: 4, core: 2. Of those that a mesh axis runs over, the one named last changes fastest.
Arguments:
- x_in: bfloat16 [16384, 1536], P(('dp', 'tensor')), may hold values from -6 to 6
- segment_ids: int32 [16, 1024], P('dp'), may hold values from 0 to 11, never falling along the last dimension, each value on 1 to 512 neighbouring positions
- norm_gain: bfloat16 [1536], P('dp'), may hold values from 0.099609375 to 1.8984375
- w_x: bfloat16 [1536, 3072], P('dp', 'tensor'), may hold values from -0.15625 to 0.15625
- w_z: bfloat16 [1536, 3072], P('dp', 'tensor'), may hold values from -0.15625 to 0.15625
- w_bc: bfloat16 [1536, 256], P('dp'), may hold values from -0.15625 to 0.15625
- w_dt: bfloat16 [1536, 48], P('dp', 'tensor'), may hold values from -0.15625 to 0.15625
- conv_x: float32 [4, 3072], P(None, 'tensor'), may hold values from -3 to 3
- conv_x_bias: float32 [3072], P('tensor'), may hold values from -3 to 3
- conv_bc: float32 [4, 256], replicated, may hold values from -3 to 3
- conv_bc_bias: float32 [256], replicated, may hold values from -3 to 3
- dt_bias: float32 [48], P('tensor'), may hold values from -6 to -2
- a_log: float32 [48], P('tensor'), may hold values from 0 to 2.77
- d_skip: float32 [48], P('tensor'), may hold values from 0.5 to 1.5
- gate_gain: float32 [3072], P('tensor'), may hold values from 0.1 to 1.9
- w_out: bfloat16 [3072, 1536], P('tensor', 'dp'), may hold values from -0.109375 to 0.109375
- cotangent: bfloat16 [16384, 1536], P(('dp', 'tensor')), may hold values from -6 to 6
Outputs:
- block_out: bfloat16 [16384, 1536], P(('dp', 'tensor'))
- x_grad: float32 [16384, 1536], P(('dp', 'tensor'))
- norm_gain_grad: float32 [1536], P('dp')
- w_x_grad: float32 [1536, 3072], P('dp', 'tensor')
- w_z_grad: float32 [1536, 3072], P('dp', 'tensor')
- w_bc_grad: float32 [1536, 256], P('dp')
- w_dt_grad: float32 [1536, 48], P('dp', 'tensor')
- conv_x_grad: float32 [4, 3072], P(None, 'tensor')
- conv_x_bias_grad: float32 [3072], P('tensor')
- conv_bc_grad: float32 [4, 256], replicated
- conv_bc_bias_grad: float32 [256], replicated
- dt_bias_grad: float32 [48], P('tensor')
- a_log_grad: float32 [48], P('tensor')
- d_skip_grad: float32 [48], P('tensor')
- gate_gain_grad: float32 [3072], P('tensor')
- w_out_grad: float32 [3072, 1536], P('tensor', 'dp')
Inputs may be any that keep to these rules, and one draw needn't show every extreme that they name: `segment_ids`: within each sequence the document numbers never fall; every document has 1 to 512 tokens and one of each sequence has exactly 512.
All inputs are finite; a program needn't handle non-finite values.
Results may differ from a plain program's by a relative error of at most 0.017.
Values may be sent and summed in bfloat16 or wider, within the bound.
No kernel may reach another device: no remote copies, remote signals or barrier semaphores. Data moves between devices by JAX's collectives and lax.ppermute only.
A program may use at most 256 MiB of HBM per device.

v0:
```python
from functools import partial

import jax
import jax.numpy as jnp
from jax import lax
from jax.sharding import PartitionSpec as P

CH = 256


epsilon = 1e-05
highest = lax.Precision.HIGHEST


def conv_reset(values, segments, weights, biases):
    length = values.shape[1]
    running_sum = biases + weights[0] * values
    for shift_by in range(1, weights.shape[0]):
        shifted = jnp.pad(values, ((0, 0), (shift_by, 0), (0, 0)))[:, :length]
        shifted_ids = jnp.pad(segments, ((0, 0), (shift_by, 0)), constant_values=-1)[:, :length]
        valid_tap = (shifted_ids == segments).astype(values.dtype)
        running_sum = running_sum + weights[shift_by] * shifted * valid_tap[:, :, None]
    return running_sum


def block_step(carry, item):
    state_mat, previous = carry
    values, step_sizes, b_rows, c_rows, doc_ids, decay_rate = item
    log_decay = step_sizes * decay_rate[None, :]
    running = jnp.cumsum(log_decay, axis=0)
    positions = jnp.arange(doc_ids.shape[0])
    same_doc = (doc_ids[:, None] == doc_ids[None, :]) & (positions[:, None] >= positions[None, :])
    log_gaps = running.T[:, :, None] - running.T[:, None, :]
    log_gaps = jnp.where(same_doc[None], log_gaps, 0.0)
    decay_mat = jnp.exp(log_gaps) * same_doc[None].astype(values.dtype)
    scores = jnp.dot(c_rows, b_rows.T, precision=highest, preferred_element_type=jnp.float32)
    mixing = scores[None] * decay_mat * step_sizes.T[:, None, :]
    inner_part = jnp.einsum("hts,shp->thp", mixing, values, precision=highest)
    carried = (doc_ids == previous).astype(values.dtype)
    from_state = jnp.einsum("tn,hpn->thp", c_rows, state_mat, precision=highest)
    outer_part = from_state * (carried[:, None] * jnp.exp(running))[:, :, None]
    final_log = running[-1]
    keep_end = (doc_ids == doc_ids[-1]).astype(values.dtype)
    weights_end = jnp.exp(final_log[None, :] - running) * step_sizes * keep_end[:, None]
    update = jnp.einsum("sh,shp,sn->hpn", weights_end, values, b_rows, precision=highest)
    still_open = (doc_ids[-1] == previous).astype(values.dtype)
    new_state = still_open * jnp.exp(final_log)[:, None, None] * state_mat + update
    return ((new_state, doc_ids[-1]), inner_part + outer_part)


def block_scan(values, step_sizes, decay_rate, b_rows, c_rows, doc_ids, block_len):
    length, head_count, head_size = values.shape
    state_size = b_rows.shape[1]
    block_count = length // block_len
    items = (
        values.reshape(block_count, block_len, head_count, head_size),
        step_sizes.reshape(block_count, block_len, head_count),
        b_rows.reshape(block_count, block_len, state_size),
        c_rows.reshape(block_count, block_len, state_size),
        doc_ids.reshape(block_count, block_len),
    )

    def step_with_rate(carry, item):
        return block_step(carry, item + (decay_rate,))

    start_state = (
        jnp.zeros((head_count, head_size, state_size), values.dtype),
        jnp.array(-1, dtype=jnp.int32),
    )
    final_carry, pieces = lax.scan(jax.checkpoint(step_with_rate), start_state, items)
    return pieces.reshape(length, head_count, head_size)


def bc_branch(bc_proj, conv_bc, conv_bc_bias, segments):
    seq_count, length = segments.shape
    widths = bc_proj.shape[1]
    bc_seq = conv_reset(bc_proj.reshape(seq_count, length, widths), segments, conv_bc, conv_bc_bias)
    return jax.nn.silu(bc_seq).reshape(seq_count * length, widths)


def mix_heads(
    x_proj, bc_act, dt_proj, conv_x, conv_x_bias, dt_bias, a_log, d_skip, segments, block_len
):
    seq_count, length = segments.shape
    channels = x_proj.shape[1]
    head_count = dt_proj.shape[1]
    head_size = channels // head_count
    state_size = bc_act.shape[1] // 2
    x_act = jax.nn.silu(
        conv_reset(x_proj.reshape(seq_count, length, channels), segments, conv_x, conv_x_bias)
    )
    values = x_act.reshape(seq_count, length, head_count, head_size)
    step_sizes = jax.nn.softplus(dt_proj + dt_bias).reshape(seq_count, length, head_count)
    decay_rate = -jnp.exp(a_log)
    bc_seq = bc_act.reshape(seq_count, length, 2 * state_size)
    scanner = jax.vmap(partial(block_scan, block_len=block_len), in_axes=(0, 0, None, 0, 0, 0))
    scanned = scanner(
        values,
        step_sizes,
        decay_rate,
        bc_seq[:, :, :state_size],
        bc_seq[:, :, state_size:],
        segments,
    )
    result = scanned + d_skip[None, None, :, None] * values
    return result.reshape(seq_count * length, channels)


def rows_times(left, right):
    return lax.dot_general(
        left, right, (((0,), (0,)), ((), ())), preferred_element_type=jnp.float32
    )


def times_trans(left, right):
    return lax.dot_general(
        left, right, (((1,), (1,)), ((), ())), preferred_element_type=jnp.float32
    )


def on_device(
    x_in,
    segment_ids,
    norm_gain,
    w_x,
    w_z,
    w_bc,
    w_dt,
    conv_x,
    conv_x_bias,
    conv_bc,
    conv_bc_bias,
    dt_bias,
    a_log,
    d_skip,
    gate_gain,
    w_out,
    cotangent,
):
    piece_rows = x_in.shape[0]
    local_channels = w_x.shape[1]
    bc_width = w_bc.shape[1]
    all_channels = local_channels * lax.axis_size("tensor")
    my_slot = lax.axis_index("tensor")
    edge_two = 2 * local_channels
    edge_three = edge_two + bc_width
    gathered = (
        lax.all_gather(norm_gain, "dp", axis=0, tiled=True),
        lax.all_gather(w_x, "dp", axis=0, tiled=True),
        lax.all_gather(w_z, "dp", axis=0, tiled=True),
        lax.all_gather(w_bc, "dp", axis=0, tiled=True),
        lax.all_gather(w_dt, "dp", axis=0, tiled=True),
        lax.all_gather(w_out, "dp", axis=1, tiled=True),
    )
    gain_full, wx_full, wz_full, wbc_full, wdt_full, wout_full = gathered
    tokens = x_in.astype(jnp.float32)
    inv_rms = lax.rsqrt(jnp.mean(tokens * tokens, axis=-1, keepdims=True) + epsilon)
    normed = (tokens * inv_rms * gain_full.astype(jnp.float32)).astype(jnp.bfloat16)
    w_cat = jnp.concatenate([wx_full, wz_full, wbc_full, wdt_full], axis=1)
    projected = jnp.dot(
        lax.all_gather(normed, "tensor", axis=0, tiled=True),
        w_cat,
        preferred_element_type=jnp.float32,
    )
    x_proj = projected[:, :local_channels]
    gate_in = projected[:, local_channels:edge_two]
    bc_proj = projected[:, edge_two:edge_three]
    dt_proj = projected[:, edge_three:]

    def bc_local(bc_values, conv_weight, conv_offset):
        return bc_branch(bc_values, conv_weight, conv_offset, segment_ids)

    bc_act, bc_pullback = jax.vjp(bc_local, bc_proj, conv_bc, conv_bc_bias)

    def mix_local(
        x_values, bc_values, dt_values, conv_weight, conv_offset, dt_offset, log_rate, skip_gain
    ):
        return mix_heads(
            x_values,
            bc_values,
            dt_values,
            conv_weight,
            conv_offset,
            dt_offset,
            log_rate,
            skip_gain,
            segment_ids,
            CH,
        )

    mixed_y, mixer_pullback = jax.vjp(
        mix_local, x_proj, bc_act, dt_proj, conv_x, conv_x_bias, dt_bias, a_log, d_skip
    )
    gate_act = jax.nn.silu(gate_in)
    gated = mixed_y * gate_act
    square_sum = lax.psum(jnp.sum(gated * gated, axis=-1), "tensor")
    gate_rms = lax.rsqrt(square_sum / all_channels + epsilon)[:, None]
    mixed = (gated * gate_rms * gate_gain).astype(jnp.bfloat16)
    branch_sum = lax.psum_scatter(
        jnp.dot(mixed, wout_full, preferred_element_type=jnp.float32).astype(jnp.bfloat16),
        "tensor",
        scatter_dimension=0,
        tiled=True,
    ).astype(jnp.float32)
    block_out = (tokens + branch_sum).astype(jnp.bfloat16)
    gain_back, wx_back, wz_back, wbc_back, wdt_back, wout_back = (
        lax.all_gather(norm_gain, "dp", axis=0, tiled=True),
        lax.all_gather(w_x, "dp", axis=0, tiled=True),
        lax.all_gather(w_z, "dp", axis=0, tiled=True),
        lax.all_gather(w_bc, "dp", axis=0, tiled=True),
        lax.all_gather(w_dt, "dp", axis=0, tiled=True),
        lax.all_gather(w_out, "dp", axis=1, tiled=True),
    )
    upstream = lax.all_gather(cotangent, "tensor", axis=0, tiled=True)
    w_out_part = rows_times(mixed, upstream)
    mixed_grad = times_trans(upstream, wout_back)
    gate_gain_grad = jnp.sum(mixed_grad * gated * gate_rms, axis=0)
    scaled_grad = mixed_grad * gate_gain
    inner_sum = lax.psum(jnp.sum(scaled_grad * gated, axis=-1), "tensor")
    gated_grad = gate_rms * scaled_grad - gated * gate_rms**3 * (inner_sum / all_channels)[:, None]
    sigmoid_gate = jax.nn.sigmoid(gate_in)
    y_grad = gated_grad * gate_act
    gate_grad = (
        gated_grad * mixed_y * sigmoid_gate * (1.0 + gate_in * (1.0 - sigmoid_gate))
    ).astype(jnp.bfloat16)
    (
        x_raw_grad,
        bc_part_grad,
        dt_raw_grad,
        conv_x_grad,
        conv_x_bias_grad,
        dt_bias_grad,
        a_log_grad,
        d_skip_grad,
    ) = mixer_pullback(y_grad)
    bc_total_grad = lax.psum(bc_part_grad, "tensor")
    bc_raw_grad, conv_bc_grad, conv_bc_bias_grad = bc_pullback(bc_total_grad)
    x_low = x_raw_grad.astype(jnp.bfloat16)
    bc_low = bc_raw_grad.astype(jnp.bfloat16)
    dt_low = dt_raw_grad.astype(jnp.bfloat16)
    grad_cat = jnp.concatenate([x_low, gate_grad, bc_low, dt_low], axis=1)
    part_cat = jnp.concatenate([x_low, gate_grad, dt_low], axis=1)
    w_part = jnp.concatenate([wx_back, wz_back, wdt_back], axis=1)
    weight_cat = rows_times(lax.all_gather(normed, "tensor", axis=0, tiled=True), grad_cat)
    normed_grad = lax.psum_scatter(
        times_trans(part_cat, w_part).astype(jnp.bfloat16),
        "tensor",
        scatter_dimension=0,
        tiled=True,
    ).astype(jnp.float32)
    own_bc = lax.dynamic_slice_in_dim(bc_low, my_slot * piece_rows, piece_rows, 0)
    normed_grad = normed_grad + times_trans(own_bc, wbc_back)
    gain_part = jnp.sum(normed_grad * tokens * inv_rms, axis=0)
    pushed = normed_grad * gain_back.astype(jnp.float32)
    x_grad = (
        cotangent.astype(jnp.float32)
        + inv_rms * pushed
        - tokens * inv_rms**3 * jnp.mean(pushed * tokens, axis=-1, keepdims=True)
    )
    w_x_part = weight_cat[:, :local_channels]
    w_z_part = weight_cat[:, local_channels:edge_two]
    w_bc_part = weight_cat[:, edge_two:edge_three]
    w_dt_part = weight_cat[:, edge_three:]
    reduced = (
        lax.psum_scatter(
            w_x_part.astype(jnp.bfloat16), "dp", scatter_dimension=0, tiled=True
        ).astype(jnp.float32),
        lax.psum_scatter(
            w_z_part.astype(jnp.bfloat16), "dp", scatter_dimension=0, tiled=True
        ).astype(jnp.float32),
        lax.psum_scatter(
            w_bc_part.astype(jnp.bfloat16), "dp", scatter_dimension=0, tiled=True
        ).astype(jnp.float32),
        lax.psum_scatter(
            w_dt_part.astype(jnp.bfloat16), "dp", scatter_dimension=0, tiled=True
        ).astype(jnp.float32),
        lax.psum_scatter(
            w_out_part.astype(jnp.bfloat16), "dp", scatter_dimension=1, tiled=True
        ).astype(jnp.float32),
        lax.psum_scatter(
            gain_part.astype(jnp.bfloat16), "dp", scatter_dimension=0, tiled=True
        ).astype(jnp.float32),
    )
    norm_gain_grad = lax.psum(reduced[5], "tensor")
    small_sums = lax.psum(
        (
            conv_x_grad,
            conv_x_bias_grad,
            conv_bc_grad,
            conv_bc_bias_grad,
            dt_bias_grad,
            a_log_grad,
            d_skip_grad,
            gate_gain_grad,
        ),
        "dp",
    )
    return (
        block_out,
        x_grad,
        norm_gain_grad,
        reduced[0],
        reduced[1],
        reduced[2],
        reduced[3],
        small_sums[0],
        small_sums[1],
        small_sums[2],
        small_sums[3],
        small_sums[4],
        small_sums[5],
        small_sums[6],
        small_sums[7],
        reduced[4],
    )


def solution(mesh):
    in_specs = (
        P(("dp", "tensor"), None),
        P("dp", None),
        P("dp"),
        P("dp", "tensor"),
        P("dp", "tensor"),
        P("dp", None),
        P("dp", "tensor"),
        P(None, "tensor"),
        P("tensor"),
        P(),
        P(),
        P("tensor"),
        P("tensor"),
        P("tensor"),
        P("tensor"),
        P("tensor", "dp"),
        P(("dp", "tensor"), None),
    )
    out_specs = (
        P(("dp", "tensor"), None),
        P(("dp", "tensor"), None),
        P("dp"),
        P("dp", "tensor"),
        P("dp", "tensor"),
        P("dp", None),
        P("dp", "tensor"),
        P(None, "tensor"),
        P("tensor"),
        P(),
        P(),
        P("tensor"),
        P("tensor"),
        P("tensor"),
        P("tensor"),
        P("tensor", "dp"),
    )
    return jax.shard_map(
        on_device, mesh=mesh, in_specs=in_specs, out_specs=out_specs, check_vma=False
    )
```

profile of v0, /device:TPU:0, one launch (start us, length us, event | category | flops | bytes accessed | tf_op | source)
XLA Modules:
  0.0 1440.4 jit_solution(5639272047914359760)
XLA Ops:
  11.6 15.4 %all-reduce.26 = bf16[1536]{0:T(1024)(128)(2,1)S(1)} all-reduce(bf16[1536]{0:T(1024)(128)(2,1)S(1)} %dynamic-update-slice), channel_id=1, replica_groups=mesh['dp'=8,'tensor'=4] {'dp'}, use_global_device_ids=true, to_apply=%add.26 | all-reduce | flops 1536 | bytes 6144
  45.7 12.5 all_gather.35
  58.3 15.7 %all-gather.11.cloned.1.call-done = bf16[1536,768]{1,0:T(8,128)(2,1)} async-done(((bf16[192,768]{1,0:T(8,128)(2,1)}), bf16[1536,768]{1,0:T(8,128)(2,1)}) %all-gather.11.cloned.1.call-update) | async-done | bytes 2359312 | tf_op jit(solution)/shard_map/all_gather | solution.py:150
  73.9 117.5 %all-gather.7.cloned.1.call-done = bf16[2048,1536]{1,0:T(8,128)(2,1)} async-done(((bf16[512,1536]{1,0:T(8,128)(2,1)}), bf16[2048,1536]{1,0:T(8,128)(2,1)}) %all-gather.7.cloned.1.call-update) | async-done | bytes 6291472 | tf_op jit(solution)/shard_map/all_gather | solution.py:161
  191.4 18.2 %fusion.119 = f32[2048,1804]{0,1:T(8,128)} fusion(bf16[2048,1536]{1,0:T(8,128)(2,1)} %all-gather.7.cloned.1.call-done, bf16[1536,12]{1,0:T(8,128)(2,1)S(1)} %bitcast.433, bf16[1536,256]{1,0:T(8,128)(2,1)S(1)} %all_gather.35, bf16[1536,768]{1,0:T(8,128)(2,1)} %all-gather.11.cloned.1.call-done, bf16[1536,768]{1,0:T(8,128)(2,1)} %all-gather.9.cloned.1.call-done), kind=kOutput, calls=%fused_computation.209 | convolution fusion | flops 11371954176 | bytes 26611712 | tf_op jit(solution)/shard_map/dot_general | solution.py:160
  263.6 88.0 %while.45 = (s32[]{:T(128)}, f32[2,12,64,128]{3,2,1,0:T(8,128)S(1)}, s32[2]{0:T(128)S(1)}, f32[4,2,256,12,64]{2,4,3,1,0:T(8,128)}, f32[4,2,12,64,128]{4,3,2,1,0:...) while((s32[]{:T(128)}, ...), condition=%wide.region_4.5_spmd.clone, body=%wide.region_1.4_spmd.clone.sunk | while | flops 2628550656 | bytes 16194227 | solution.py:70
  410.4 16.7 %multiply_reduce_fusion.6 = (f32[768]{0:T(1024)}, f32[2048,768]{0,1:T(8,128)}, bf16[2048,768]{0,1:T(8,128)(2,1)}) fusion(f32[2048,768]{0,1:T(8,128)} %bitcast.412, f32[2048,1804]{0,1:T(8,128)} %fusion.119, f32[2048]{0:T(1024)S(1)} %broadcast_multiply_fusion.2, f32[2048,768]{0,1:T(8,128)} %get-tuple-element.942, f32[2048]{0:T(1024)S(1)} %get-tuple-element.978, ...), kind=kLoop, calls=%fused_computation.190 | loop fusion | flops 33029376 | bytes 40928256 | tf_op jit(solution)/shard_map/transpose(jvp())/reduce_sum | solution.py:105
  449.9 424.5 %while.46 = (s32[]{:T(128)}, f32[12]{0:T(128)}, f32[2,12,64,128]{3,2,1,0:T(8,128)S(1)}, f32[4,2,256,12,64]{2,4,3,1,0:T(8,128)}, f32[4,2,256,12]{3,1,2,0:T(2,128)...) while((s32[]{:T(128)}, f32[12]{0:T(128)}, ...), condition=%wide.region_23.24_spmd.clone, body=%wide.region_10.23_spmd.clone.sunk | while | flops 6077933568 | bytes 65325048 | solution.py:70
  486.0 13.2 fusion.264
  591.5 13.2 fusion.264
  697.7 13.2 fusion.264
  803.8 13.2 fusion.264
  896.4 19.9 %multiply_reduce_fusion.10 = (f32[768]{0:T(1024)S(1)}, f32[768]{0:T(1024)S(1)}, f32[768]{0:T(1024)S(1)}, f32[768]{0:T(1024)S(1)}, f32[768]{0:T(1024)S(1)}, /*index=5*/f32[2,1024,768]{1,2,0:T(8,128)}) fusion(f32[2,1024,768]{1,2,0:T(8,128)} %bitcast.410, f32[2,1024]{1,0:T(2,128)S(1)} %copy-done.30, f32[2,1024]{1,0:T(2,128)S(1)} %copy-done.28, ...), kind=kLoop, calls=%fused_computation.194 | loop fusion | flops 36172032 | bytes 37791744 | tf_op jit(solution)/shard_map/transpose(jvp())/reduce_sum | solution.py:22
  933.4 28.4 %all-reduce.31.cloned.1.call-done = f32[2,1024,256]{2,1,0:T(8,128)} async-done(((f32[2,1024,256]{2,1,0:T(8,128)}), f32[2,1024,256]{2,1,0:T(8,128)}) %all-reduce.31.cloned.1.call-update) | async-done | bytes 2097168 | tf_op jit(solution)/shard_map/psum | solution.py:236
  968.4 22.6 %convolution_convert_fusion.2 = bf16[1536,1804]{0,1:T(8,128)(2,1)} fusion(bf16[2048,1536]{1,0:T(8,128)(2,1)} %all-gather.7.cloned.1.call-done, bf16[2048,12]{0,1:T(8,128)(2,1)S(1)} %get-tuple-element.938, bf16[2048,256]{0,1:T(8,128)(2,1)S(1)} %copy.472, bf16[2048,768]{0,1:T(8,128)(2,1)} %get-tuple-element.965, bf16[2048,768]{0,1:T(8,128)(2,1)} %bitcast.430), kind=kOutput, calls=%fused_computation.154 | convolution fusion | flops 11382114304 | bytes 19222528 | tf_op jit(solution)/shard_map/dot_general | solution.py:110
  1017.6 16.9 %convolution_convert_fusion.1 = bf16[2048,1536]{1,0:T(8,128)(2,1)} fusion(bf16[2048,12]{0,1:T(8,128)(2,1)S(1)} %get-tuple-element.938, bf16[2048,768]{0,1:T(8,128)(2,1)} %get-tuple-element.965, bf16[2048,768]{0,1:T(8,128)(2,1)} %bitcast.431, bf16[1536,12]{1,0:T(8,128)(2,1)S(1)} %bitcast.434, bf16[1536,768]{1,0:T(8,128)(2,1)} %all-gather.11.cloned.1.call-done, ...), kind=kOutput, calls=%fused_computation.153 | convolution fusion | flops 9775607808 | bytes 17387520 | tf_op jit(solution)/shard_map/dot_general | solution.py:116
  1047.8 24.7 %all-reduce.28 = (f32[4,768]{1,0:T(4,128)}, f32[768]{0:T(1024)}, f32[4,256]{1,0:T(4,128)}, f32[256]{0:T(256)}, f32[12]{0:T(128)}, /*index=5*/f32[12]{0:T(128)}, f32[12]{0:T(128)}, f32[768]{0:T(1024)}) all-reduce(f32[4,768]{1,0:T(4,128)S(1)} %pad_add_fusion.1, ...), channel_id=1, replica_groups=mesh['dp'=8,'tensor'=4] {'dp'}, use_global_device_ids=true, to_apply=%region_38.39 | all-reduce | flops 5924 | bytes 47392 | tf_op jit(solution)/shard_map/psum | solution.py:285
  1075.8 34.1 %reduce-scatter.20.cloned.1.call-done = bf16[768,192]{0,1:T(8,128)(2,1)} async-done(((bf16[768,1536]{0,1:T(8,128)(2,1)}), bf16[768,192]{0,1:T(8,128)(2,1)}) %reduce-scatter.20.cloned.1.call-update) | async-done | bytes 294928 | tf_op jit(solution)/shard_map/reduce_scatter | solution.py:277
  1111.7 43.8 %reduce-scatter.24.cloned.1.call-done = bf16[192,768]{1,0:T(8,128)(2,1)} async-done(((bf16[1536,768]{1,0:T(8,128)(2,1)}), bf16[192,768]{1,0:T(8,128)(2,1)}) %reduce-scatter.24.cloned.1.call-update) | async-done | bytes 294928
  1157.5 43.6 %reduce-scatter.22.cloned.1.call-done = bf16[192,768]{1,0:T(8,128)(2,1)} async-done(((bf16[1536,768]{1,0:T(8,128)(2,1)}), bf16[192,768]{1,0:T(8,128)(2,1)}) %reduce-scatter.22.cloned.1.call-update) | async-done | bytes 294928
  1203.3 110.9 %reduce-scatter.18.cloned.1.call-done = bf16[512,1536]{1,0:T(8,128)(2,1)} async-done(((bf16[2048,1536]{1,0:T(8,128)(2,1)}), bf16[512,1536]{1,0:T(8,128)(2,1)}) %reduce-scatter.18.cloned.1.call-update) | async-done | bytes 1572880 | tf_op jit(solution)/shard_map/reduce_scatter | solution.py:245
  1318.7 14.0 all-reduce.27
  1332.8 14.1 psum.87
  1346.9 81.1 %reduce-scatter.16.cloned.1.call-done = bf16[512,1536]{1,0:T(8,128)(2,1)} async-done(((bf16[2048,1536]{1,0:T(8,128)(2,1)}), bf16[512,1536]{1,0:T(8,128)(2,1)}) %reduce-scatter.16.cloned.1.call-update) | async-done | bytes 1572880 | tf_op jit(solution)/shard_map/reduce_scatter | solution.py:199
  (778 shorter events, 719.0 us)
Async XLA Ops:
  7.3 51.0 %all-gather.9.cloned.1.call-start = ((), (), s32[]{:S(2)}) async-start(), calls=%async_computation.8 | async-start | bytes 2654208 | tf_op jit(solution)/shard_map/all_gather | solution.py:149
  8.0 65.9 %all-gather.11.cloned.1.call-start = ((), (), s32[]{:S(2)}) async-start(), calls=%async_computation.9 | async-start | bytes 2654208 | tf_op jit(solution)/shard_map/all_gather | solution.py:150
  8.7 182.7 %all-gather.7.cloned.1.call-start = ((), (), s32[]{:S(2)}) async-start(), calls=%async_computation.7 | async-start | bytes 7864320 | tf_op jit(solution)/shard_map/all_gather | solution.py:161
  33.0 354.9 %all-gather.13.cloned.1.call-start = ((), (), s32[]{:S(2)}) async-start(), calls=%async_computation.10 | async-start | bytes 2654208 | tf_op jit(solution)/shard_map/all_gather | solution.py:153
  33.6 354.3 %all-gather.15.cloned.1.call-start = ((), (), s32[]{:S(2)}) async-start(), calls=%async_computation.12 | async-start | bytes 7864320 | tf_op jit(solution)/shard_map/all_gather | solution.py:214
  34.2 927.6 %all-reduce.31.cloned.1.call-start = ((), (), s32[]{:S(2)}) async-start(), calls=%async_computation.14 | async-start | bytes 4194304 | tf_op jit(solution)/shard_map/psum | solution.py:236
  34.3 195.6 %copy-start.25 = (f32[2,1024]{1,0:T(2,128)}, f32[2,1024]{1,0:T(2,128)S(1)}, u32[]{:S(2)}) copy-start(f32[2,1024]{1,0:T(2,128)S(1)} %get-tuple-element.980) | copy-start | bytes 24580
  34.4 195.6 %copy-start.27 = (f32[2,1024]{1,0:T(2,128)}, f32[2,1024]{1,0:T(2,128)S(1)}, u32[]{:S(2)}) copy-start(f32[2,1024]{1,0:T(2,128)S(1)} %get-tuple-element.981) | copy-start | bytes 24580
  34.4 195.6 %copy-start.29 = (f32[2,1024]{1,0:T(2,128)}, f32[2,1024]{1,0:T(2,128)S(1)}, u32[]{:S(2)}) copy-start(f32[2,1024]{1,0:T(2,128)S(1)} %get-tuple-element.982) | copy-start | bytes 24580
  35.6 374.7 %copy-start.37 = (f32[768]{0:T(1024)}, f32[768]{0:T(1024)S(1)}, u32[]{:S(2)}) copy-start(f32[768]{0:T(1024)S(1)} %mul.1010) | copy-start | bytes 9220
  35.7 194.3 %copy-start.41 = (f32[768]{0:T(1024)}, f32[768]{0:T(1024)S(1)}, u32[]{:S(2)}) copy-start(f32[768]{0:T(1024)S(1)} %get-tuple-element.864) | copy-start | bytes 9220
  35.7 194.3 %copy-start.43 = (f32[768]{0:T(1024)}, f32[768]{0:T(1024)S(1)}, u32[]{:S(2)}) copy-start(f32[768]{0:T(1024)S(1)} %get-tuple-element.865) | copy-start | bytes 9220
  877.4 195.1 %reduce-scatter.28.cloned.1.call-start = ((), (), s32[]{:S(2)}) async-start(), calls=%async_computation.19 | async-start | bytes 442368
  992.8 81.2 %reduce-scatter.26.cloned.1.call-start = ((), (), s32[]{:S(2)}) async-start(), calls=%async_computation.18 | async-start | bytes 884736
  995.2 114.7 %reduce-scatter.20.cloned.1.call-start = ((), (), s32[]{:S(2)}) async-start(), calls=%async_computation.15 | async-start | bytes 2654208 | tf_op jit(solution)/shard_map/reduce_scatter | solution.py:277
  1006.0 149.5 %reduce-scatter.24.cloned.1.call-start = ((), (), s32[]{:S(2)}) async-start(), calls=%async_computation.17 | async-start | bytes 2654208
  1015.0 186.2 %reduce-scatter.22.cloned.1.call-start = ((), (), s32[]{:S(2)}) async-start(), calls=%async_computation.16 | async-start | bytes 2654208
  1017.5 296.6 %reduce-scatter.18.cloned.1.call-start = ((), (), s32[]{:S(2)}) async-start(), calls=%async_computation.13 | async-start | bytes 7864320 | tf_op jit(solution)/shard_map/reduce_scatter | solution.py:245
  1034.5 393.5 %reduce-scatter.16.cloned.1.call-start = ((), (), s32[]{:S(2)}) async-start(), calls=%async_computation.11 | async-start | bytes 7864320 | tf_op jit(solution)/shard_map/reduce_scatter | solution.py:199
  1046.7 267.5 %copy-start.11 = (bf16[512,1536]{1,0:T(8,128)(2,1)S(1)}, bf16[512,1536]{1,0:T(8,128)(2,1)}, u32[]{:S(2)}) copy-start(bf16[512,1536]{1,0:T(8,128)(2,1)} %param.21) | copy-start | bytes 4718596
  1046.7 267.5 %copy-start.36 = (f32[1536]{0:T(1024)S(1)}, f32[1536]{0:T(1024)}, u32[]{:S(2)}) copy-start(f32[1536]{0:T(1024)} %copy-done.35) | copy-start | bytes 18436
  1046.7 267.5 %copy-start.53 = (f32[512]{0:T(512)S(1)}, f32[512]{0:T(512)}, u32[]{:S(2)}) copy-start(f32[512]{0:T(512)} %copy-done.52) | copy-start | bytes 6148
  1075.0 353.0 %copy-start.16 = (bf16[512,1536]{1,0:T(8,128)(2,1)S(1)}, bf16[512,1536]{1,0:T(8,128)(2,1)}, u32[]{:S(2)}) copy-start(bf16[512,1536]{1,0:T(8,128)(2,1)} %param.37) | copy-start | bytes 4718596
  1075.0 353.0 %copy-start.66 = (f32[512]{0:T(512)S(1)}, f32[512]{0:T(512)}, u32[]{:S(2)}) copy-start(f32[512]{0:T(512)} %get-tuple-element.987) | copy-start | bytes 6148
  (126 other events, 2890.2 us)
Sparse Core Ops, SparseCore 0:
  9.9 31.6 all-gather.8
  43.6 30.3 all-gather.10
  76.1 115.3 all-gather.6
  193.2 27.0 all-gather.12
  221.7 115.3 all-gather.14
  877.5 84.1 all-reduce.30
  992.9 32.9 reduce-scatter.27
  1029.0 35.0 reduce-scatter.25
  1067.5 42.3 reduce-scatter.19
  1113.1 42.3 reduce-scatter.23
  1158.8 42.3 reduce-scatter.21
  1203.3 110.7 reduce-scatter.17
  1316.4 111.5 reduce-scatter.15
where the time goes:
time: 1450 us; the launch traced here: 1440 us
  waiting for transfers between devices  478 us (33%)
  matrix products  337 us (23%)
  local copies, waits for them, and re-layouts  274 us (19%)
  other arithmetic  225 us (16%)
  blocking collectives  108 us (7%)
  between operations  16.5 us (1%)
    all_gather x1, waiting for transfers between devices, on_device(): lax.all_gather(normed, 'tensor', axis=0, tiled=True)  118 us
    dot_general x12, matrix products, block_step(): inner_part = jnp.einsum('hts,shp->thp', mixing, values, precision=highest)  114 us
    reduce_scatter x1, waiting for transfers between devices, on_device(): lax.psum_scatter(times_trans(part_cat, w_part).astype(jnp.bfloat16), 'ten...  111 us
    unnamed x17, waiting for transfers between devices  90 us
    reduce_scatter x1, waiting for transfers between devices, on_device(): lax.psum_scatter(jnp.dot(mixed, wout_full, preferred_element_type=jnp.flo...  81.1 us
    another operation x77, local copies, waits for them, and re-layouts  56.4 us
    another operation x41, other arithmetic  52.4 us
    dot_general x12, matrix products, block_step(): jnp.einsum('sh,shp,sn->hpn', weights_end, values, b_rows, precision=highest)  50.5 us
  transfers between devices with their start and end apart: 13, of which 8 were waited for; matrix products, arithmetic and copies ran while one was open for 22% of the time, Pallas kernels for 0%

commit v1 on v0

v1 whole, which is shorter than its diff:
```python
import jax
import jax.numpy as jnp
from jax import lax
from jax.experimental import pallas as pl
from jax.experimental.pallas import tpu as pltpu
from jax.sharding import PartitionSpec as P

CH = 256
HALO = 16
GROUP = 4
LOG2E = 1.4426950408889634
epsilon = 1e-05
f32 = jnp.float32
bf16 = jnp.bfloat16
highest = lax.Precision.HIGHEST


def mm(a, b):
    return lax.dot_general(a, b, (((1,), (0,)), ((), ())), preferred_element_type=f32)


def mmt(a, b):
    return lax.dot_general(a, b, (((1,), (1,)), ((), ())), preferred_element_type=f32)


def tmm(a, b):
    return lax.dot_general(a, b, (((0,), (0,)), ((), ())), preferred_element_type=f32)


def exact(a, b):
    return lax.dot_general(
        a, b, (((1,), (0,)), ((), ())), precision=highest, preferred_element_type=f32
    )


def head_map(channels, kind):
    return (jnp.arange(channels)[:, None] // 64 == jnp.arange(128)[None, :]).astype(kind)


def spread(cols, first, rows, lane_low):
    parts = []
    for pair in range(GROUP // 2):
        left = jnp.broadcast_to(cols[:, first + 2 * pair : first + 2 * pair + 1], (rows, 128))
        right = jnp.broadcast_to(cols[:, first + 2 * pair + 1 : first + 2 * pair + 2], (rows, 128))
        parts.append(jnp.where(lane_low, left, right))
    return jnp.concatenate(parts, axis=1)


def conv_pre(x_ref, cw_ref, flags, start, rows):
    pre = cw_ref[4:5, :] + cw_ref[0:1, :] * x_ref[0, HALO + start : HALO + start + rows, :]
    for k in range(1, 4):
        shifted = x_ref[0, HALO + start - k : HALO + start - k + rows, :]
        pre = pre + (cw_ref[k : k + 1, :] * shifted) * flags[:, k - 1 : k]
    return pre


def masked_scores(cb_ref, bc_ref, fl_ref, rv_ref, n_chunks, rows):
    for c in range(n_chunks):
        at = slice(c * rows, (c + 1) * rows)
        ids_col = fl_ref[0, at, 3:4]
        ids_row = rv_ref[0, 24:25, at]
        t_at = lax.broadcasted_iota(jnp.int32, (rows, rows), 0)
        s_at = lax.broadcasted_iota(jnp.int32, (rows, rows), 1)
        keep = (ids_col == ids_row) & (t_at >= s_at)
        scores = lax.dot_general(
            bc_ref[0, at, 128:], bc_ref[0, at, :128], (((1,), (1,)), ((), ())),
            precision=highest, preferred_element_type=f32,
        )
        cb_ref[c] = jnp.where(keep, scores, 0.0)


def scan_fwd_body(n_chunks, rows, hv_ref, fl_ref, rv_ref, al_ref, bc_ref, bt_ref, x_ref, cw_ref, y_ref, st_ref, cb_ref):
    group = pl.program_id(1)
    turn = lax.rem(128 - GROUP * group, 128)

    @pl.when(group == 0)
    def _():
        masked_scores(cb_ref, bc_ref, fl_ref, rv_ref, n_chunks, rows)

    lane_low = lax.broadcasted_iota(jnp.int32, (rows, 128), 1) < 64
    state = jnp.zeros((128, GROUP * 64), f32)
    for c in range(n_chunks):
        at = slice(c * rows, (c + 1) * rows)
        cols = pltpu.roll(hv_ref[0, at, :], turn, 1)
        flags = fl_ref[0, at, :]
        pre = conv_pre(x_ref, cw_ref, flags, c * rows, rows)
        act = pre * jax.nn.sigmoid(pre)
        u = act * spread(cols, 32, rows, lane_low)
        ub = u.astype(bf16)
        y = cw_ref[5:6, :] * act
        if c > 0:
            c_rows = bc_ref[0, at, 128:].astype(bf16)
            y = y + mm(c_rows, state.astype(bf16)) * spread(cols, 64, rows, lane_low)
        scores = cb_ref[c]
        parts = []
        for pair in range(GROUP // 2):
            u_pair = ub[:, 128 * pair : 128 * pair + 128]
            outs = []
            for j in (2 * pair, 2 * pair + 1):
                gap = cols[:, j : j + 1] - rv_ref[0, pl.ds(group * GROUP + j, 1), at]
                mix = (scores * jnp.exp2(jnp.minimum(gap, 0.0))).astype(bf16)
                outs.append(mm(mix, u_pair))
            parts.append(jnp.where(lane_low, outs[0], outs[1]))
        y_ref[0, at, :] = y + jnp.concatenate(parts, axis=1)
        wu = (u * spread(cols, 96, rows, lane_low)).astype(bf16)
        state = al_ref[0, c : c + 1, :] * state + mm(bt_ref[0, :128, at], wu)
        st_ref[0, c] = state


def scan_fwd(hv, fl, rv, al, bc, bt, x_ext, cw, rows):
    pieces, length, _ = hv.shape
    n_chunks = length // rows
    width = GROUP * 64
    channels = x_ext.shape[2]
    groups = channels // width
    return pl.pallas_call(
        lambda *refs: scan_fwd_body(n_chunks, rows, *refs),
        grid=(pieces, groups),
        in_specs=[
            pl.BlockSpec((1, length, 128), lambda s, g: (s, 0, 0)),
            pl.BlockSpec((1, length, 8), lambda s, g: (s, 0, 0)),
            pl.BlockSpec((1, 32, length), lambda s, g: (s, 0, 0)),
            pl.BlockSpec((1, 8, width), lambda s, g: (s, 0, g)),
            pl.BlockSpec((1, length, 256), lambda s, g: (s, 0, 0)),
            pl.BlockSpec((1, 256, length), lambda s, g: (s, 0, 0)),
            pl.BlockSpec((1, HALO + length, width), lambda s, g: (s, 0, g)),
            pl.BlockSpec((8, width), lambda s, g: (0, g)),
        ],
        out_specs=[
            pl.BlockSpec((1, length, width), lambda s, g: (s, 0, g)),
            pl.BlockSpec((1, n_chunks, 128, width), lambda s, g: (s, 0, 0, g)),
        ],
        out_shape=[
            jax.ShapeDtypeStruct((pieces, length, channels), f32),
            jax.ShapeDtypeStruct((pieces, n_chunks, 128, channels), f32),
        ],
        scratch_shapes=[pltpu.VMEM((n_chunks, rows, rows), f32)],
        cost_estimate=pl.CostEstimate(
            flops=pieces * groups * GROUP * length * (rows + 256) * 128 * 2,
            transcendentals=pieces * groups * GROUP * length * rows,
            bytes_accessed=pieces * length * channels * 8,
        ),
        name="scan_fwd",
    )(hv, fl, rv, al, bc, bt, x_ext, cw)


def scan_bwd_body(
    n_chunks, rows, hv_ref, fl_ref, rv_ref, al_ref, bc_ref, bt_ref, x_ref, cw_ref, dy_ref, st_ref, sr_ref, rr_ref, seg_ref,
    xl_ref, tail_ref, head_ref, dbc_ref, dcol_ref, drow_ref, dcw_ref, cb_ref, dcb_ref, dpre_ref,
):
    group = pl.program_id(1)
    turn = lax.rem(128 - GROUP * group, 128)
    length = n_chunks * rows
    width = GROUP * 64

    @pl.when(group == 0)
    def _():
        masked_scores(cb_ref, bc_ref, fl_ref, rv_ref, n_chunks, rows)
        dcb_ref[...] = jnp.zeros_like(dcb_ref)
        dbc_ref[...] = jnp.zeros_like(dbc_ref)
        dcol_ref[...] = jnp.zeros_like(dcol_ref)
        drow_ref[...] = jnp.zeros_like(drow_ref)

    lane_low = lax.broadcasted_iota(jnp.int32, (rows, 128), 1) < 64
    lane = lax.broadcasted_iota(jnp.int32, (rows, 128), 1)
    row_at = lax.broadcasted_iota(jnp.int32, (rows, width), 0)
    grad_state = rr_ref[0].astype(f32)
    recv = sr_ref[0].astype(f32)
    states = [recv]
    carry = recv
    for c in range(n_chunks - 1):
        carry = al_ref[0, c : c + 1, :] * carry
        states.append(st_ref[0, c] + carry)
    tap_sums = [jnp.zeros((1, width), f32) for _ in range(6)]
    dpre_ref[length : length + 8, :] = jnp.zeros((8, width), f32)
    for c in reversed(range(n_chunks)):
        at = slice(c * rows, (c + 1) * rows)
        cols = pltpu.roll(hv_ref[0, at, :], turn, 1)
        flags = fl_ref[0, at, :]
        pre = conv_pre(x_ref, cw_ref, flags, c * rows, rows)
        sig = jax.nn.sigmoid(pre)
        act = pre * sig
        step_wide = spread(cols, 32, rows, lane_low)
        end_wide = spread(cols, 96, rows, lane_low)
        u = act * step_wide
        ub = u.astype(bf16)
        dy = dy_ref[0, at, :]
        dyb = dy.astype(bf16)
        b_rows = bc_ref[0, at, :128].astype(bf16)
        c_rows = bc_ref[0, at, 128:].astype(bf16)
        state_b = states[c].astype(bf16)
        dye = dy * spread(cols, 64, rows, lane_low)
        dyeb = dye.astype(bf16)
        gs_b = grad_state.astype(bf16)
        wub = (u * end_wide).astype(bf16)
        dbc_ref[0, at, 128:] += mmt(dyeb, state_b)
        dbc_ref[0, at, :128] += mmt(wub, gs_b)
        du_state = mm(b_rows, gs_b) * end_wide
        u_du = u * du_state
        at_end = jnp.sum(u_du, axis=0, keepdims=True) + al_ref[0, c : c + 1, :] * jnp.sum(
            grad_state * states[c], axis=0, keepdims=True
        )
        log_grad = dye * mm(c_rows, state_b) - u_du
        log_grad = jnp.where(row_at == rows - 1, log_grad + at_end, log_grad)
        grad_state = al_ref[0, c : c + 1, :] * grad_state + mm(bt_ref[0, 128:, at], dyeb)
        scores = cb_ref[c]
        dcb = dcb_ref[c]
        parts = []
        row_sums = jnp.zeros((rows, 128), f32)
        for pair in range(GROUP // 2):
            lanes = slice(128 * pair, 128 * pair + 128)
            u_pair = ub[:, lanes]
            dy_pair = dyb[:, lanes]
            outs = []
            for j in (2 * pair, 2 * pair + 1):
                gap = cols[:, j : j + 1] - rv_ref[0, pl.ds(group * GROUP + j, 1), at]
                decay = jnp.exp2(jnp.minimum(gap, 0.0))
                mix = (scores * decay).astype(bf16)
                own = lane_low if j % 2 == 0 else jnp.logical_not(lane_low)
                prod = mmt(jnp.where(own, dy_pair, jnp.zeros_like(dy_pair)), u_pair) * decay
                dcb = dcb + prod
                full = prod * scores
                row_sums = jnp.where(
                    lane == group * GROUP + j, jnp.sum(full, axis=1, keepdims=True), row_sums
                )
                drow_ref[0, pl.ds(group * GROUP + j, 1), at] = jnp.sum(full, axis=0, keepdims=True)
                outs.append(tmm(mix, dy_pair))
            parts.append(jnp.where(lane_low, outs[0], outs[1]))
        dcb_ref[c] = dcb
        du = jnp.concatenate(parts, axis=1) + du_state
        seg = seg_ref[...]
        dcol_ref[0, at, :128] += row_sums + lax.dot_general(
            log_grad, seg, (((1,), (0,)), ((), ())), precision=highest, preferred_element_type=f32
        )
        dcol_ref[0, at, 128:] += lax.dot_general(
            du * act, seg, (((1,), (0,)), ((), ())), precision=highest, preferred_element_type=f32
        )
        dact = du * step_wide + cw_ref[5:6, :] * dy
        dpre = dact * (sig * (1.0 + pre * (1.0 - sig)))
        dpre_ref[at, :] = dpre
        tap_sums[0] += jnp.sum(dpre * x_ref[0, HALO + c * rows : HALO + (c + 1) * rows, :], axis=0, keepdims=True)
        for k in range(1, 4):
            shifted = x_ref[0, HALO + c * rows - k : HALO + (c + 1) * rows - k, :]
            tap_sums[k] += jnp.sum(dpre * flags[:, k - 1 : k] * shifted, axis=0, keepdims=True)
        tap_sums[4] += jnp.sum(dpre, axis=0, keepdims=True)
        tap_sums[5] += jnp.sum(dy * act, axis=0, keepdims=True)
        xg = cw_ref[0:1, :] * dpre
        for k in range(1, 4):
            xg = xg + (cw_ref[k : k + 1, :] * dpre_ref[c * rows + k : (c + 1) * rows + k, :]) * flags[:, 3 + k : 4 + k]
        xl_ref[0, at, :] = xg.astype(bf16)
        if c == n_chunks - 1:
            tail_ref[0] = xg[rows - 16 :, :]
        if c == 0:
            head_ref[0] = dpre[:8, :]
    dcw_ref[0] = jnp.concatenate(tap_sums + [jnp.zeros((2, width), f32)], axis=0)

    @pl.when(group == pl.num_programs(1) - 1)
    def _():
        for c in range(n_chunks):
            at = slice(c * rows, (c + 1) * rows)
            ids_col = fl_ref[0, at, 3:4]
            ids_row = rv_ref[0, 24:25, at]
            t_at = lax.broadcasted_iota(jnp.int32, (rows, rows), 0)
            s_at = lax.broadcasted_iota(jnp.int32, (rows, rows), 1)
            keep = (ids_col == ids_row) & (t_at >= s_at)
            grad = jnp.where(keep, dcb_ref[c], 0.0).astype(bf16)
            dbc_ref[0, at, 128:] += mm(grad, bc_ref[0, at, :128].astype(bf16))
            dbc_ref[0, at, :128] += tmm(grad, bc_ref[0, at, 128:].astype(bf16))


def scan_bwd(hv, fl, rv, al, bc, bt, x_ext, cw, dy, states, s_recv, r_recv, rows):
    pieces, length, _ = hv.shape
    n_chunks = length // rows
    width = GROUP * 64
    channels = x_ext.shape[2]
    groups = channels // width
    seg = head_map(channels, f32)
    return pl.pallas_call(
        lambda *refs: scan_bwd_body(n_chunks, rows, *refs),
        grid=(pieces, groups),
        in_specs=[
            pl.BlockSpec((1, length, 128), lambda s, g: (s, 0, 0)),
            pl.BlockSpec((1, length, 8), lambda s, g: (s, 0, 0)),
            pl.BlockSpec((1, 32, length), lambda s, g: (s, 0, 0)),
            pl.BlockSpec((1, 8, width), lambda s, g: (s, 0, g)),
            pl.BlockSpec((1, length, 256), lambda s, g: (s, 0, 0)),
            pl.BlockSpec((1, 256, length), lambda s, g: (s, 0, 0)),
            pl.BlockSpec((1, HALO + length, width), lambda s, g: (s, 0, g)),
            pl.BlockSpec((8, width), lambda s, g: (0, g)),
            pl.BlockSpec((1, length, width), lambda s, g: (s, 0, g)),
            pl.BlockSpec((1, n_chunks, 128, width), lambda s, g: (s, 0, 0, g)),
            pl.BlockSpec((1, 128, width), lambda s, g: (s, 0, g)),
            pl.BlockSpec((1, 128, width), lambda s, g: (s, 0, g)),
            pl.BlockSpec((width, 128), lambda s, g: (g, 0)),
        ],
        out_specs=[
            pl.BlockSpec((1, length, width), lambda s, g: (s, 0, g)),
            pl.BlockSpec((1, 16, width), lambda s, g: (s, 0, g)),
            pl.BlockSpec((1, 8, width), lambda s, g: (s, 0, g)),
            pl.BlockSpec((1, length, 256), lambda s, g: (s, 0, 0)),
            pl.BlockSpec((1, length, 256), lambda s, g: (s, 0, 0)),
            pl.BlockSpec((1, 32, length), lambda s, g: (s, 0, 0)),
            pl.BlockSpec((1, 8, width), lambda s, g: (s, 0, g)),
        ],
        out_shape=[
            jax.ShapeDtypeStruct((pieces, length, channels), bf16),
            jax.ShapeDtypeStruct((pieces, 16, channels), f32),
            jax.ShapeDtypeStruct((pieces, 8, channels), f32),
            jax.ShapeDtypeStruct((pieces, length, 256), f32),
            jax.ShapeDtypeStruct((pieces, length, 256), f32),
            jax.ShapeDtypeStruct((pieces, 32, length), f32),
            jax.ShapeDtypeStruct((pieces, 8, channels), f32),
        ],
        scratch_shapes=[
            pltpu.VMEM((n_chunks, rows, rows), f32),
            pltpu.VMEM((n_chunks, rows, rows), f32),
            pltpu.VMEM((length + 8, width), f32),
        ],
        cost_estimate=pl.CostEstimate(
            flops=pieces * groups * GROUP * length * (rows + 256) * 128 * 6,
            transcendentals=pieces * groups * GROUP * length * rows,
            bytes_accessed=pieces * length * channels * 12,
        ),
        name="scan_bwd",
    )(hv, fl, rv, al, bc, bt, x_ext, cw, dy, states, s_recv, r_recv, seg)


def swap(value):
    size = lax.axis_size("dp")
    return lax.ppermute(value, "dp", [(i, i ^ 1) for i in range(size)])


def across(value, bit):
    size = lax.axis_size("dp")
    return lax.ppermute(value, "dp", [(i, i ^ (1 << bit)) for i in range(size)])


def around(value, by):
    size = lax.axis_size("tensor")
    return lax.ppermute(value, "tensor", [(i, (i + by) % size) for i in range(size)])


def along_sequence(value, pieces, forward):
    size = lax.axis_size("tensor")
    pairs = [(i, i + 1) for i in range(size - 1) if (i + 1) % pieces]
    if not forward:
        pairs = [(b, a) for a, b in pairs]
    return lax.ppermute(value, "tensor", pairs)


class Place:
    def __init__(self):
        dp = lax.axis_index("dp")
        self.core = dp % 2
        self.slots = lax.axis_size("tensor")
        self.slot = lax.axis_index("tensor")
        self.bits = [b for b in range(1, lax.axis_size("dp").bit_length() - 1)]
        self.side = {b: (dp >> b) % 2 for b in range(lax.axis_size("dp").bit_length() - 1)}

    def gather_slots(self, block):
        blocks = [block] + [around(block, d) for d in range(1, self.slots)]
        shape = (block.shape[0], self.slots, block.shape[1])
        index = lax.broadcasted_iota(jnp.int32, shape, 1)
        out = jnp.broadcast_to(block[:, None, :], shape)
        for d in range(1, self.slots):
            from_slot = (self.slot - d) % self.slots
            out = jnp.where(index == from_slot, blocks[d][:, None, :], out)
        return out

    def scatter_slots(self, blocks):
        def block(at):
            return lax.dynamic_index_in_dim(blocks, at % self.slots, 1, keepdims=False)

        total = block(self.slot).astype(f32)
        for d in range(1, self.slots):
            total = total + around(block(self.slot + d), d).astype(f32)
        return total

    def ordered(self, bit, mine, other, axis):
        mine, other = jnp.expand_dims(mine, axis), jnp.expand_dims(other, axis)
        low = self.side[bit] == 0
        return jnp.where(
            low,
            jnp.concatenate([mine, other], axis=axis),
            jnp.concatenate([other, mine], axis=axis),
        )

    def gather_rows(self, block, upward):
        done = block
        for bit in self.bits if upward else self.bits[::-1]:
            axis = 0 if upward else len(done.shape) - 2
            done = self.ordered(bit, done, across(done, bit), axis)
        return done.reshape((-1, block.shape[1]))

    def scatter_rows(self, whole, upward, low_bit=1):
        bits = [b for b in self.bits if b >= low_bit]
        if low_bit == 0:
            bits = [0] + bits
        count = len(bits)
        rows = whole.shape[0] >> count
        left = sorted(bits, reverse=True)
        now = whole.reshape((2,) * count + (rows, whole.shape[1]))
        for bit in bits if upward else bits[::-1]:
            axis = left.index(bit)
            left.remove(bit)
            side = self.side[bit]
            keep = lax.dynamic_index_in_dim(now, side, axis, keepdims=False)
            give = lax.dynamic_index_in_dim(now, 1 - side, axis, keepdims=False)
            now = (keep.astype(f32) + across(give, bit).astype(f32)).astype(whole.dtype)
        return now

    def gather_weight(self, mine, other):
        both = self.ordered(0, mine, other, 0).reshape((-1, mine.shape[1]))
        blocks = self.gather_slots(both)
        half = self.slots // 2
        first = blocks[:, :half].reshape((both.shape[0], -1))
        second = blocks[:, half:].reshape((both.shape[0], -1))
        return jnp.concatenate(
            [self.gather_rows(first, True), self.gather_rows(second, False)], axis=1
        )

    def scatter_weight(self, part):
        columns = part.shape[1] // 2
        half = self.slots // 2
        first = self.scatter_rows(part[:, :columns], False)
        second = self.scatter_rows(part[:, columns:], True)
        rows = first.shape[0]
        blocks = jnp.concatenate(
            [first.reshape((rows, half, -1)), second.reshape((rows, half, -1))], axis=1
        )
        mine = self.scatter_slots(blocks).reshape((2, rows // 2, -1))
        keep = lax.dynamic_index_in_dim(mine, self.core, 0, keepdims=False)
        give = lax.dynamic_index_in_dim(mine, 1 - self.core, 0, keepdims=False)
        out = self.ordered(0, keep, swap(give), 1)
        return out.reshape((rows // 2, -1))

    def sum_chips(self, value):
        for bit in self.bits:
            value = value + across(value, bit)
        return value

    def sum_slots(self, value):
        total = value.astype(f32)
        for d in range(1, self.slots):
            total = total + around(value, d).astype(f32)
        return total


def on_device(
    x_in,
    segment_ids,
    norm_gain,
    w_x,
    w_z,
    w_bc,
    w_dt,
    conv_x,
    conv_x_bias,
    conv_bc,
    conv_bc_bias,
    dt_bias,
    a_log,
    d_skip,
    gate_gain,
    w_out,
    cotangent,
):
    place = Place()
    core, slots, slot = place.core, place.slots, place.slot
    length, features = x_in.shape
    sequences, whole_length = segment_ids.shape
    pieces = whole_length // length
    own_rows = w_x.shape[0]
    slot_channels = w_x.shape[1]
    slot_heads = w_dt.shape[1]
    half_channels = slot_channels // 2
    half_heads = slot_heads // 2
    channels = half_channels * slots
    heads = half_heads * slots
    all_channels = 2 * channels
    all_heads = 2 * heads
    bc_width = w_bc.shape[1]
    n_chunks = length // CH

    def split(weight):
        return weight.reshape((own_rows, 2, half_channels))

    stacked = jnp.stack([split(w_x), split(w_z), split(w_out.T)])
    mine = lax.dynamic_index_in_dim(stacked, core, 2, keepdims=False)
    other = swap(lax.dynamic_index_in_dim(stacked, 1 - core, 2, keepdims=False))
    wx = place.gather_weight(mine[0], other[0])
    dt_slots = place.gather_slots(w_dt).reshape((own_rows, all_heads))
    thin = jnp.concatenate([w_bc, dt_slots, norm_gain[:, None]], axis=1)
    thin = jnp.pad(thin, ((0, 0), (0, bc_width + 128 - thin.shape[1])))
    thin = place.ordered(0, thin, swap(thin), 0).reshape((2 * own_rows, -1))
    thin = place.gather_rows(thin, True)
    wz = place.gather_weight(mine[1], other[1])
    wo = place.gather_weight(mine[2], other[2])

    rows = jnp.concatenate(
        [
            conv_x,
            conv_x_bias[None],
            gate_gain[None],
            jnp.pad(jnp.concatenate([dt_bias, a_log, d_skip])[None], ((0, 0), (0, slot_channels - 3 * slot_heads))),
            jnp.zeros((1, slot_channels), f32),
        ],
        axis=0,
    )
    rows = place.gather_slots(rows)
    own = lax.dynamic_index_in_dim(
        rows.reshape((8, slots, 2, half_channels)), core, 2, keepdims=False
    ).reshape((8, channels))
    gain_row = own[5:6]
    lane = jnp.arange(128)
    head_at = lane % 32
    global_head = (head_at // half_heads) * slot_heads + core * half_heads + head_at % half_heads
    pick = ((lane[:, None] == global_head[None, :]) & (head_at < heads)[None, :]).astype(f32)
    small = rows[6, :, : 3 * slot_heads].reshape((slots, 3, slot_heads)).transpose(1, 0, 2)
    small = jnp.pad(small.reshape((3, all_heads)), ((0, 5), (0, 128 - all_heads)))
    small = exact(small, pick)
    bias_lanes = small[0]
    rate_lanes = jnp.where(head_at < heads, -jnp.exp(small[1]), 0.0)
    to_heads = head_map(channels, f32)
    skip_row = exact(small[2:3] * (lane < 32), to_heads.T)
    cw = jnp.concatenate([own[:5], skip_row, jnp.zeros((2, channels), f32)], axis=0)

    padded = jnp.pad(segment_ids, ((0, 0), (HALO, HALO)), constant_values=-1)
    ids_own = lax.dynamic_slice(
        padded, (slot // pieces, (slot % pieces) * length), (1, length + 2 * HALO)
    )
    ids_all = jnp.concatenate([ids_own, swap(ids_own)], axis=0)
    ids = ids_all[:, HALO : HALO + length]
    before = ids_all[:, HALO - 1]

    def near(k):
        return ids_all[:, HALO + k : HALO + k + length] == ids

    flags = [near(-1), near(-2), near(-3), ids, near(1), near(2), near(3), jnp.zeros_like(ids)]
    flags = jnp.stack([v.astype(f32) for v in flags], axis=-1)

    x_rows = jnp.concatenate([along_sequence(x_in[-HALO:], pieces, True), x_in], axis=0)
    tokens_ext = x_rows.astype(f32)
    inv_ext = lax.rsqrt(jnp.mean(tokens_ext * tokens_ext, axis=-1, keepdims=True) + epsilon)
    gain = thin[:, bc_width + all_heads].astype(f32)[None, :]
    normed_own = (tokens_ext * inv_ext * gain).astype(bf16)
    normed_other = swap(normed_own)
    normed_ext = jnp.concatenate([normed_own, normed_other], axis=0)
    normed = jnp.concatenate([normed_own[HALO:], normed_other[HALO:]], axis=0)
    tokens, inv_rms = tokens_ext[HALO:], inv_ext[HALO:]
    cot = jnp.concatenate([cotangent, swap(cotangent)], axis=0)

    dt_pick = jnp.dot(thin[:, bc_width:], pick.astype(bf16), preferred_element_type=f32).astype(bf16)
    thin_proj = mm(normed_ext, jnp.concatenate([thin[:, :bc_width], dt_pick], axis=1))
    thin_proj = thin_proj.reshape((2, HALO + length, -1))
    bc_ext = thin_proj[:, :, :bc_width]
    dt_in = thin_proj[:, HALO:, bc_width:] + bias_lanes
    x_ext = mm(normed_ext, wx).reshape((2, HALO + length, channels))

    bc_pre = conv_bc_bias + conv_bc[0] * bc_ext[:, HALO:]
    for k in range(1, conv_bc.shape[0]):
        shifted = bc_ext[:, HALO - k : HALO - k + length]
        bc_pre = bc_pre + conv_bc[k] * shifted * flags[:, :, k - 1 : k]
    bc_act = jax.nn.silu(bc_pre)
    bc_turned = bc_act.astype(bf16).transpose(0, 2, 1)
    c_low = bc_act[:, :, bc_width // 2 :].astype(bf16)

    step = jax.nn.softplus(dt_in)
    log_step = (step * rate_lanes).reshape((2 * n_chunks, CH, 128))
    tri = (jnp.arange(CH)[:, None] >= jnp.arange(CH)[None, :]).astype(f32)
    running = jnp.einsum("ts,csh->cth", tri, log_step, precision=highest)
    running = running.reshape((2, n_chunks, CH, 128))
    last = running[:, :, -1:, :]
    ids_chunks = ids.reshape((2, n_chunks, CH, 1))
    chunk_end = ids_chunks[:, :, -1:, :]
    chunk_before = jnp.concatenate(
        [before[:, None, None, None], chunk_end[:, :-1]], axis=1
    )
    still = (chunk_end == chunk_before).astype(f32)
    alpha = still * jnp.exp(last)
    lead = jnp.cumsum(last, axis=1) - last
    since_piece = (ids_chunks == before[:, None, None, None]).astype(f32) * jnp.exp(running + lead)
    since_piece = since_piece.reshape((2 * length, 128))
    group_lane = lane // 32
    hv = jnp.where(
        group_lane == 0,
        running * LOG2E,
        jnp.where(
            group_lane == 1,
            step.reshape((2, n_chunks, CH, 128)),
            jnp.where(
                group_lane == 2,
                (ids_chunks == chunk_before).astype(f32) * jnp.exp(running),
                (ids_chunks == chunk_end).astype(f32) * jnp.exp(last - running),
            ),
        ),
    ).reshape((2, length, 128))
    rv = jnp.concatenate(
        [
            hv[:, :, :24].transpose(0, 2, 1),
            ids.astype(f32)[:, None, :],
            jnp.zeros((2, 7, length), f32),
        ],
        axis=1,
    )
    first_lanes = (lane < 32).astype(f32)
    al = exact((alpha * first_lanes).reshape((2 * n_chunks, 128)), to_heads.T)
    al = al.reshape((2, n_chunks, channels))
    whole_alpha = jnp.prod(al, axis=1, keepdims=True)
    al = jnp.pad(al, ((0, 0), (0, 8 - n_chunks), (0, 0)))
    wide_since = mm((since_piece * first_lanes).astype(bf16), to_heads.T.astype(bf16))
    wide_since = wide_since.reshape((2, length, channels))

    def hand_on(local, forward):
        low = local.astype(bf16)
        for _ in range(pieces - 2):
            came = along_sequence(low, pieces, forward)
            low = (local + whole_alpha * came.astype(f32)).astype(bf16)
        return along_sequence(low, pieces, forward)

    y_here, states = scan_fwd(hv, flags, rv, al, bc_act, bc_turned, x_ext, cw, CH)
    state_in = hand_on(states[:, -1], True)
    y = y_here + wide_since * lax.dot_general(
        c_low, state_in, (((2,), (1,)), ((0,), (0,))), preferred_element_type=f32
    )

    gate_in = mm(normed, wz)
    mixed_grad = mm(cot, wo)
    y = y.reshape((2 * length, channels))
    sig = jax.nn.sigmoid(gate_in)
    act = gate_in * sig
    gated = y * act
    scaled = mixed_grad * gain_row
    sums = jnp.stack([jnp.sum(gated * gated, axis=1), jnp.sum(scaled * gated, axis=1)])
    sums = sums.reshape((2, 2, length))
    sums = (sums + swap(sums)[:, ::-1]).reshape((2, 2 * length))
    gate_rms = lax.rsqrt(sums[0] / all_channels + epsilon)[:, None]
    mixed = (gated * gate_rms * gain_row).astype(bf16)
    gate_gain_part = jnp.sum(mixed_grad * gated * gate_rms, axis=0)
    gated_grad = gate_rms * scaled - gated * gate_rms**3 * (sums[1] / all_channels)[:, None]
    y_grad = (gated_grad * act).reshape((2, length, channels))
    gate_grad = (gated_grad * y * sig * (1.0 + gate_in * (1.0 - sig))).astype(bf16)

    state_grad = lax.dot_general(
        c_low, (y_grad * wide_since).astype(bf16), (((1,), (1,)), ((0,), (0,))), preferred_element_type=f32
    )
    state_grad = hand_on(state_grad, False)
    wo_part = tmm(cot, mixed).astype(bf16)
    w_out_grad = place.scatter_weight(wo_part).T
    branch = mmt(mixed, wo)
    block_out = (tokens + branch[:length] + swap(branch[length:].astype(bf16)).astype(f32)).astype(bf16)
    wz_part = tmm(normed, gate_grad).astype(bf16)
    w_z_grad = place.scatter_weight(wz_part)

    x_low, tail, head, dbc, dcol, drow, dcw = scan_bwd(
        hv, flags, rv, al, bc_act, bc_turned, x_ext, cw, y_grad, states, state_in, state_grad, CH
    )

    head = along_sequence(head, pieces, False)

    def past_end(begin, taps):
        total = jnp.zeros((begin.shape[0], HALO, begin.shape[2]), f32)
        for k in range(1, taps.shape[0]):
            moved = jnp.pad(begin[:, :k], ((0, 0), (HALO - k, 0), (0, 0)))
            total = total + taps[k] * moved * flags[: begin.shape[0], length - HALO :, 3 + k : 4 + k]
        return total

    fixed = (tail + past_end(head, own[:4])).astype(bf16)
    x_low = lax.dynamic_update_slice(x_low, fixed, (0, length - HALO, 0)).reshape((2 * length, channels))

    bc_grad = dbc[0] + swap(dbc[1])
    pre = bc_pre[0]
    sig_bc = jax.nn.sigmoid(pre)
    bc_dpre = bc_grad * (sig_bc * (1.0 + pre * (1.0 - sig_bc)))
    bc_head = along_sequence(bc_dpre[:8], pieces, False)
    bc_raw = conv_bc[0] * bc_dpre
    bc_taps = [jnp.sum(bc_dpre * bc_ext[0, HALO:], axis=0)]
    longer = jnp.concatenate([bc_dpre, bc_head], axis=0)
    for k in range(1, conv_bc.shape[0]):
        bc_raw = bc_raw + conv_bc[k] * longer[k : k + length] * flags[0, :, 3 + k : 4 + k]
        shifted = bc_ext[0, HALO - k : HALO - k + length]
        bc_taps.append(jnp.sum(bc_dpre * shifted * flags[0, :, k - 1 : k], axis=0))
    bc_low = bc_raw.astype(bf16)
    bc_small = jnp.stack(bc_taps + [jnp.sum(bc_dpre, axis=0)] + [jnp.zeros((bc_width,), f32)] * 3)
    bc_small = place.sum_chips(bc_small + swap(bc_small))
    bc_small = place.sum_slots(bc_small)

    dcum = dcol[:, :, :128] - jnp.pad(drow.transpose(0, 2, 1), ((0, 0), (0, 0), (0, 96)))
    dlog = jnp.einsum("ts,csh->cth", tri.T, dcum.reshape((2 * n_chunks, CH, 128)), precision=highest)
    dstep = dcol[:, :, 128:] + dlog.reshape((2, length, 128)) * rate_lanes
    dt_raw = (dstep * jax.nn.sigmoid(dt_in)).reshape((2 * length, 128))
    rate_part = jnp.sum(dlog * log_step, axis=(0, 1))
    place_back = (pick * first_lanes).T.astype(bf16)
    dt_low = mm(dt_raw.astype(bf16), place_back).astype(bf16)

    dcw = jnp.sum(dcw, axis=0)
    head_rows = jnp.stack([jnp.sum(dt_raw, axis=0), rate_part]) * first_lanes
    head_rows = exact(head_rows, to_heads.T)
    packed = jnp.concatenate(
        [dcw[:5], gate_gain_part[None], dcw[5:6], head_rows, jnp.zeros((7, channels), f32)], axis=0
    )
    packed = place.sum_chips(packed).reshape((16, slots, half_channels))
    packed = place.scatter_slots(packed)
    packed = place.ordered(0, packed, swap(packed), 1).reshape((16, slot_channels))
    by_head = packed[6:9].reshape((3, slot_heads, 64))

    wx_part = tmm(normed, x_low).astype(bf16)
    w_x_grad = place.scatter_weight(wx_part)
    thin_low = jnp.concatenate(
        [jnp.concatenate([bc_low, jnp.zeros_like(bc_low)], axis=0), dt_low], axis=1
    )
    thin_part = tmm(normed, thin_low).astype(bf16)
    thin_grad = place.scatter_rows(thin_part, True, low_bit=0)
    thin_grad = place.sum_slots(thin_grad)
    w_bc_grad = thin_grad[:, :bc_width]
    w_dt_grad = lax.dynamic_slice_in_dim(thin_grad, bc_width + slot * slot_heads, slot_heads, 1)

    normed_grad = mmt(x_low, wx) + mmt(gate_grad, wz) + mmt(thin_low, thin)
    normed_grad = normed_grad[:length] + swap(normed_grad[length:].astype(bf16)).astype(f32)
    gain_part = jnp.sum(normed_grad * tokens * inv_rms, axis=0)
    pushed = normed_grad * gain
    x_grad = (
        cotangent.astype(f32)
        + inv_rms * pushed
        - tokens * inv_rms**3 * jnp.mean(pushed * tokens, axis=-1, keepdims=True)
    )
    gain_rows = gain_part.reshape((features // own_rows * 2, own_rows // 2))
    gain_rows = place.scatter_rows(gain_rows, True, low_bit=0)
    norm_gain_grad = place.sum_slots(gain_rows).reshape((own_rows,))
    return (
        block_out,
        x_grad,
        norm_gain_grad,
        w_x_grad,
        w_z_grad,
        w_bc_grad,
        w_dt_grad,
        packed[:4],
        packed[4],
        bc_small[:4],
        bc_small[4],
        by_head[1, :, 0],
        by_head[2, :, 0],
        jnp.sum(by_head[0], axis=1),
        packed[5],
        w_out_grad,
    )


def solution(mesh):
    rows = P(("dp", "tensor"), None)
    both = P("dp", "tensor")
    heads = P("tensor")
    in_specs = (
        rows, P("dp", None), P("dp"), both, both, P("dp", None), both, P(None, "tensor"), heads,
        P(), P(), heads, heads, heads, heads, P("tensor", "dp"), rows,
    )
    out_specs = (
        rows, rows, P("dp"), both, both, P("dp", None), both, P(None, "tensor"), heads,
        P(), P(), heads, heads, heads, heads, P("tensor", "dp"),
    )
    return jax.shard_map(
        on_device, mesh=mesh, in_specs=in_specs, out_specs=out_specs, check_vma=False
    )
```

time: 1450 us -> 886 us (0.61)
  waiting for transfers between devices: 478 us -> 229 us
  matrix products: 337 us -> 108 us
  starting transfers between devices: 0.93 us -> 152 us
  other arithmetic: 225 us -> 104 us
  blocking collectives: 108 us -> 0 us
  Pallas kernels: 0 us -> 87.9 us
  local copies, waits for them, and re-layouts: 274 us -> 192 us
    dot_general x63 -> x23, matrix products: 337 us -> 108 us  [the longest x6 36.6 us: mm(): lax.dot_general(a, b, (((1,), (0,)), ((), ())), preferred_element_type=f32)]
    ppermute x0 -> x91, waiting for transfers between devices: none -> 229 us  [the longest x36 148 us: across(): return lax.ppermute(value, 'dp', [(i, i ^ 1 << bit) for i in range(size)])]
    reduce_scatter x3 -> x0, waiting for transfers between devices: 226 us -> none  [the longest x1 111 us: on_device(): lax.psum_scatter(times_trans(part_cat, w_part).astype(jnp.bfloat16), 'ten...]
    ppermute x0 -> x91, starting transfers between devices: none -> 152 us  [the longest x36 101 us: around(): lax.ppermute(value, 'tensor', [(i, (i + by) % size) for i in range(size)])]
    all_gather x5 -> x0, waiting for transfers between devices: 133 us -> none  [the longest x1 118 us: on_device(): lax.all_gather(normed, 'tensor', axis=0, tiled=True)]
    unnamed x17 -> x0, waiting for transfers between devices: 90 us -> none
    pallas_call x0 -> x2, Pallas kernels: none -> 87.9 us  [the longest x1 60.9 us: scan_bwd(): pl.pallas_call(lambda *refs: scan_bwd_body(n_chunks, rows, *refs), grid=(...]
    reduce_sum x15 -> x6, other arithmetic: 65.6 us -> 7.7 us  [the longest x1 3.32 us: on_device(): gain_part = jnp.sum(normed_grad * tokens * inv_rms, axis=0)]
  transfers between devices with their start and end apart: 13 -> 91, of which waited for: 8 -> 25; matrix products, arithmetic and copies ran while one was open for 22% -> 32% of each run, Pallas kernels for 0% -> 7%
where the time goes in v1:
time: 886 us; the launch traced here: 877 us
  waiting for transfers between devices  229 us (26%)
  local copies, waits for them, and re-layouts  192 us (22%)
  starting transfers between devices  152 us (17%)
  matrix products  108 us (12%)
  other arithmetic  104 us (12%)
  Pallas kernels  87.9 us (10%)
    ppermute x36, waiting for transfers between devices, across(): return lax.ppermute(value, 'dp', [(i, i ^ 1 << bit) for i in range(size)])  148 us
    ppermute x36, starting transfers between devices, around(): lax.ppermute(value, 'tensor', [(i, (i + by) % size) for i in range(size)])  101 us
    ppermute x36, waiting for transfers between devices, around(): lax.ppermute(value, 'tensor', [(i, (i + by) % size) for i in range(size)])  68.3 us
    pallas_call x1, Pallas kernels, scan_bwd(): pl.pallas_call(lambda *refs: scan_bwd_body(n_chunks, rows, *refs), grid=(...  60.9 us
    unnamed x382, local copies, waits for them, and re-layouts  46.5 us
    ppermute x36, starting transfers between devices, across(): return lax.ppermute(value, 'dp', [(i, i ^ 1 << bit) for i in range(size)])  39.5 us
    dot_general x6, matrix products, mm(): lax.dot_general(a, b, (((1,), (0,)), ((), ())), preferred_element_type=f32)  36.6 us
    dot_general x4, matrix products, tmm(): lax.dot_general(a, b, (((0,), (0,)), ((), ())), preferred_element_type=f32)  29.3 us
  transfers between devices with their start and end apart: 91, of which 25 were waited for; matrix products, arithmetic and copies ran while one was open for 32% of the time, Pallas kernels for 7%

profile of v1, /device:TPU:0, one launch (start us, length us, event | category | flops | bytes accessed | tf_op | source)
XLA Modules:
  0.0 876.8 jit_solution(12263046276871793109)
XLA Ops:
  71.1 18.4 %collective-permute-done.14 = bf16[384,384]{1,0:T(8,128)(2,1)S(1)} collective-permute-done((bf16[384,384]{1,0:T(8,128)(2,1)S(1)}, bf16[384,384]{1,0:T(8,128)(2,1)S(1)}, u32[]{:S(2)}, u32[]{:S(2)}) %collective-permute-start.14) | collective-permute-done | bytes 294944 | tf_op jit(solution)/shard_map/ppermute | solution.py:340
  89.4 14.6 %collective-permute-start.30 = (bf16[384,384]{1,0:T(8,128)(2,1)S(1)}, bf16[384,384]{1,0:T(8,128)(2,1)S(1)}, u32[]{:S(2)}, u32[]{:S(2)}) collective-permute-start(bf16[384,384]{1,0:T(8,128)(2,1)S(1)} %bitcast.559), channel_id=1, source_target_pairs={{0,2},{1,3},{2,0},{3,1},{4,6},{5,7},{6,4},{7,5},{8,10},{9,11},{10,... | collective-permute-start | bytes 884744 | tf_op jit(solution)/shard_map/ppermute | solution.py:340
  111.5 15.5 %collective-permute-done.22 = bf16[384,384]{1,0:T(8,128)(2,1)S(1)} collective-permute-done((bf16[384,384]{1,0:T(8,128)(2,1)S(1)}, bf16[384,384]{1,0:T(8,128)(2,1)S(1)}, u32[]{:S(2)}, u32[]{:S(2)}) %collective-permute-start.22) | collective-permute-done | bytes 294944 | tf_op jit(solution)/shard_map/ppermute | solution.py:340
  128.5 10.5 %collective-permute-done.30 = bf16[384,384]{1,0:T(8,128)(2,1)S(1)} collective-permute-done((bf16[384,384]{1,0:T(8,128)(2,1)S(1)}, bf16[384,384]{1,0:T(8,128)(2,1)S(1)}, u32[]{:S(2)}, u32[]{:S(2)}) %collective-permute-start.30) | collective-permute-done | bytes 294944 | tf_op jit(solution)/shard_map/ppermute | solution.py:340
  192.8 12.3 %collective-permute-done.26 = bf16[384,768]{1,0:T(8,128)(2,1)S(1)} collective-permute-done((bf16[384,768]{1,0:T(8,128)(2,1)}, bf16[384,768]{1,0:T(8,128)(2,1)S(1)}, u32[]{:S(2)}, u32[]{:S(2)}) %collective-permute-start.26) | collective-permute-done | bytes 589856 | tf_op jit(solution)/shard_map/ppermute | solution.py:335
  229.0 17.8 %collective-permute-done.27 = bf16[2,384,768]{2,1,0:T(8,128)(2,1)S(1)} collective-permute-done((bf16[2,384,768]{2,1,0:T(8,128)(2,1)S(1)}, bf16[2,384,768]{2,1,0:T(8,128)(2,1)S(1)}, u32[]{:S(2)}, u32[]{:S(2)}) %collective-permute-start.27) | collective-permute-done | bytes 1179680 | tf_op jit(solution)/shard_map/ppermute | solution.py:335
  249.8 43.8 %collective-permute-done.19 = bf16[2,384,768]{2,1,0:T(8,128)(2,1)S(1)} collective-permute-done((bf16[2,384,768]{2,1,0:T(8,128)(2,1)S(1)}, bf16[2,384,768]{2,1,0:T(8,128)(2,1)S(1)}, u32[]{:S(2)}, u32[]{:S(2)}) %collective-permute-start.19) | collective-permute-done | bytes 1179680 | tf_op jit(solution)/shard_map/ppermute | solution.py:335
  303.7 14.1 %collective-permute-done.17 = bf16[2,384,768]{2,1,0:T(8,128)(2,1)S(1)} collective-permute-done((bf16[2,384,768]{2,1,0:T(8,128)(2,1)S(1)}, bf16[2,384,768]{2,1,0:T(8,128)(2,1)S(1)}, u32[]{:S(2)}, u32[]{:S(2)}) %collective-permute-start.17) | collective-permute-done | bytes 1179680 | tf_op jit(solution)/shard_map/ppermute | solution.py:335
  352.3 9.8 %fusion.12 = f32[1056,1536]{1,0:T(8,128)} fusion(bf16[1536,768]{1,0:T(8,128)(2,1)} %bitcast.520, bf16[1536,768]{1,0:T(8,128)(2,1)} %bitcast.522, bf16[528,1536]{1,0:T(8,128)(2,1)} %copy-done.77, bf16[528,1536]{1,0:T(8,128)(2,1)S(1)} %copy-done.14), kind=kOutput, calls=%fused_computation.40 | convolution fusion | flops 4998758400 | bytes 14450688 | tf_op jit(solution)/shard_map/dot_general | solution.py:19
  362.1 27.0 %scan_fwd.1 = (f32[2,512,1536]{2,1,0:T(8,128)}, f32[2,2,128,1536]{3,2,1,0:T(8,128)}) custom-call(f32[2,512,128]{2,1,0:T(8,128)} %copy.426.refs_0_, f32[2,512,8]{2,1,0:T(8,128)} %copy.427.refs_1_, f32[2,32,512]{2,1,0:T(8,128)} %maximum_maximum_fusion.refs_2_, f32[2,8,1536]{2,1,0:T(8,128)} %pad.41.refs_3_, f32[2,512,256]{2,1,0:T(8,128)} %copy.428.refs_4_, ...), custom_call_target="tpu_custom_call" | custom-call | flops 3221225472 | bytes 12582912 | tf_op jit(solution)/shard_map/scan_fwd/pallas_call | solution.py:116
  396.5 8.8 %fusion.11 = f32[1024,1536]{1,0:T(8,128)} fusion(bf16[1536,768]{1,0:T(8,128)(2,1)S(1)} %bitcast.524, bf16[1536,768]{1,0:T(8,128)(2,1)S(1)} %bitcast.530, bf16[512,1536]{1,0:T(8,128)(2,1)S(1)} %slice.506, bf16[512,1536]{1,0:T(8,128)(2,1)} %slice.505), kind=kOutput, calls=%fused_computation.39 | convolution fusion | flops 4847566848 | bytes 14155776 | tf_op jit(solution)/shard_map/dot_general | solution.py:19
  413.2 14.1 %multiply_reduce_fusion.1 = (f32[1024]{0:T(1024)S(1)}, f32[1024]{0:T(1024)S(1)}, f32[1024,1536]{1,0:T(8,128)}, f32[1024,1536]{1,0:T(8,128)}) fusion(f32[1536]{0:T(1024)S(1)} %mul.567, f32[1024,1536]{1,0:T(8,128)} %fusion.11, f32[2,512,1536]{2,1,0:T(8,128)S(1)} %multiply_add_fusion, bf16[1024,1536]{1,0:T(8,128)(2,1)} %copy-done.85, ...), kind=kOutput, calls=%fused_computation.13 | convolution fusion | flops 4857001984 | bytes 33044480 | tf_op jit(solution)/shard_map/dot_general | solution.py:19
  434.8 10.7 %convolution_convert_fusion = bf16[1536,1536]{1,0:T(8,128)(2,1)} fusion(bf16[1024,1536]{1,0:T(8,128)(2,1)} %copy-done.85, f32[1024,1536]{1,0:T(8,128)} %get-tuple-element.144, f32[1024]{0:T(1024)S(1)} %bitcast.580, f32[1536]{0:T(1024)S(1)} %mul.567), kind=kOutput, calls=%fused_computation | convolution fusion | flops 4838916096 | bytes 14166016 | tf_op jit(solution)/shard_map/dot_general | solution.py:27
  447.4 8.0 fusion.2
  469.2 7.2 fusion.8
  517.7 60.9 %scan_bwd.1 = (bf16[2,512,1536]{2,1,0:T(8,128)(2,1)}, f32[2,16,1536]{2,1,0:T(8,128)}, f32[2,8,1536]{2,1,0:T(8,128)}, f32[2,512,256]{2,1,0:T(8,128)}, f32[2,512,2...) custom-call(f32[2,512,128]{2,1,0:T(8,128)} %copy.426.refs_0_, f32[2,512,8]{2,1,0:T(8,128)} %copy.427.refs_1_, ...), custom_call_target="tpu_custom_call" | custom-call | flops 9663676416 | bytes 18874368 | tf_op jit(solution)/shard_map/scan_bwd/pallas_call | solution.py:278
  593.6 7.5 convolution_convert_fusion.2
  663.1 8.8 add_add_fusion
  691.1 32.1 %collective-permute-done.60 = bf16[384,768]{0,1:T(8,128)(2,1)S(1)} collective-permute-done((bf16[384,768]{0,1:T(8,128)(2,1)S(1)}, bf16[384,768]{0,1:T(8,128)(2,1)S(1)}, u32[]{:S(2)}, u32[]{:S(2)}) %collective-permute-start.60) | collective-permute-done | bytes 589856 | tf_op jit(solution)/shard_map/ppermute | solution.py:335
  734.9 9.7 %collective-permute-start.61 = (bf16[384,384]{0,1:T(8,128)(2,1)}, bf16[384,384]{0,1:T(8,128)(2,1)}, u32[]{:S(2)}, u32[]{:S(2)}) collective-permute-start(bf16[384,384]{0,1:T(8,128)(2,1)} %get-tuple-element.196), channel_id=1, source_target_pairs={{0,1},{1,2},{2,3},{3,0},{4,5},{5,6},{6,7},{7,4},{8,9},{9,10},{10,1... | collective-permute-start | bytes 884744 | tf_op jit(solution)/shard_map/ppermute | solution.py:340
  744.6 8.9 %collective-permute-done.88 = bf16[384,384]{0,1:T(8,128)(2,1)S(1)} collective-permute-done((bf16[384,384]{0,1:T(8,128)(2,1)S(1)}, bf16[384,384]{0,1:T(8,128)(2,1)S(1)}, u32[]{:S(2)}, u32[]{:S(2)}) %collective-permute-start.88) | collective-permute-done | bytes 294944 | tf_op jit(solution)/shard_map/ppermute | solution.py:340
  753.5 10.1 %collective-permute-start.63 = (bf16[384,384]{0,1:T(8,128)(2,1)}, bf16[384,384]{0,1:T(8,128)(2,1)}, u32[]{:S(2)}, u32[]{:S(2)}) collective-permute-start(bf16[384,384]{0,1:T(8,128)(2,1)} %get-tuple-element.198), channel_id=1, source_target_pairs={{0,3},{1,0},{2,1},{3,2},{4,7},{5,4},{6,5},{7,6},{8,11},{9,8},{10,9... | collective-permute-start | bytes 884744 | tf_op jit(solution)/shard_map/ppermute | solution.py:340
  784.6 12.9 %collective-permute-done.67 = bf16[192,384]{1,0:T(8,128)(2,1)S(1)} collective-permute-done((bf16[192,384]{1,0:T(8,128)(2,1)S(1)}, bf16[192,384]{1,0:T(8,128)(2,1)S(1)}, u32[]{:S(2)}, u32[]{:S(2)}) %collective-permute-start.67) | collective-permute-done | bytes 147488 | tf_op jit(solution)/shard_map/ppermute | solution.py:335
  843.7 12.0 %collective-permute-start.47 = (f32[2,96]{1,0:T(2,128)}, f32[2,96]{1,0:T(2,128)}, u32[]{:S(2)}, u32[]{:S(2)}) collective-permute-start(f32[2,96]{1,0:T(2,128)} %fusion.167), channel_id=1, source_target_pairs={{0,2},{1,3},{2,0},{3,1},{4,6},{5,7},{6,4},{7,5},{8,10},{9,11},{10,... | collective-permute-start | bytes 2312 | tf_op jit(solution)/shard_map/ppermute | solution.py:340
  (880 shorter events, 477.2 us)
Async XLA Ops:
  0.7 40.9 %collective-permute-start.1 = (bf16[192,12]{0,1:T(8,128)(2,1)}, bf16[192,12]{0,1:T(8,128)(2,1)S(1)}, u32[]{:S(2)}, u32[]{:S(2)}) collective-permute-start(bf16[192,12]{0,1:T(8,128)(2,1)} %param.23), channel_id=1, source_target_pairs={{0,3},{1,0},{2,1},{3,2},{4,7},{5,4},{6,5},{7,6},{8,11},{9,8},{10,9... | collective-permute-start | bytes 13832 | tf_op jit(solution)/shard_map/ppermute | solution.py:340
  5.8 37.2 %collective-permute-start.2 = (bf16[192,12]{0,1:T(8,128)(2,1)}, bf16[192,12]{0,1:T(8,128)(2,1)S(1)}, u32[]{:S(2)}, u32[]{:S(2)}) collective-permute-start(bf16[192,12]{0,1:T(8,128)(2,1)} %param.23), channel_id=1, source_target_pairs={{0,2},{1,3},{2,0},{3,1},{4,6},{5,7},{6,4},{7,5},{8,10},{9,11},{10,... | collective-permute-start | bytes 13832 | tf_op jit(solution)/shard_map/ppermute | solution.py:340
  5.8 37.4 %collective-permute-start.3 = (bf16[192,12]{0,1:T(8,128)(2,1)}, bf16[192,12]{0,1:T(8,128)(2,1)S(1)}, u32[]{:S(2)}, u32[]{:S(2)}) collective-permute-start(bf16[192,12]{0,1:T(8,128)(2,1)} %param.23), channel_id=1, source_target_pairs={{0,1},{1,2},{2,3},{3,0},{4,5},{5,6},{6,7},{7,4},{8,9},{9,10},{10,1... | collective-permute-start | bytes 13832 | tf_op jit(solution)/shard_map/ppermute | solution.py:340
  64.3 39.7 %collective-permute-start.21 = (bf16[384,384]{1,0:T(8,128)(2,1)S(1)}, bf16[384,384]{1,0:T(8,128)(2,1)S(1)}, u32[]{:S(2)}, u32[]{:S(2)}) collective-permute-start(bf16[384,384]{1,0:T(8,128)(2,1)S(1)} %bitcast.554), channel_id=1, source_target_pairs={{0,3},{1,0},{2,1},{3,2},{4,7},{5,4},{6,5},{7,6},{8,11},{9,8},{10,9... | collective-permute-start | bytes 884744 | tf_op jit(solution)/shard_map/ppermute | solution.py:340
  68.4 58.6 %collective-permute-start.22 = (bf16[384,384]{1,0:T(8,128)(2,1)S(1)}, bf16[384,384]{1,0:T(8,128)(2,1)S(1)}, u32[]{:S(2)}, u32[]{:S(2)}) collective-permute-start(bf16[384,384]{1,0:T(8,128)(2,1)S(1)} %bitcast.555), channel_id=1, source_target_pairs={{0,2},{1,3},{2,0},{3,1},{4,6},{5,7},{6,4},{7,5},{8,10},{9,11},{10,... | collective-permute-start | bytes 884744 | tf_op jit(solution)/shard_map/ppermute | solution.py:340
  71.0 56.0 %collective-permute-start.23 = (bf16[384,384]{1,0:T(8,128)(2,1)S(1)}, bf16[384,384]{1,0:T(8,128)(2,1)S(1)}, u32[]{:S(2)}, u32[]{:S(2)}) collective-permute-start(bf16[384,384]{1,0:T(8,128)(2,1)S(1)} %bitcast.556), channel_id=1, source_target_pairs={{0,1},{1,2},{2,3},{3,0},{4,5},{5,6},{6,7},{7,4},{8,9},{9,10},{10,1... | collective-permute-start | bytes 884744 | tf_op jit(solution)/shard_map/ppermute | solution.py:340
  89.4 39.1 %collective-permute-start.29 = (bf16[384,384]{1,0:T(8,128)(2,1)S(1)}, bf16[384,384]{1,0:T(8,128)(2,1)S(1)}, u32[]{:S(2)}, u32[]{:S(2)}) collective-permute-start(bf16[384,384]{1,0:T(8,128)(2,1)S(1)} %bitcast.558), channel_id=1, source_target_pairs={{0,3},{1,0},{2,1},{3,2},{4,7},{5,4},{6,5},{7,6},{8,11},{9,8},{10,9... | collective-permute-start | bytes 884744 | tf_op jit(solution)/shard_map/ppermute | solution.py:340
  89.4 49.6 %collective-permute-start.30 = (bf16[384,384]{1,0:T(8,128)(2,1)S(1)}, bf16[384,384]{1,0:T(8,128)(2,1)S(1)}, u32[]{:S(2)}, u32[]{:S(2)}) collective-permute-start(bf16[384,384]{1,0:T(8,128)(2,1)S(1)} %bitcast.559), channel_id=1, source_target_pairs={{0,2},{1,3},{2,0},{3,1},{4,6},{5,7},{6,4},{7,5},{8,10},{9,11},{10,... | collective-permute-start | bytes 884744 | tf_op jit(solution)/shard_map/ppermute | solution.py:340
  127.0 101.0 %collective-permute-start.28 = (bf16[512,1536]{1,0:T(8,128)(2,1)}, bf16[512,1536]{1,0:T(8,128)(2,1)}, u32[]{:S(2)}, u32[]{:S(2)}) collective-permute-start(bf16[512,1536]{1,0:T(8,128)(2,1)} %param.33), channel_id=1, source_target_pairs={{0,4},{4,0},{8,12},{12,8},{16,20},{20,16},{24,28},{28,24},{1,5},{5... | collective-permute-start | bytes 4718600 | tf_op jit(solution)/shard_map/ppermute | solution.py:330
  127.0 54.7 %collective-permute-start.6 = (bf16[2,384,384]{2,1,0:T(8,128)(2,1)}, bf16[2,384,384]{2,1,0:T(8,128)(2,1)}, u32[]{:S(2)}, u32[]{:S(2)}) collective-permute-start(bf16[2,384,384]{2,1,0:T(8,128)(2,1)} %maximum_select_fusion.18), channel_id=1, source_target_pairs={{0,16},{4,20},{8,24},{12,28},{16,0},{20,4},{24,8},{28,12},{1,17},{... | collective-permute-start | bytes 1769480 | tf_op jit(solution)/shard_map/ppermute | solution.py:335
  216.1 82.4 %collective-permute-start.33 = (bf16[2,384,768]{2,1,0:T(8,128)(2,1)S(1)}, bf16[2,384,768]{2,1,0:T(8,128)(2,1)S(1)}, u32[]{:S(2)}, u32[]{:S(2)}) collective-permute-start(bf16[2,384,768]{2,1,0:T(8,128)(2,1)S(1)} %maximum_select_fusion.15), channel_id=1, source_target_pairs={{0,16},{4,20},{8,24},{12,28},{16,0},{20,4},{24,8},{28,12},{1,17},{... | collective-permute-start | bytes 3538952 | tf_op jit(solution)/shard_map/ppermute | solution.py:335
  219.0 81.1 %collective-permute-start.35 = (bf16[2,384,768]{2,1,0:T(8,128)(2,1)S(1)}, bf16[2,384,768]{2,1,0:T(8,128)(2,1)S(1)}, u32[]{:S(2)}, u32[]{:S(2)}) collective-permute-start(bf16[2,384,768]{2,1,0:T(8,128)(2,1)S(1)} %maximum_select_fusion.16), channel_id=1, source_target_pairs={{0,8},{4,12},{8,0},{12,4},{16,24},{20,28},{24,16},{28,20},{1,9},{5... | collective-permute-start | bytes 3538952 | tf_op jit(solution)/shard_map/ppermute | solution.py:335
  221.5 72.1 %collective-permute-start.19 = (bf16[2,384,768]{2,1,0:T(8,128)(2,1)S(1)}, bf16[2,384,768]{2,1,0:T(8,128)(2,1)S(1)}, u32[]{:S(2)}, u32[]{:S(2)}) collective-permute-start(bf16[2,384,768]{2,1,0:T(8,128)(2,1)S(1)} %maximum_select_fusion.9), channel_id=1, source_target_pairs={{0,8},{4,12},{8,0},{12,4},{16,24},{20,28},{24,16},{28,20},{1,9},{5... | collective-permute-start | bytes 3538952 | tf_op jit(solution)/shard_map/ppermute | solution.py:335
  229.0 90.6 %collective-permute-start.7 = (bf16[528,1536]{1,0:T(8,128)(2,1)S(1)}, bf16[528,1536]{1,0:T(8,128)(2,1)S(1)}, u32[]{:S(2)}, u32[]{:S(2)}) collective-permute-start(bf16[528,1536]{1,0:T(8,128)(2,1)S(1)} %copy-done.13), channel_id=1, source_target_pairs={{0,4},{4,0},{8,12},{12,8},{16,20},{20,16},{24,28},{28,24},{1,5},{5... | collective-permute-start | bytes 4866056 | tf_op jit(solution)/shard_map/ppermute | solution.py:330
  246.8 55.2 %collective-permute-start.25 = (bf16[2,384,768]{2,1,0:T(8,128)(2,1)S(1)}, bf16[2,384,768]{2,1,0:T(8,128)(2,1)S(1)}, u32[]{:S(2)}, u32[]{:S(2)}) collective-permute-start(bf16[2,384,768]{2,1,0:T(8,128)(2,1)S(1)} %maximum_select_fusion.11), channel_id=1, source_target_pairs={{0,16},{4,20},{8,24},{12,28},{16,0},{20,4},{24,8},{28,12},{1,17},{... | collective-permute-start | bytes 3538952 | tf_op jit(solution)/shard_map/ppermute | solution.py:335
  480.3 149.9 %collective-permute-start.85 = (bf16[2,384,768]{1,2,0:T(8,128)(2,1)}, bf16[2,384,768]{1,2,0:T(8,128)(2,1)}, u32[]{:S(2)}, u32[]{:S(2)}) collective-permute-start(bf16[2,384,768]{1,2,0:T(8,128)(2,1)} %bitcast.545), channel_id=1, source_target_pairs={{0,8},{4,12},{8,0},{12,4},{16,24},{20,28},{24,16},{28,20},{1,9},{5... | collective-permute-start | bytes 3538952 | tf_op jit(solution)/shard_map/ppermute | solution.py:335
  486.8 148.4 %collective-permute-start.83 = (bf16[2,384,768]{1,2,0:T(8,128)(2,1)}, bf16[2,384,768]{1,2,0:T(8,128)(2,1)}, u32[]{:S(2)}, u32[]{:S(2)}) collective-permute-start(bf16[2,384,768]{1,2,0:T(8,128)(2,1)} %bitcast.170), channel_id=1, source_target_pairs={{0,16},{4,20},{8,24},{12,28},{16,0},{20,4},{24,8},{28,12},{1,17},{... | collective-permute-start | bytes 3538952 | tf_op jit(solution)/shard_map/ppermute | solution.py:335
  633.7 53.7 %collective-permute-start.86 = (bf16[384,768]{0,1:T(8,128)(2,1)}, bf16[384,768]{0,1:T(8,128)(2,1)}, u32[]{:S(2)}, u32[]{:S(2)}) collective-permute-start(bf16[384,768]{0,1:T(8,128)(2,1)} %dynamic-slice_bitcast_fusion), channel_id=1, source_target_pairs={{0,16},{4,20},{8,24},{12,28},{16,0},{20,4},{24,8},{28,12},{1,17},{... | collective-permute-start | bytes 1769480 | tf_op jit(solution)/shard_map/ppermute | solution.py:335
  637.8 51.5 %collective-permute-start.84 = (bf16[384,768]{0,1:T(8,128)(2,1)}, bf16[384,768]{0,1:T(8,128)(2,1)}, u32[]{:S(2)}, u32[]{:S(2)}) collective-permute-start(bf16[384,768]{0,1:T(8,128)(2,1)} %dynamic-slice_bitcast_fusion.1), channel_id=1, source_target_pairs={{0,8},{4,12},{8,0},{12,4},{16,24},{20,28},{24,16},{28,20},{1,9},{5... | collective-permute-start | bytes 1769480 | tf_op jit(solution)/shard_map/ppermute | solution.py:335
  682.8 92.9 %collective-permute-start.51 = (bf16[2,384,768]{1,2,0:T(8,128)(2,1)}, bf16[2,384,768]{1,2,0:T(8,128)(2,1)}, u32[]{:S(2)}, u32[]{:S(2)}) collective-permute-start(bf16[2,384,768]{1,2,0:T(8,128)(2,1)} %bitcast.114), channel_id=1, source_target_pairs={{0,8},{4,12},{8,0},{12,4},{16,24},{20,28},{24,16},{28,20},{1,9},{5... | collective-permute-start | bytes 3538952 | tf_op jit(solution)/shard_map/ppermute | solution.py:335
  684.3 97.1 %collective-permute-start.49 = (bf16[2,384,768]{1,2,0:T(8,128)(2,1)}, bf16[2,384,768]{1,2,0:T(8,128)(2,1)}, u32[]{:S(2)}, u32[]{:S(2)}) collective-permute-start(bf16[2,384,768]{1,2,0:T(8,128)(2,1)} %bitcast.108), channel_id=1, source_target_pairs={{0,16},{4,20},{8,24},{12,28},{16,0},{20,4},{24,8},{28,12},{1,17},{... | collective-permute-start | bytes 3538952 | tf_op jit(solution)/shard_map/ppermute | solution.py:335
  685.2 38.1 %collective-permute-start.60 = (bf16[384,768]{0,1:T(8,128)(2,1)S(1)}, bf16[384,768]{0,1:T(8,128)(2,1)S(1)}, u32[]{:S(2)}, u32[]{:S(2)}) collective-permute-start(bf16[384,768]{0,1:T(8,128)(2,1)S(1)} %copy-done.87), channel_id=1, source_target_pairs={{0,16},{4,20},{8,24},{12,28},{16,0},{20,4},{24,8},{28,12},{1,17},{... | collective-permute-start | bytes 1769480 | tf_op jit(solution)/shard_map/ppermute | solution.py:335
  768.8 48.4 %collective-permute-start.42 = (bf16[512,1536]{1,0:T(8,128)(2,1)}, bf16[512,1536]{1,0:T(8,128)(2,1)}, u32[]{:S(2)}, u32[]{:S(2)}) collective-permute-start(bf16[512,1536]{1,0:T(8,128)(2,1)} %slice.719), channel_id=1, source_target_pairs={{0,4},{4,0},{8,12},{12,8},{16,20},{20,16},{24,28},{28,24},{1,5},{5... | collective-permute-start | bytes 4718600 | tf_op jit(solution)/shard_map/ppermute | solution.py:330
  807.1 59.5 %collective-permute-start.37 = (bf16[512,1536]{1,0:T(8,128)(2,1)}, bf16[512,1536]{1,0:T(8,128)(2,1)}, u32[]{:S(2)}, u32[]{:S(2)}) collective-permute-start(bf16[512,1536]{1,0:T(8,128)(2,1)} %slice.720), channel_id=1, source_target_pairs={{0,4},{4,0},{8,12},{12,8},{16,20},{20,16},{24,28},{28,24},{1,5},{5... | collective-permute-start | bytes 4718600 | tf_op jit(solution)/shard_map/ppermute | solution.py:330
  (233 other events, 2799.5 us)

commit v2 on v1

--- a/solution.py
+++ b/solution.py
@@ -107,23 +107,23 @@
         st_ref[0, c] = state
 
 
-def scan_fwd(hv, fl, rv, al, bc, bt, x_ext, cw, rows):
-    pieces, length, _ = hv.shape
+def scan_fwd(hv, fl, rv, al, bc, bt, x_ext, cw, rows, first=0, count=2):
+    length = hv.shape[1]
     n_chunks = length // rows
     width = GROUP * 64
     channels = x_ext.shape[2]
     groups = channels // width
     return pl.pallas_call(
         lambda *refs: scan_fwd_body(n_chunks, rows, *refs),
-        grid=(pieces, groups),
+        grid=(count, groups),
         in_specs=[
-            pl.BlockSpec((1, length, 128), lambda s, g: (s, 0, 0)),
-            pl.BlockSpec((1, length, 8), lambda s, g: (s, 0, 0)),
-            pl.BlockSpec((1, 32, length), lambda s, g: (s, 0, 0)),
-            pl.BlockSpec((1, 8, width), lambda s, g: (s, 0, g)),
-            pl.BlockSpec((1, length, 256), lambda s, g: (s, 0, 0)),
-            pl.BlockSpec((1, 256, length), lambda s, g: (s, 0, 0)),
-            pl.BlockSpec((1, HALO + length, width), lambda s, g: (s, 0, g)),
+            pl.BlockSpec((1, length, 128), lambda s, g: (first + s, 0, 0)),
+            pl.BlockSpec((1, length, 8), lambda s, g: (first + s, 0, 0)),
+            pl.BlockSpec((1, 32, length), lambda s, g: (first + s, 0, 0)),
+            pl.BlockSpec((1, 8, width), lambda s, g: (first + s, 0, g)),
+            pl.BlockSpec((1, length, 256), lambda s, g: (first + s, 0, 0)),
+            pl.BlockSpec((1, 256, length), lambda s, g: (first + s, 0, 0)),
+            pl.BlockSpec((1, HALO + length, width), lambda s, g: (first + s, 0, g)),
             pl.BlockSpec((8, width), lambda s, g: (0, g)),
         ],
         out_specs=[
@@ -131,14 +131,14 @@
             pl.BlockSpec((1, n_chunks, 128, width), lambda s, g: (s, 0, 0, g)),
         ],
         out_shape=[
-            jax.ShapeDtypeStruct((pieces, length, channels), f32),
-            jax.ShapeDtypeStruct((pieces, n_chunks, 128, channels), f32),
+            jax.ShapeDtypeStruct((count, length, channels), f32),
+            jax.ShapeDtypeStruct((count, n_chunks, 128, channels), f32),
         ],
         scratch_shapes=[pltpu.VMEM((n_chunks, rows, rows), f32)],
         cost_estimate=pl.CostEstimate(
-            flops=pieces * groups * GROUP * length * (rows + 256) * 128 * 2,
-            transcendentals=pieces * groups * GROUP * length * rows,
-            bytes_accessed=pieces * length * channels * 8,
+            flops=count * groups * GROUP * length * (rows + 256) * 128 * 2,
+            transcendentals=count * groups * GROUP * length * rows,
+            bytes_accessed=count * length * channels * 8,
         ),
         name="scan_fwd",
     )(hv, fl, rv, al, bc, bt, x_ext, cw)
@@ -268,8 +268,8 @@
             dbc_ref[0, at, :128] += tmm(grad, bc_ref[0, at, 128:].astype(bf16))
 
 
-def scan_bwd(hv, fl, rv, al, bc, bt, x_ext, cw, dy, states, s_recv, r_recv, rows):
-    pieces, length, _ = hv.shape
+def scan_bwd(hv, fl, rv, al, bc, bt, x_ext, cw, dy, states, s_recv, r_recv, rows, first=0, count=2):
+    length = hv.shape[1]
     n_chunks = length // rows
     width = GROUP * 64
     channels = x_ext.shape[2]
@@ -277,20 +277,20 @@
     seg = head_map(channels, f32)
     return pl.pallas_call(
         lambda *refs: scan_bwd_body(n_chunks, rows, *refs),
-        grid=(pieces, groups),
+        grid=(count, groups),
         in_specs=[
-            pl.BlockSpec((1, length, 128), lambda s, g: (s, 0, 0)),
-            pl.BlockSpec((1, length, 8), lambda s, g: (s, 0, 0)),
-            pl.BlockSpec((1, 32, length), lambda s, g: (s, 0, 0)),
-            pl.BlockSpec((1, 8, width), lambda s, g: (s, 0, g)),
-            pl.BlockSpec((1, length, 256), lambda s, g: (s, 0, 0)),
-            pl.BlockSpec((1, 256, length), lambda s, g: (s, 0, 0)),
-            pl.BlockSpec((1, HALO + length, width), lambda s, g: (s, 0, g)),
+            pl.BlockSpec((1, length, 128), lambda s, g: (first + s, 0, 0)),
+            pl.BlockSpec((1, length, 8), lambda s, g: (first + s, 0, 0)),
+            pl.BlockSpec((1, 32, length), lambda s, g: (first + s, 0, 0)),
+            pl.BlockSpec((1, 8, width), lambda s, g: (first + s, 0, g)),
+            pl.BlockSpec((1, length, 256), lambda s, g: (first + s, 0, 0)),
+            pl.BlockSpec((1, 256, length), lambda s, g: (first + s, 0, 0)),
+            pl.BlockSpec((1, HALO + length, width), lambda s, g: (first + s, 0, g)),
             pl.BlockSpec((8, width), lambda s, g: (0, g)),
-            pl.BlockSpec((1, length, width), lambda s, g: (s, 0, g)),
-            pl.BlockSpec((1, n_chunks, 128, width), lambda s, g: (s, 0, 0, g)),
-            pl.BlockSpec((1, 128, width), lambda s, g: (s, 0, g)),
-            pl.BlockSpec((1, 128, width), lambda s, g: (s, 0, g)),
+            pl.BlockSpec((1, length, width), lambda s, g: (first + s, 0, g)),
+            pl.BlockSpec((1, n_chunks, 128, width), lambda s, g: (first + s, 0, 0, g)),
+            pl.BlockSpec((1, 128, width), lambda s, g: (first + s, 0, g)),
+            pl.BlockSpec((1, 128, width), lambda s, g: (first + s, 0, g)),
             pl.BlockSpec((width, 128), lambda s, g: (g, 0)),
         ],
         out_specs=[
@@ -303,13 +303,13 @@
             pl.BlockSpec((1, 8, width), lambda s, g: (s, 0, g)),
         ],
         out_shape=[
-            jax.ShapeDtypeStruct((pieces, length, channels), bf16),
-            jax.ShapeDtypeStruct((pieces, 16, channels), f32),
-            jax.ShapeDtypeStruct((pieces, 8, channels), f32),
-            jax.ShapeDtypeStruct((pieces, length, 256), f32),
-            jax.ShapeDtypeStruct((pieces, length, 256), f32),
-            jax.ShapeDtypeStruct((pieces, 32, length), f32),
-            jax.ShapeDtypeStruct((pieces, 8, channels), f32),
+            jax.ShapeDtypeStruct((count, length, channels), bf16),
+            jax.ShapeDtypeStruct((count, 16, channels), f32),
+            jax.ShapeDtypeStruct((count, 8, channels), f32),
+            jax.ShapeDtypeStruct((count, length, 256), f32),
+            jax.ShapeDtypeStruct((count, length, 256), f32),
+            jax.ShapeDtypeStruct((count, 32, length), f32),
+            jax.ShapeDtypeStruct((count, 8, channels), f32),
         ],
         scratch_shapes=[
             pltpu.VMEM((n_chunks, rows, rows), f32),
@@ -317,14 +317,113 @@
             pltpu.VMEM((length + 8, width), f32),
         ],
         cost_estimate=pl.CostEstimate(
-            flops=pieces * groups * GROUP * length * (rows + 256) * 128 * 6,
-            transcendentals=pieces * groups * GROUP * length * rows,
-            bytes_accessed=pieces * length * channels * 12,
+            flops=count * groups * GROUP * length * (rows + 256) * 128 * 6,
+            transcendentals=count * groups * GROUP * length * rows,
+            bytes_accessed=count * length * channels * 12,
         ),
         name="scan_bwd",
     )(hv, fl, rv, al, bc, bt, x_ext, cw, dy, states, s_recv, r_recv, seg)
 
 
+def project_body(places, at_ref, act_ref, *refs):
+    blocks, out_ref, full_ref = refs[:-2], refs[-2], refs[-1]
+
+    @pl.when(pl.program_id(0) == 0)
+    def _():
+        for ref, (d, k) in zip(blocks, places):
+            rows, columns = ref.shape[1:]
+            row = pl.multiple_of(at_ref[k], rows)
+            column = pl.multiple_of(at_ref[4 + d], columns)
+            full_ref[pl.ds(row, rows), pl.ds(column, columns)] = ref[0]
+
+    out_ref[...] = mm(act_ref[...], full_ref[...])
+
+
+def project(act, at, items, weight, channels):
+    rows, features = act.shape
+    tile = rows // 3 if rows % 48 == 0 else rows // 4
+    blocks = [item[0] for item in items]
+    places = [item[1:] for item in items]
+    return pl.pallas_call(
+        lambda *refs: project_body(places, *refs),
+        grid_spec=pltpu.PrefetchScalarGridSpec(
+            num_scalar_prefetch=1,
+            grid=(rows // tile,),
+            in_specs=[pl.BlockSpec((tile, features), lambda i, at: (i, 0))]
+            + [
+                pl.BlockSpec((1,) + b.shape[1:], lambda i, at: (weight, 0, 0), pipeline_mode=pl.Buffered(1))
+                for b in blocks
+            ],
+            out_specs=[
+                pl.BlockSpec((tile, channels), lambda i, at: (i, 0)),
+                pl.BlockSpec((features, channels), lambda i, at: (0, 0), pipeline_mode=pl.Buffered(1)),
+            ],
+        ),
+        out_shape=[
+            jax.ShapeDtypeStruct((rows, channels), f32),
+            jax.ShapeDtypeStruct((features, channels), bf16),
+        ],
+        cost_estimate=pl.CostEstimate(
+            flops=2 * rows * features * channels,
+            transcendentals=0,
+            bytes_accessed=rows * features * 2 + rows * channels * 4 + features * channels * 4,
+        ),
+        name="project",
+    )(at, act, *blocks)
+
+
+def weight_parts_body(count, group, flip, at_ref, *refs):
+    keep_ref, give_ref = refs[-2:]
+    rows, columns = keep_ref.shape[3:]
+    per = (len(refs) - 2 - count) // count
+    for w in range(count):
+        left_ref, right_refs = refs[w], refs[count + w * per : count + (w + 1) * per]
+
+        @pl.when(pl.program_id(0) == w)
+        def _():
+            rights = [
+                jnp.concatenate(
+                    [ref[:, pl.ds(pl.multiple_of(at_ref[4 + d], columns), columns)] for d in group], axis=1
+                )
+                for ref in right_refs
+            ]
+            tokens = right_refs[0].shape[0]
+            for k in range(4):
+                left = pl.ds(pl.multiple_of(at_ref[k], rows), rows)
+                part = mm(left_ref[left, :tokens], rights[0])
+                for i in range(1, per):
+                    part = part + mm(left_ref[left, i * tokens : (i + 1) * tokens], rights[i])
+                part = part.astype(bf16)
+                away, place = (k // 2, k % 2) if flip == 0 else (k % 2, k // 2)
+                target = give_ref if away else keep_ref
+                for i in range(len(group)):
+                    target[0, i, place] = part[:, i * columns : (i + 1) * columns]
+
+
+def weight_parts(at, lefts, rights, group, own_rows, columns, flip):
+    rights = [piece for right in rights for piece in right]
+    count = len(lefts)
+    shape = (count, len(group), 2, 2 * own_rows, columns)
+    whole = lambda v: pl.BlockSpec(v.shape, lambda w, at: (0, 0), pipeline_mode=pl.Buffered(1))
+    tokens = lefts[0].shape[1]
+    return pl.pallas_call(
+        lambda *refs: weight_parts_body(count, group, flip, *refs),
+        grid_spec=pltpu.PrefetchScalarGridSpec(
+            num_scalar_prefetch=1,
+            grid=(count,),
+            in_specs=[whole(v) for v in lefts] + [whole(v) for v in rights],
+            out_specs=[pl.BlockSpec((1,) + shape[1:], lambda w, at: (w, 0, 0, 0, 0))] * 2,
+        ),
+        out_shape=[jax.ShapeDtypeStruct(shape, bf16)] * 2,
+        cost_estimate=pl.CostEstimate(
+            flops=2 * count * tokens * 8 * own_rows * columns * len(group),
+            transcendentals=0,
+            bytes_accessed=count * tokens * (8 * own_rows + columns * len(group)) * 2,
+        ),
+        name="weight_parts",
+    )(at, *lefts, *rights)
+
+
 def swap(value):
     size = lax.axis_size("dp")
     return lax.ppermute(value, "dp", [(i, i ^ 1) for i in range(size)])
@@ -337,6 +436,7 @@
 
 def around(value, by):
     size = lax.axis_size("tensor")
+    by = by % size
     return lax.ppermute(value, "tensor", [(i, (i + by) % size) for i in range(size)])
 
 
@@ -434,6 +534,54 @@
         out = self.ordered(0, keep, swap(give), 1)
         return out.reshape((rows // 2, -1))
 
+    def fast(self, half_channels):
+        return len(self.bits) == 2 and half_channels % 128 == 0
+
+    def offsets(self, own_rows, half_channels):
+        chip = lax.axis_index("dp") // 2
+        rows = [(chip ^ k) * 2 * own_rows for k in range(4)]
+        columns = [(self.slot - d) % self.slots * half_channels for d in range(self.slots)]
+        return jnp.stack(rows + columns).astype(jnp.int32)
+
+    def unit(self, d, block):
+        first, second = self.bits if d % 2 == 0 else self.bits[::-1]
+        return across(block, first), across(block, second)
+
+    def forward(self, d, one):
+        return across(one, self.bits[1] if d % 2 == 0 else self.bits[0])
+
+    def items(self, d, here, one, two, both):
+        order = (here, one, two, both) if d % 2 == 0 else (here, two, one, both)
+        return [(block, d, k) for k, block in enumerate(order)]
+
+    def first_exchange(self, at, give):
+        return across(give, self.bits[1 - at])
+
+    def second_term(self, keep, came):
+        return (keep[:, :, 1].astype(f32) + came[:, :, 1].astype(f32)).astype(bf16)
+
+    def second_exchange(self, at, term):
+        return across(term, self.bits[at])
+
+    def slot_sum(self, keeps, cames, lasts, groups):
+        own = {}
+        for group, keep, came, last in zip(groups, keeps, cames, lasts):
+            total = keep[:, :, 0].astype(f32) + came[:, :, 0].astype(f32) + last.astype(f32)
+            for i, d in enumerate(group):
+                own[d] = total[:, i]
+        return own[0], [around(own[d].astype(bf16), -d) for d in range(1, self.slots)]
+
+    def to_owner(self, own, others):
+        total = own
+        for other in others:
+            total = total + other.astype(f32)
+        weights, rows, columns = total.shape
+        total = total.reshape((weights, 2, rows // 2, columns))
+        keep = lax.dynamic_index_in_dim(total, self.core, 1, keepdims=False)
+        give = lax.dynamic_index_in_dim(total, 1 - self.core, 1, keepdims=False)
+        out = self.ordered(0, keep, swap(give), 2)
+        return out.reshape((weights, rows // 2, 2 * columns))
+
     def sum_chips(self, value):
         for bit in self.bits:
             value = value + across(value, bit)
@@ -446,7 +594,7 @@
         return total
 
 
-def on_device(
+def on_device_general(
     x_in,
     segment_ids,
     norm_gain,
@@ -747,6 +895,398 @@
     )
 
 
+def tie(*values):
+    return lax.optimization_barrier(values)
+
+
+def on_device(*args):
+    if Place().fast(args[3].shape[1] // 2):
+        return on_device_fast(*args)
+    return on_device_general(*args)
+
+
+def on_device_fast(
+    x_in,
+    segment_ids,
+    norm_gain,
+    w_x,
+    w_z,
+    w_bc,
+    w_dt,
+    conv_x,
+    conv_x_bias,
+    conv_bc,
+    conv_bc_bias,
+    dt_bias,
+    a_log,
+    d_skip,
+    gate_gain,
+    w_out,
+    cotangent,
+):
+    place = Place()
+    core, slots, slot = place.core, place.slots, place.slot
+    length, features = x_in.shape
+    sequences, whole_length = segment_ids.shape
+    pieces = whole_length // length
+    own_rows = w_x.shape[0]
+    slot_channels = w_x.shape[1]
+    slot_heads = w_dt.shape[1]
+    half_channels = slot_channels // 2
+    half_heads = slot_heads // 2
+    channels = half_channels * slots
+    heads = half_heads * slots
+    all_channels = 2 * channels
+    all_heads = 2 * heads
+    bc_width = w_bc.shape[1]
+    n_chunks = length // CH
+    groups = [tuple(range(0, slots, 2)), tuple(range(1, slots, 2))]
+    at = place.offsets(own_rows, half_channels)
+
+    def split(weight):
+        return weight.reshape((own_rows, 2, half_channels))
+
+    stacked = jnp.stack([split(w_x), split(w_z), split(w_out.T)])
+    mine = lax.dynamic_index_in_dim(stacked, core, 2, keepdims=False)
+    other = swap(lax.dynamic_index_in_dim(stacked, 1 - core, 2, keepdims=False))
+    both = place.ordered(0, mine, other, 1).reshape((3, 2 * own_rows, half_channels))
+    (
+        both, x_in, segment_ids, norm_gain, w_bc, w_dt, conv_x, conv_x_bias, dt_bias, a_log, d_skip, gate_gain, cotangent,
+    ) = tie(both, x_in, segment_ids, norm_gain, w_bc, w_dt, conv_x, conv_x_bias, dt_bias, a_log, d_skip, gate_gain, cotangent)
+
+    wx_here = [both[:1]] + [around(both[:1], d) for d in range(1, slots)]
+    wx_items = []
+    for d in range(slots):
+        one, two = place.unit(d, wx_here[d])
+        wx_items += place.items(d, wx_here[d], one, two, place.forward(d, one))
+    pair, _ = tie(both[1:], wx_here[1:])
+    pair_here = [pair] + [around(pair, d) for d in range(1, slots)]
+
+    rows = jnp.concatenate(
+        [
+            conv_x,
+            conv_x_bias[None],
+            gate_gain[None],
+            jnp.pad(
+                jnp.concatenate([dt_bias, a_log, d_skip])[None], ((0, 0), (0, slot_channels - 3 * slot_heads))
+            ),
+            jnp.zeros((1, slot_channels), f32),
+            jnp.pad(w_dt.T.astype(f32), ((0, 0), (0, slot_channels - own_rows))),
+        ],
+        axis=0,
+    )
+    rows = place.gather_slots(rows)
+    dt_slots = rows[8:, :, :own_rows].transpose(2, 1, 0).reshape((own_rows, all_heads)).astype(bf16)
+    thin = jnp.concatenate([w_bc, dt_slots, norm_gain[:, None]], axis=1)
+    thin = jnp.pad(thin, ((0, 0), (0, bc_width + 128 - thin.shape[1])))
+    thin = place.ordered(0, thin, swap(thin), 0).reshape((2 * own_rows, -1))
+    thin = place.gather_rows(thin, True)
+    own = lax.dynamic_index_in_dim(
+        rows[:8].reshape((8, slots, 2, half_channels)), core, 2, keepdims=False
+    ).reshape((8, channels))
+    gain_row = own[5:6]
+    lane = jnp.arange(128)
+    head_at = lane % 32
+    global_head = (head_at // half_heads) * slot_heads + core * half_heads + head_at % half_heads
+    pick = ((lane[:, None] == global_head[None, :]) & (head_at < heads)[None, :]).astype(f32)
+    small = rows[6, :, : 3 * slot_heads].reshape((slots, 3, slot_heads)).transpose(1, 0, 2)
+    small = jnp.pad(small.reshape((3, all_heads)), ((0, 5), (0, 128 - all_heads)))
+    small = exact(small, pick)
+    bias_lanes = small[0]
+    rate_lanes = jnp.where(head_at < heads, -jnp.exp(small[1]), 0.0)
+    to_heads = head_map(channels, f32)
+    skip_row = exact(small[2:3] * (lane < 32), to_heads.T)
+    cw = jnp.concatenate([own[:5], skip_row, jnp.zeros((2, channels), f32)], axis=0)
+
+    padded = jnp.pad(segment_ids, ((0, 0), (HALO, HALO)), constant_values=-1)
+    ids_own = lax.dynamic_slice(
+        padded, (slot // pieces, (slot % pieces) * length), (1, length + 2 * HALO)
+    )
+    ids_all = jnp.concatenate([ids_own, swap(ids_own)], axis=0)
+    ids = ids_all[:, HALO : HALO + length]
+    before = ids_all[:, HALO - 1]
+
+    def near(k):
+        return ids_all[:, HALO + k : HALO + k + length] == ids
+
+    flags = [near(-1), near(-2), near(-3), ids, near(1), near(2), near(3), jnp.zeros_like(ids)]
+    flags = jnp.stack([v.astype(f32) for v in flags], axis=-1)
+
+    x_rows = jnp.concatenate([along_sequence(x_in[-HALO:], pieces, True), x_in], axis=0)
+    tokens_ext = x_rows.astype(f32)
+    inv_ext = lax.rsqrt(jnp.mean(tokens_ext * tokens_ext, axis=-1, keepdims=True) + epsilon)
+    gain = thin[:, bc_width + all_heads].astype(f32)[None, :]
+    normed_own = (tokens_ext * inv_ext * gain).astype(bf16)
+    normed_other = swap(normed_own)
+    normed_ext = jnp.concatenate([normed_own, normed_other], axis=0)
+    normed = jnp.concatenate([normed_own[HALO:], normed_other[HALO:]], axis=0)
+    tokens, inv_rms = tokens_ext[HALO:], inv_ext[HALO:]
+    cot = jnp.concatenate([cotangent, swap(cotangent)], axis=0)
+    normed_turned, cot_turned = normed.T, cot.T
+
+    dt_pick = jnp.dot(thin[:, bc_width:], pick.astype(bf16), preferred_element_type=f32).astype(bf16)
+    thin_proj = mm(normed_ext, jnp.concatenate([thin[:, :bc_width], dt_pick], axis=1))
+    thin_proj = thin_proj.reshape((2, HALO + length, -1))
+    bc_ext = thin_proj[:, :, :bc_width]
+    dt_in = thin_proj[:, HALO:, bc_width:] + bias_lanes
+
+    bc_pre = conv_bc_bias + conv_bc[0] * bc_ext[:, HALO:]
+    for k in range(1, conv_bc.shape[0]):
+        shifted = bc_ext[:, HALO - k : HALO - k + length]
+        bc_pre = bc_pre + conv_bc[k] * shifted * flags[:, :, k - 1 : k]
+    bc_act = jax.nn.silu(bc_pre)
+    bc_turned = bc_act.astype(bf16).transpose(0, 2, 1)
+    c_low = bc_act[:, :, bc_width // 2 :].astype(bf16)
+
+    step = jax.nn.softplus(dt_in)
+    log_step = (step * rate_lanes).reshape((2 * n_chunks, CH, 128))
+    tri = (jnp.arange(CH)[:, None] >= jnp.arange(CH)[None, :]).astype(f32)
+    running = jnp.einsum("ts,csh->cth", tri, log_step, precision=highest)
+    running = running.reshape((2, n_chunks, CH, 128))
+    last = running[:, :, -1:, :]
+    ids_chunks = ids.reshape((2, n_chunks, CH, 1))
+    chunk_end = ids_chunks[:, :, -1:, :]
+    chunk_before = jnp.concatenate([before[:, None, None, None], chunk_end[:, :-1]], axis=1)
+    still = (chunk_end == chunk_before).astype(f32)
+    alpha = still * jnp.exp(last)
+    lead = jnp.cumsum(last, axis=1) - last
+    since_piece = (ids_chunks == before[:, None, None, None]).astype(f32) * jnp.exp(running + lead)
+    since_piece = since_piece.reshape((2 * length, 128))
+    group_lane = lane // 32
+    hv = jnp.where(
+        group_lane == 0,
+        running * LOG2E,
+        jnp.where(
+            group_lane == 1,
+            step.reshape((2, n_chunks, CH, 128)),
+            jnp.where(
+                group_lane == 2,
+                (ids_chunks == chunk_before).astype(f32) * jnp.exp(running),
+                (ids_chunks == chunk_end).astype(f32) * jnp.exp(last - running),
+            ),
+        ),
+    ).reshape((2, length, 128))
+    rv = jnp.concatenate(
+        [
+            hv[:, :, :24].transpose(0, 2, 1),
+            ids.astype(f32)[:, None, :],
+            jnp.zeros((2, 7, length), f32),
+        ],
+        axis=1,
+    )
+    first_lanes = (lane < 32).astype(f32)
+    al = exact((alpha * first_lanes).reshape((2 * n_chunks, 128)), to_heads.T)
+    al = al.reshape((2, n_chunks, channels))
+    whole_alpha = jnp.prod(al, axis=1, keepdims=True)
+    al = jnp.pad(al, ((0, 0), (0, 8 - n_chunks), (0, 0)))
+    wide_since = mm((since_piece * first_lanes).astype(bf16), to_heads.T.astype(bf16))
+    wide_since = wide_since.reshape((2, length, channels))
+
+    def hand_on(local, forward):
+        low = local.astype(bf16)
+        for _ in range(pieces - 2):
+            came = along_sequence(low, pieces, forward)
+            low = (local + whole_alpha * came.astype(f32)).astype(bf16)
+        return along_sequence(low, pieces, forward)
+
+    (wx_blocks, pair_here[0], pair_here[1], normed_ext, hv, rv, al, bc_act, bc_turned, cw, wide_since, c_low, normed,
+     normed_turned, cot, cot_turned) = tie(
+        [item[0] for item in wx_items], pair_here[0], pair_here[1], normed_ext, hv, rv, al, bc_act, bc_turned, cw,
+        wide_since, c_low, normed, normed_turned, cot, cot_turned)
+    wx_items = [(block,) + item[1:] for block, item in zip(wx_blocks, wx_items)]
+    one, two, both_k = {}, {}, {}
+    one[0], two[0] = place.unit(0, pair_here[0])
+    one[1], two[1] = place.unit(1, pair_here[1])
+    x_ext, wx = project(normed_ext, at, wx_items, 0, channels)
+    x_ext = x_ext.reshape((2, HALO + length, channels))
+
+    x_ext, one[0], two[0], one[1], two[1], pair_here[2], pair_here[3] = tie(
+        x_ext, one[0], two[0], one[1], two[1], pair_here[2], pair_here[3])
+    both_k[0], both_k[1] = place.forward(0, one[0]), place.forward(1, one[1])
+    one[2], one[3] = across(pair_here[2], place.bits[0]), across(pair_here[3], place.bits[1])
+    y_here, states = scan_fwd(hv, flags, rv, al, bc_act, bc_turned, x_ext, cw, CH)
+
+    y_here, states, both_k[0], both_k[1], one[2], one[3] = tie(y_here, states, both_k[0], both_k[1], one[2], one[3])
+    two[2], two[3] = across(pair_here[2], place.bits[1]), across(pair_here[3], place.bits[0])
+    both_k[2], both_k[3] = place.forward(2, one[2]), place.forward(3, one[3])
+    pair_items = []
+    for d in range(slots):
+        pair_items += place.items(d, pair_here[d], one[d], two[d], both_k[d])
+    state_in = hand_on(states[:, -1], True)
+    y = y_here + wide_since * lax.dot_general(
+        c_low, state_in, (((2,), (1,)), ((0,), (0,))), preferred_element_type=f32
+    )
+
+    gate_in, wz = project(normed, at, pair_items, 0, channels)
+    mixed_grad, wo = project(cot, at, pair_items, 1, channels)
+    y = y.reshape((2 * length, channels))
+    sig = jax.nn.sigmoid(gate_in)
+    act = gate_in * sig
+    gated = y * act
+    scaled = mixed_grad * gain_row
+    sums = jnp.stack([jnp.sum(gated * gated, axis=1), jnp.sum(scaled * gated, axis=1)])
+    sums = sums.reshape((2, 2, length))
+    sums = (sums + swap(sums)[:, ::-1]).reshape((2, 2 * length))
+    gate_rms = lax.rsqrt(sums[0] / all_channels + epsilon)[:, None]
+    mixed = (gated * gate_rms * gain_row).astype(bf16)
+    gate_gain_part = jnp.sum(mixed_grad * gated * gate_rms, axis=0)
+    gated_grad = gate_rms * scaled - gated * gate_rms**3 * (sums[1] / all_channels)[:, None]
+    y_grad = (gated_grad * act).reshape((2, length, channels))
+    gate_grad = (gated_grad * y * sig * (1.0 + gate_in * (1.0 - sig))).astype(bf16)
+    state_grad = lax.dot_general(
+        c_low, (y_grad * wide_since).astype(bf16), (((1,), (1,)), ((0,), (0,))), preferred_element_type=f32
+    )
+    state_grad = hand_on(state_grad, False)
+    parts = [
+        weight_parts(at, [normed_turned, cot_turned], [[gate_grad], [mixed]], group, own_rows, half_channels, flip)
+        for flip, group in enumerate(groups)
+    ]
+    parts, y_grad, mixed, gate_grad = tie(parts, y_grad, mixed, gate_grad)
+    pair_came = [place.first_exchange(i, parts[i][1]) for i in range(2)]
+
+    branch_other = swap(mmt(mixed[length:], wo).astype(bf16))
+    branch = mmt(mixed[:length], wo)
+    block_out = (tokens + branch + branch_other.astype(f32)).astype(bf16)
+    normed_grad_other = mmt(gate_grad[length:], wz)
+    normed_grad = mmt(gate_grad[:length], wz)
+
+    def backward(piece):
+        return scan_bwd(
+            hv, flags, rv, al, bc_act, bc_turned, x_ext, cw, y_grad, states, state_in, state_grad, CH, piece, 1
+        )
+
+    back_other = backward(1)
+    pair_came, back_other, y_grad, block_out, normed_grad, normed_grad_other = tie(
+        pair_came, back_other, y_grad, block_out, normed_grad, normed_grad_other)
+    terms = [place.second_term(parts[i][0], pair_came[i]) for i in range(2)]
+    pair_last = [place.second_exchange(i, terms[i]) for i in range(2)]
+    back_own = backward(0)
+    dbc_other = swap(back_other[3][0])
+    pair_last, back_own, dbc_other, normed_grad, normed_grad_other = tie(
+        pair_last, back_own, dbc_other, normed_grad, normed_grad_other)
+    pair_own, pair_others = place.slot_sum([p[0] for p in parts], pair_came, pair_last, groups)
+
+    head = along_sequence(jnp.concatenate([back_own[2], back_other[2]]), pieces, False)
+
+    def past_end(begin, taps):
+        total = jnp.zeros((begin.shape[0], HALO, begin.shape[2]), f32)
+        for k in range(1, taps.shape[0]):
+            moved = jnp.pad(begin[:, :k], ((0, 0), (HALO - k, 0), (0, 0)))
+            total = total + taps[k] * moved * flags[: begin.shape[0], length - HALO :, 3 + k : 4 + k]
+        return total
+
+    fix = past_end(head, own[:4])
+    x_low = [
+        lax.dynamic_update_slice(back[0][0], (back[1][0] + fix[i]).astype(bf16), (length - HALO, 0))
+        for i, back in enumerate((back_own, back_other))
+    ]
+    x_parts = [
+        weight_parts(at, [normed_turned], [x_low], group, own_rows, half_channels, flip)
+        for flip, group in enumerate(groups)
+    ]
+    x_came = [place.first_exchange(i, x_parts[i][1]) for i in range(2)]
+
+    bc_grad = back_own[3][0] + dbc_other
+    pre = bc_pre[0]
+    sig_bc = jax.nn.sigmoid(pre)
+    bc_dpre = bc_grad * (sig_bc * (1.0 + pre * (1.0 - sig_bc)))
+    bc_head = along_sequence(bc_dpre[:8], pieces, False)
+    bc_raw = conv_bc[0] * bc_dpre
+    bc_taps = [jnp.sum(bc_dpre * bc_ext[0, HALO:], axis=0)]
+    longer = jnp.concatenate([bc_dpre, bc_head], axis=0)
+    for k in range(1, conv_bc.shape[0]):
+        bc_raw = bc_raw + conv_bc[k] * longer[k : k + length] * flags[0, :, 3 + k : 4 + k]
+        shifted = bc_ext[0, HALO - k : HALO - k + length]
+        bc_taps.append(jnp.sum(bc_dpre * shifted * flags[0, :, k - 1 : k], axis=0))
+    bc_low = bc_raw.astype(bf16)
+    bc_small = jnp.stack(bc_taps + [jnp.sum(bc_dpre, axis=0)] + [jnp.zeros((bc_width,), f32)] * 11)
+    bc_small = bc_small + swap(bc_small)
+
+    dcol = jnp.concatenate([back_own[4], back_other[4]])
+    drow = jnp.concatenate([back_own[5], back_other[5]])
+    dcum = dcol[:, :, :128] - jnp.pad(drow.transpose(0, 2, 1), ((0, 0), (0, 0), (0, 96)))
+    dlog = jnp.einsum("ts,csh->cth", tri.T, dcum.reshape((2 * n_chunks, CH, 128)), precision=highest)
+    dstep = dcol[:, :, 128:] + dlog.reshape((2, length, 128)) * rate_lanes
+    dt_raw = (dstep * jax.nn.sigmoid(dt_in)).reshape((2 * length, 128))
+    rate_part = jnp.sum(dlog * log_step, axis=(0, 1))
+    place_back = (pick * first_lanes).T.astype(bf16)
+    dt_low = mm(dt_raw.astype(bf16), place_back).astype(bf16)
+    thin_low = jnp.concatenate(
+        [jnp.concatenate([bc_low, jnp.zeros_like(bc_low)], axis=0), dt_low], axis=1
+    )
+    thin_part = mm(normed_turned, thin_low).astype(bf16)
+
+    dcw = back_own[6][0] + back_other[6][0]
+    head_rows = jnp.stack([jnp.sum(dt_raw, axis=0), rate_part]) * first_lanes
+    head_rows = exact(head_rows, to_heads.T)
+    packed = jnp.concatenate(
+        [dcw[:5], gate_gain_part[None], dcw[5:6], head_rows, jnp.zeros((7, channels), f32)], axis=0
+    )
+    packed = place.sum_chips(jnp.concatenate([packed, bc_small], axis=1))
+
+    normed_grad_other = normed_grad_other + mmt(x_low[1], wx) + mmt(thin_low[length:], thin)
+    normed_grad_other = swap(normed_grad_other.astype(bf16))
+    normed_grad = normed_grad + mmt(x_low[0], wx) + mmt(thin_low[:length], thin)
+    thin_grad = place.scatter_rows(thin_part, True, low_bit=0)
+
+    x_came, packed, thin_grad, normed_grad_other, normed_grad, pair_own, pair_others = tie(
+        x_came, packed, thin_grad, normed_grad_other, normed_grad, pair_own, pair_others)
+    x_terms = [place.second_term(x_parts[i][0], x_came[i]) for i in range(2)]
+    x_last = [place.second_exchange(i, x_terms[i]) for i in range(2)]
+
+    bc_small = packed[:, channels:]
+    packed = packed[:, :channels].reshape((16, slots, half_channels))
+
+    def block(index):
+        return lax.dynamic_index_in_dim(packed, index % slots, 1, keepdims=False)
+
+    own_sums = jnp.concatenate([block(slot), bc_small], axis=1)
+    for d in range(1, slots):
+        own_sums = own_sums + around(jnp.concatenate([block(slot + d), bc_small], axis=1), d)
+    packed = own_sums[:, :half_channels]
+    bc_small = own_sums[:, half_channels:]
+    packed = place.ordered(0, packed, swap(packed), 1).reshape((16, slot_channels))
+    by_head = packed[6:9].reshape((3, slot_heads, 64))
+
+    normed_grad = normed_grad + normed_grad_other.astype(f32)
+    gain_part = jnp.sum(normed_grad * tokens * inv_rms, axis=0)
+    pushed = normed_grad * gain
+    x_grad = (
+        cotangent.astype(f32)
+        + inv_rms * pushed
+        - tokens * inv_rms**3 * jnp.mean(pushed * tokens, axis=-1, keepdims=True)
+    )
+    gain_rows = gain_part.reshape((features // own_rows * 2, own_rows // 2))
+    gain_rows = place.scatter_rows(gain_rows, True, low_bit=0)
+    w_z_grad, w_out_grad = place.to_owner(pair_own, pair_others)
+
+    x_last, gain_rows, x_grad = tie(x_last, gain_rows, x_grad)
+    x_own, x_others = place.slot_sum([p[0] for p in x_parts], x_came, x_last, groups)
+    thin_grad = place.sum_slots(thin_grad)
+    w_bc_grad = thin_grad[:, :bc_width]
+    w_dt_grad = lax.dynamic_slice_in_dim(thin_grad, bc_width + slot * slot_heads, slot_heads, 1)
+    norm_gain_grad = place.sum_slots(gain_rows).reshape((own_rows,))
+    w_x_grad = place.to_owner(x_own, x_others)[0]
+    return (
+        block_out,
+        x_grad,
+        norm_gain_grad,
+        w_x_grad,
+        w_z_grad,
+        w_bc_grad,
+        w_dt_grad,
+        packed[:4],
+        packed[4],
+        bc_small[:4],
+        bc_small[4],
+        by_head[1, :, 0],
+        by_head[2, :, 0],
+        jnp.sum(by_head[0], axis=1),
+        packed[5],
+        w_out_grad.T,
+    )
+
+
 def solution(mesh):
     rows = P(("dp", "tensor"), None)
     both = P("dp", "tensor")

time: 886 us -> 762 us (0.86)
  waiting for transfers between devices: 229 us -> 136 us
  Pallas kernels: 87.9 us -> 165 us
  local copies, waits for them, and re-layouts: 192 us -> 143 us
  matrix products: 108 us -> 62.3 us
  starting transfers between devices: 152 us -> 119 us
  other arithmetic: 104 us -> 120 us
    ppermute x36 -> x42, waiting for transfers between devices: 148 us -> 55 us  [across(): return lax.ppermute(value, 'dp', [(i, i ^ 1 << bit) for i in range(size)])]
    pallas_call x0 -> x7, Pallas kernels: none -> 73.8 us  [the longest x4 39 us: weight_parts(): pl.pallas_call(lambda *refs: weight_parts_body(count, group, flip, *refs)...]
    ppermute x36 -> x24, starting transfers between devices: 101 us -> 49 us  [around(): lax.ppermute(value, 'tensor', [(i, (i + by) % size) for i in range(size)])]
    dot_general x9 -> x5, matrix products: 43.8 us -> 12.1 us  [the longest x1 5.55 us: on_device_fast(): lax.dot_general(c_low, (y_grad * wide_since).astype(bf16), (((1,), (1,)),...]
    optimization_barrier x0 -> x14, local copies, waits for them, and re-layouts: none -> 28.1 us  [tie(): return lax.optimization_barrier(values)]
    dot_general x6 -> x4, matrix products: 36.6 us -> 9.75 us  [mm(): lax.dot_general(a, b, (((1,), (0,)), ((), ())), preferred_element_type=f32)]
    dynamic_slice x20 -> x6, local copies, waits for them, and re-layouts: 26.4 us -> 3.05 us  [the longest x1 1.83 us: on_device_fast(): mine = lax.dynamic_index_in_dim(stacked, core, 2, keepdims=False)]
    convert_element_type x15 -> x3, other arithmetic: 19 us -> 2.11 us  [scatter_rows(): now = (keep.astype(f32) + across(give, bit).astype(f32)).astype(whole.dtype)]
  transfers between devices with their start and end apart: 91 -> 84, of which waited for: 25 -> 17; matrix products, arithmetic and copies ran while one was open for 32% -> 34% of each run, Pallas kernels for 7% -> 19%
where the time goes in v2:
time: 762 us; the launch traced here: 750 us
  Pallas kernels  165 us (22%)
  local copies, waits for them, and re-layouts  143 us (19%)
  waiting for transfers between devices  136 us (18%)
  other arithmetic  120 us (16%)
  starting transfers between devices  119 us (16%)
  matrix products  62.3 us (8%)
    ppermute x24, waiting for transfers between devices, around(): lax.ppermute(value, 'tensor', [(i, (i + by) % size) for i in range(size)])  69.4 us
    pallas_call x2, Pallas kernels, scan_bwd(): pl.pallas_call(lambda *refs: scan_bwd_body(n_chunks, rows, *refs), grid=(...  64 us
    ppermute x42, waiting for transfers between devices, across(): return lax.ppermute(value, 'dp', [(i, i ^ 1 << bit) for i in range(size)])  55 us
    ppermute x24, starting transfers between devices, around(): lax.ppermute(value, 'tensor', [(i, (i + by) % size) for i in range(size)])  49 us
    ppermute x42, starting transfers between devices, across(): return lax.ppermute(value, 'dp', [(i, i ^ 1 << bit) for i in range(size)])  43 us
    pallas_call x4, Pallas kernels, weight_parts(): pl.pallas_call(lambda *refs: weight_parts_body(count, group, flip, *refs)...  39 us
    dot_general x8, matrix products, mmt(): lax.dot_general(a, b, (((1,), (1,)), ((), ())), preferred_element_type=f32)  35.3 us
    pallas_call x3, Pallas kernels, project(): pl.pallas_call(lambda *refs: project_body(places, *refs), grid_spec=pltpu...  34.8 us
  transfers between devices with their start and end apart: 84, of which 17 were waited for; matrix products, arithmetic and copies ran while one was open for 34% of the time, Pallas kernels for 19%

profile of v2, /device:TPU:0, one launch (start us, length us, event | category | flops | bytes accessed | tf_op | source)
XLA Modules:
  0.0 749.5 jit_solution(9341941903489690467)
XLA Ops:
  36.4 9.2 %collective-permute-done.19 = f32[20,768]{1,0:T(8,128)S(1)} collective-permute-done((f32[20,768]{1,0:T(8,128)S(1)}, f32[20,768]{1,0:T(8,128)S(1)}, u32[]{:S(2)}, u32[]{:S(2)}) %collective-permute-start.19) | collective-permute-done | bytes 61472 | tf_op jit(solution)/shard_map/ppermute | solution.py:440
  45.6 8.7 %collective-permute-start.17 = (bf16[16,1536]{0,1:T(8,128)(2,1)S(1)}, bf16[16,1536]{0,1:T(8,128)(2,1)S(1)}, u32[]{:S(2)}, u32[]{:S(2)}) collective-permute-start(bf16[16,1536]{0,1:T(8,128)(2,1)S(1)} %copy.258), channel_id=1, source_target_pairs={{0,1},{2,3},{4,5},{6,7},{8,9},{10,11},{12,13},{14,15},{16,17},{18,... | collective-permute-start | bytes 147464 | tf_op jit(solution)/shard_map/ppermute | solution.py:448
  75.9 8.2 %collective-permute-done.23 = bf16[2,384,384]{2,1,0:T(8,128)(2,1)} collective-permute-done((bf16[2,384,384]{2,1,0:T(8,128)(2,1)}, bf16[2,384,384]{2,1,0:T(8,128)(2,1)}, u32[]{:S(2)}, u32[]{:S(2)}) %collective-permute-start.23) | collective-permute-done | bytes 589856 | tf_op jit(solution)/shard_map/ppermute | solution.py:434
  185.4 16.5 %collective-permute-done.31.refs_10_ = bf16[2,384,384]{2,1,0:T(8,128)(2,1)} collective-permute-done((bf16[2,384,384]{2,1,0:T(8,128)(2,1)}, bf16[2,384,384]{2,1,0:T(8,128)(2,1)}, u32[]{:S(2)}, u32[]{:S(2)}) %collective-permute-start.31) | collective-permute-done | bytes 589856 | tf_op jit(solution)/shard_map/ppermute | solution.py:440
  207.6 12.2 %project.3 = (f32[1056,1536]{1,0:T(8,128)}, bf16[1536,1536]{1,0:T(8,128)(2,1)}) custom-call(s32[8]{0:T(128)} %stack.107.refs_0_, bf16[1056,1536]{1,0:T(8,128)(2,1)} %copy.288.refs_1_, bf16[1,384,384]{2,1,0:T(8,128)(2,1)} %slice.416.refs_2_, bf16[1,384,384]{2,1,0:T(8,128)(2,1)} %collective-permute-done.1.refs_3_, ...), custom_call_target="tpu_custom_call" | custom-call | flops 4982833152 | bytes 19169280 | tf_op jit(solution)/shard_map/project/pallas_call | solution.py:347
  229.8 27.2 %scan_fwd.1 = (f32[2,512,1536]{2,1,0:T(8,128)}, f32[2,2,128,1536]{3,2,1,0:T(8,128)}) custom-call(f32[2,512,128]{2,1,0:T(8,128)} %copy.289.refs_0_, f32[2,512,8]{2,1,0:T(8,128)} %copy.290.refs_1_, f32[2,32,512]{2,1,0:T(8,128)} %maximum_maximum_fusion.refs_2_, f32[2,8,1536]{2,1,0:T(8,128)} %pad.50.refs_3_, f32[2,512,256]{2,1,0:T(8,128)} %copy.291.refs_4_, ...), custom_call_target="tpu_custom_call" | custom-call | flops 3221225472 | bytes 12582912 | tf_op jit(solution)/shard_map/scan_fwd/pallas_call | solution.py:116
  274.5 12.6 %collective-permute-start.37 = (bf16[2,128,1536]{2,1,0:T(8,128)(2,1)S(1)}, bf16[2,128,1536]{2,1,0:T(8,128)(2,1)S(1)}, u32[]{:S(2)}, u32[]{:S(2)}) collective-permute-start(bf16[2,128,1536]{2,1,0:T(8,128)(2,1)S(1)} %fusion.26), channel_id=1, source_target_pairs={{0,1},{2,3},{4,5},{6,7},{8,9},{10,11},{12,13},{14,15},{16,17},{18,... | collective-permute-start | bytes 2359304 | tf_op jit(solution)/shard_map/ppermute | solution.py:448
  287.2 11.3 %project.5 = (f32[1024,1536]{1,0:T(8,128)}, bf16[1536,1536]{1,0:T(8,128)(2,1)}) custom-call(s32[8]{0:T(128)} %stack.107.refs_0_, bf16[1024,1536]{1,0:T(8,128)(2,1)} %copy.295.refs_1_, bf16[2,384,384]{2,1,0:T(8,128)(2,1)} %slice.417.refs_2_, bf16[2,384,384]{2,1,0:T(8,128)(2,1)} %collective-permute-done.27.refs_3_, ...), custom_call_target="tpu_custom_call" | custom-call | flops 4831838208 | bytes 18874368 | tf_op jit(solution)/shard_map/project/pallas_call | solution.py:347
  298.5 11.3 %project.4 = (f32[1024,1536]{1,0:T(8,128)}, bf16[1536,1536]{1,0:T(8,128)(2,1)}) custom-call(s32[8]{0:T(128)} %stack.107.refs_0_, bf16[1024,1536]{1,0:T(8,128)(2,1)} %copy.294.refs_1_, bf16[2,384,384]{2,1,0:T(8,128)(2,1)} %slice.417.refs_2_, bf16[2,384,384]{2,1,0:T(8,128)(2,1)} %collective-permute-done.27.refs_3_, ...), custom_call_target="tpu_custom_call" | custom-call | flops 4831838208 | bytes 18874368 | tf_op jit(solution)/shard_map/project/pallas_call | solution.py:347
  314.3 8.6 %multiply_add_fusion = f32[2,512,1536]{2,1,0:T(8,128)S(1)} fusion(f32[2,512,1536]{2,1,0:T(8,128)} %get-tuple-element.199, f32[2,512,1536]{2,1,0:T(8,128)} %fusion.69, f32[2,512,1536]{2,1,0:T(8,128)} %fusion.182), kind=kLoop, calls=%fused_computation.13 | loop fusion | flops 3145728 | bytes 25165824 | tf_op jit(solution)/shard_map/add | solution.py:1116
  323.0 9.9 %multiply_reduce_fusion.1 = (f32[1024]{0:T(1024)S(1)}, f32[1024]{0:T(1024)S(1)}, f32[1024,1536]{1,0:T(8,128)}) fusion(f32[1024,1536]{1,0:T(8,128)} %get-tuple-element.212, f32[1536]{0:T(1024)S(1)} %mul.603, f32[1024,1536]{1,0:T(8,128)} %get-tuple-element.210, f32[2,512,1536]{2,1,0:T(8,128)S(1)} %multiply_add_fusion), kind=kLoop, calls=%fused_computation.9 | loop fusion | flops 15726592 | bytes 25180160 | tf_op jit(solution)/shard_map/reduce_sum | solution.py:1127
  337.5 15.6 %fusion.6 = (f32[1024,1536]{1,0:T(8,128)}, bf16[1024,1536]{1,0:T(8,128)(2,1)}, f32[1536]{0:T(1024)S(1)}, bf16[1024,1536]{1,0:T(8,128)(2,1)}) fusion(f32[1024]{0:T(1024)S(1)} %bitcast.421, f32[1024,1536]{1,0:T(8,128)} %get-tuple-element.369, f32[1024,1536]{1,0:T(8,128)} %get-tuple-element.212, f32[1024]{0:T(1024)S(1)} %multiply_multiply_fusion, ...), kind=kLoop, calls=%fused_computation.28 | loop fusion | flops 36174336 | bytes 37773312 | tf_op jit(solution)/shard_map/mul | solution.py:1134
  353.1 12.3 %weight_parts.4 = (bf16[2,2,2,384,384]{4,3,2,1,0:T(8,128)(2,1)}, bf16[2,2,2,384,384]{4,3,2,1,0:T(8,128)(2,1)}) custom-call(s32[8]{0:T(128)} %stack.107.refs_0_, bf16[1536,1024]{1,0:T(8,128)(2,1)} %get-tuple-element.164.refs_1_, bf16[1536,1024]{1,0:T(8,128)(2,1)} %get-tuple-element.165.refs_2_, bf16[1024,1536]{1,0:T(8,128)(2,1)} %get-tuple-element.229.refs_3_, ...), custom_call_target="tpu_custom_call" | custom-call | flops 4831838208 | bytes 9437184 | tf_op jit(solution)/shard_map/weight_parts/pallas_call | solution.py:409
  365.4 12.3 %weight_parts.5 = (bf16[2,2,2,384,384]{4,3,2,1,0:T(8,128)(2,1)}, bf16[2,2,2,384,384]{4,3,2,1,0:T(8,128)(2,1)}) custom-call(s32[8]{0:T(128)} %stack.107.refs_0_, bf16[1536,1024]{1,0:T(8,128)(2,1)} %get-tuple-element.164.refs_1_, bf16[1536,1024]{1,0:T(8,128)(2,1)} %get-tuple-element.165.refs_2_, bf16[1024,1536]{1,0:T(8,128)(2,1)} %get-tuple-element.229.refs_3_, ...), custom_call_target="tpu_custom_call" | custom-call | flops 4831838208 | bytes 9437184 | tf_op jit(solution)/shard_map/weight_parts/pallas_call | solution.py:409
  410.7 32.0 %scan_bwd.2 = (bf16[1,512,1536]{2,1,0:T(8,128)(2,1)}, f32[1,16,1536]{2,1,0:T(8,128)}, f32[1,8,1536]{2,1,0:T(8,128)}, f32[1,512,256]{2,1,0:T(8,128)}, f32[1,512,2...) custom-call(f32[2,512,128]{2,1,0:T(8,128)} %copy.289.refs_0_, f32[2,512,8]{2,1,0:T(8,128)} %copy.290.refs_1_, ...), custom_call_target="tpu_custom_call" | custom-call | flops 4831838208 | bytes 9437184 | tf_op jit(solution)/shard_map/scan_bwd/pallas_call | solution.py:278
  442.8 8.5 %fusion.7 = bf16[512,1536]{0,1:T(8,128)(2,1)} fusion(bf16[512,1536]{0,1:T(8,128)(2,1)} %collective-permute-done.46, bf16[1536,1536]{1,0:T(8,128)(2,1)} %get-tuple-element.228, f32[528,1536]{0,1:T(8,128)} %maximum_convert_fusion, bf16[1024,1536]{1,0:T(8,128)(2,1)} %get-tuple-element.227.refs_4_), kind=kOutput, calls=%fused_computation.29 | convolution fusion | flops 2419064832 | bytes 12582912 | tf_op jit(solution)/shard_map/dot_general | solution.py:23
  472.5 32.0 %scan_bwd.3 = (bf16[1,512,1536]{2,1,0:T(8,128)(2,1)}, f32[1,16,1536]{2,1,0:T(8,128)}, f32[1,8,1536]{2,1,0:T(8,128)}, f32[1,512,256]{2,1,0:T(8,128)}, f32[1,512,2...) custom-call(f32[2,512,128]{2,1,0:T(8,128)} %copy.289.refs_0_, f32[2,512,8]{2,1,0:T(8,128)} %copy.290.refs_1_, ...), custom_call_target="tpu_custom_call" | custom-call | flops 4831838208 | bytes 9437184 | tf_op jit(solution)/shard_map/scan_bwd/pallas_call | solution.py:278
  535.7 6.8 collective-permute-start.61
  560.9 7.2 weight_parts.6
  568.1 7.2 weight_parts.7
  588.5 24.0 %collective-permute-done.58 = bf16[2,192,384]{2,1,0:T(8,128)(2,1)S(1)} collective-permute-done((bf16[2,192,384]{2,1,0:T(8,128)(2,1)S(1)}, bf16[2,192,384]{2,1,0:T(8,128)(2,1)S(1)}, u32[]{:S(2)}, u32[]{:S(2)}) %collective-permute-start.58) | collective-permute-done | bytes 294944 | tf_op jit(solution)/shard_map/ppermute | solution.py:434
  625.2 33.6 %collective-permute-done.62 = bf16[2,384,384]{2,1,0:T(8,128)(2,1)S(1)} collective-permute-done((bf16[2,384,384]{2,1,0:T(8,128)(2,1)S(1)}, bf16[2,384,384]{2,1,0:T(8,128)(2,1)S(1)}, u32[]{:S(2)}, u32[]{:S(2)}) %collective-permute-start.62) | collective-permute-done | bytes 589856 | tf_op jit(solution)/shard_map/ppermute | solution.py:440
  687.8 8.6 %collective-permute-done.68 = f32[2,96]{1,0:T(2,128)S(1)} collective-permute-done((f32[2,96]{1,0:T(2,128)S(1)}, f32[2,96]{1,0:T(2,128)S(1)}, u32[]{:S(2)}, u32[]{:S(2)}) %collective-permute-start.68) | collective-permute-done | bytes 800 | tf_op jit(solution)/shard_map/ppermute | solution.py:434
  724.0 9.9 %collective-permute-start.69 = (f32[2,96]{1,0:T(2,128)S(1)}, f32[2,96]{1,0:T(2,128)S(1)}, u32[]{:S(2)}, u32[]{:S(2)}) collective-permute-start(f32[2,96]{1,0:T(2,128)S(1)} %copy-done.118), channel_id=1, source_target_pairs={{0,1},{1,2},{2,3},{3,0},{4,5},{5,6},{6,7},{7,4},{8,9},{9,10},{10,1... | collective-permute-start | bytes 2312 | tf_op jit(solution)/shard_map/ppermute | solution.py:440
  (756 shorter events, 400.3 us)
Async XLA Ops:
  15.7 80.4 %collective-permute-start.4 = (bf16[1,384,384]{2,1,0:T(8,128)(2,1)}, bf16[1,384,384]{2,1,0:T(8,128)(2,1)}, u32[]{:S(2)}, u32[]{:S(2)}) collective-permute-start(bf16[1,384,384]{2,1,0:T(8,128)(2,1)} %slice.416.refs_2_), channel_id=1, source_target_pairs={{0,1},{1,2},{2,3},{3,0},{4,5},{5,6},{6,7},{7,4},{8,9},{9,10},{10,1... | collective-permute-start | bytes 884744 | tf_op jit(solution)/shard_map/ppermute | solution.py:440
  18.3 79.3 %collective-permute-start.8 = (bf16[1,384,384]{2,1,0:T(8,128)(2,1)}, bf16[1,384,384]{2,1,0:T(8,128)(2,1)}, u32[]{:S(2)}, u32[]{:S(2)}) collective-permute-start(bf16[1,384,384]{2,1,0:T(8,128)(2,1)} %slice.416.refs_2_), channel_id=1, source_target_pairs={{0,2},{1,3},{2,0},{3,1},{4,6},{5,7},{6,4},{7,5},{8,10},{9,11},{10,... | collective-permute-start | bytes 884744 | tf_op jit(solution)/shard_map/ppermute | solution.py:440
  36.4 62.7 %collective-permute-start.12 = (bf16[1,384,384]{2,1,0:T(8,128)(2,1)}, bf16[1,384,384]{2,1,0:T(8,128)(2,1)}, u32[]{:S(2)}, u32[]{:S(2)}) collective-permute-start(bf16[1,384,384]{2,1,0:T(8,128)(2,1)} %slice.416.refs_2_), channel_id=1, source_target_pairs={{0,3},{1,0},{2,1},{3,2},{4,7},{5,4},{6,5},{7,6},{8,11},{9,8},{10,9... | collective-permute-start | bytes 884744 | tf_op jit(solution)/shard_map/ppermute | solution.py:440
  57.2 48.5 %collective-permute-start.26 = (bf16[512,1536]{0,1:T(8,128)(2,1)}, bf16[512,1536]{0,1:T(8,128)(2,1)}, u32[]{:S(2)}, u32[]{:S(2)}) collective-permute-start(bf16[512,1536]{0,1:T(8,128)(2,1)} %copy.287), channel_id=1, source_target_pairs={{0,4},{4,0},{8,12},{12,8},{16,20},{20,16},{24,28},{28,24},{1,5},{5... | collective-permute-start | bytes 4718600 | tf_op jit(solution)/shard_map/ppermute | solution.py:429
  97.6 56.9 %collective-permute-start.2 = (bf16[1,384,384]{2,1,0:T(8,128)(2,1)}, bf16[1,384,384]{2,1,0:T(8,128)(2,1)}, u32[]{:S(2)}, u32[]{:S(2)}) collective-permute-start(bf16[1,384,384]{2,1,0:T(8,128)(2,1)} %slice.416.refs_2_), channel_id=1, source_target_pairs={{0,16},{4,20},{8,24},{12,28},{16,0},{20,4},{24,8},{28,12},{1,17},{... | collective-permute-start | bytes 884744 | tf_op jit(solution)/shard_map/ppermute | solution.py:434
  99.1 56.4 %collective-permute-start.5 = (bf16[1,384,384]{2,1,0:T(8,128)(2,1)}, bf16[1,384,384]{2,1,0:T(8,128)(2,1)}, u32[]{:S(2)}, u32[]{:S(2)}) collective-permute-start(bf16[1,384,384]{2,1,0:T(8,128)(2,1)} %collective-permute-done.4.refs_6_), channel_id=1, source_target_pairs={{0,8},{4,12},{8,0},{12,4},{16,24},{20,28},{24,16},{28,20},{1,9},{5... | collective-permute-start | bytes 884744 | tf_op jit(solution)/shard_map/ppermute | solution.py:434
  105.7 53.3 %collective-permute-start.6 = (bf16[1,384,384]{2,1,0:T(8,128)(2,1)}, bf16[1,384,384]{2,1,0:T(8,128)(2,1)}, u32[]{:S(2)}, u32[]{:S(2)}) collective-permute-start(bf16[1,384,384]{2,1,0:T(8,128)(2,1)} %collective-permute-done.4.refs_6_), channel_id=1, source_target_pairs={{0,16},{4,20},{8,24},{12,28},{16,0},{20,4},{24,8},{28,12},{1,17},{... | collective-permute-start | bytes 884744 | tf_op jit(solution)/shard_map/ppermute | solution.py:434
  111.7 50.2 %collective-permute-start.9 = (bf16[1,384,384]{2,1,0:T(8,128)(2,1)}, bf16[1,384,384]{2,1,0:T(8,128)(2,1)}, u32[]{:S(2)}, u32[]{:S(2)}) collective-permute-start(bf16[1,384,384]{2,1,0:T(8,128)(2,1)} %collective-permute-done.8.refs_10_), channel_id=1, source_target_pairs={{0,8},{4,12},{8,0},{12,4},{16,24},{20,28},{24,16},{28,20},{1,9},{5... | collective-permute-start | bytes 884744 | tf_op jit(solution)/shard_map/ppermute | solution.py:434
  113.2 41.8 %collective-permute-start.3 = (bf16[1,384,384]{2,1,0:T(8,128)(2,1)}, bf16[1,384,384]{2,1,0:T(8,128)(2,1)}, u32[]{:S(2)}, u32[]{:S(2)}) collective-permute-start(bf16[1,384,384]{2,1,0:T(8,128)(2,1)} %collective-permute-done.1.refs_3_), channel_id=1, source_target_pairs={{0,16},{4,20},{8,24},{12,28},{16,0},{20,4},{24,8},{28,12},{1,17},{... | collective-permute-start | bytes 884744 | tf_op jit(solution)/shard_map/ppermute | solution.py:434
  179.3 40.4 %collective-permute-start.32 = (bf16[2,384,384]{2,1,0:T(8,128)(2,1)}, bf16[2,384,384]{2,1,0:T(8,128)(2,1)}, u32[]{:S(2)}, u32[]{:S(2)}) collective-permute-start(bf16[2,384,384]{2,1,0:T(8,128)(2,1)} %slice.417.refs_2_), channel_id=1, source_target_pairs={{0,3},{1,0},{2,1},{3,2},{4,7},{5,4},{6,5},{7,6},{8,11},{9,8},{10,9... | collective-permute-start | bytes 1769480 | tf_op jit(solution)/shard_map/ppermute | solution.py:440
  229.2 57.9 %collective-permute-start.38 = (bf16[2,384,384]{2,1,0:T(8,128)(2,1)}, bf16[2,384,384]{2,1,0:T(8,128)(2,1)}, u32[]{:S(2)}, u32[]{:S(2)}) collective-permute-start(bf16[2,384,384]{2,1,0:T(8,128)(2,1)} %collective-permute-done.31.refs_10_), channel_id=1, source_target_pairs={{0,16},{4,20},{8,24},{12,28},{16,0},{20,4},{24,8},{28,12},{1,17},{... | collective-permute-start | bytes 1769480 | tf_op jit(solution)/shard_map/ppermute | solution.py:434
  385.0 66.3 %collective-permute-start.43 = (bf16[2,2,2,384,384]{4,3,0,1,2:T(8,128)(2,1)}, bf16[2,2,2,384,384]{4,3,0,1,2:T(8,128)(2,1)}, u32[]{:S(2)}, u32[]{:S(2)}) collective-permute-start(bf16[2,2,2,384,384]{4,3,0,1,2:T(8,128)(2,1)} %copy.296), channel_id=1, source_target_pairs={{0,16},{4,20},{8,24},{12,28},{16,0},{20,4},{24,8},{28,12},{1,17},{... | collective-permute-start | bytes 7077896 | tf_op jit(solution)/shard_map/ppermute | solution.py:434
  385.8 65.5 %collective-permute-start.44 = (bf16[2,2,2,384,384]{4,3,2,1,0:T(8,128)(2,1)}, bf16[2,2,2,384,384]{4,3,2,1,0:T(8,128)(2,1)}, u32[]{:S(2)}, u32[]{:S(2)}) collective-permute-start(bf16[2,2,2,384,384]{4,3,2,1,0:T(8,128)(2,1)} %get-tuple-element.218), channel_id=1, source_target_pairs={{0,8},{4,12},{8,0},{12,4},{16,24},{20,28},{24,16},{28,20},{1,9},{5... | collective-permute-start | bytes 7077896 | tf_op jit(solution)/shard_map/ppermute | solution.py:434
  394.4 48.4 %collective-permute-start.46 = (bf16[512,1536]{0,1:T(8,128)(2,1)}, bf16[512,1536]{0,1:T(8,128)(2,1)}, u32[]{:S(2)}, u32[]{:S(2)}) collective-permute-start(bf16[512,1536]{0,1:T(8,128)(2,1)} %convolution_convert_fusion), channel_id=1, source_target_pairs={{0,4},{4,0},{8,12},{12,8},{16,20},{20,16},{24,28},{28,24},{1,5},{5... | collective-permute-start | bytes 4718600 | tf_op jit(solution)/shard_map/ppermute | solution.py:429
  454.1 50.4 %collective-permute-start.47 = (bf16[2,2,384,384]{3,2,0,1:T(8,128)(2,1)}, bf16[2,2,384,384]{3,2,0,1:T(8,128)(2,1)}, u32[]{:S(2)}, u32[]{:S(2)}) collective-permute-start(bf16[2,2,384,384]{3,2,0,1:T(8,128)(2,1)} %fusion.17), channel_id=1, source_target_pairs={{0,8},{4,12},{8,0},{12,4},{16,24},{20,28},{24,16},{28,20},{1,9},{5... | collective-permute-start | bytes 3538952 | tf_op jit(solution)/shard_map/ppermute | solution.py:434
  458.1 46.4 %collective-permute-start.48 = (bf16[2,2,384,384]{3,2,1,0:T(8,128)(2,1)}, bf16[2,2,384,384]{3,2,1,0:T(8,128)(2,1)}, u32[]{:S(2)}, u32[]{:S(2)}) collective-permute-start(bf16[2,2,384,384]{3,2,1,0:T(8,128)(2,1)} %fusion.18), channel_id=1, source_target_pairs={{0,16},{4,20},{8,24},{12,28},{16,0},{20,4},{24,8},{28,12},{1,17},{... | collective-permute-start | bytes 3538952 | tf_op jit(solution)/shard_map/ppermute | solution.py:434
  463.6 40.9 %collective-permute-start.49 = (f32[512,256]{0,1:T(8,128)}, f32[512,256]{0,1:T(8,128)}, u32[]{:S(2)}, u32[]{:S(2)}) collective-permute-start(f32[512,256]{0,1:T(8,128)} %bitcast.64), channel_id=1, source_target_pairs={{0,4},{4,0},{8,12},{12,8},{16,20},{20,16},{24,28},{28,24},{1,5},{5... | collective-permute-start | bytes 1572872 | tf_op jit(solution)/shard_map/ppermute | solution.py:429
  510.7 46.7 %collective-permute-start.50 = (f32[2,8,1536]{2,1,0:T(8,128)}, f32[2,8,1536]{2,1,0:T(8,128)}, u32[]{:S(2)}, u32[]{:S(2)}) collective-permute-start(f32[2,8,1536]{2,1,0:T(8,128)} %pad_maximum_fusion.6), channel_id=1, source_target_pairs={{1,0},{3,2},{5,4},{7,6},{9,8},{11,10},{13,12},{15,14},{17,16},{19,... | collective-permute-start | bytes 294920 | tf_op jit(solution)/shard_map/ppermute | solution.py:448
  535.7 86.9 %collective-permute-start.61 = (bf16[2,384,384]{2,1,0:T(8,128)(2,1)}, bf16[2,384,384]{2,1,0:T(8,128)(2,1)}, u32[]{:S(2)}, u32[]{:S(2)}) collective-permute-start(bf16[2,384,384]{2,1,0:T(8,128)(2,1)} %get-tuple-element.407), channel_id=1, source_target_pairs={{0,3},{1,0},{2,1},{3,2},{4,7},{5,4},{6,5},{7,6},{8,11},{9,8},{10,9... | collective-permute-start | bytes 1769480 | tf_op jit(solution)/shard_map/ppermute | solution.py:440
  576.8 82.0 %collective-permute-start.51 = (bf16[1,2,2,384,384]{4,3,1,2,0:T(8,128)(2,1)S(1)}, bf16[1,2,2,384,384]{4,3,1,2,0:T(8,128)(2,1)S(1)}, u32[]{:S(2)}, u32[]{:S(2)}) collective-permute-start(bf16[1,2,2,384,384]{4,3,1,2,0:T(8,128)(2,1)S(1)} %copy.310), channel_id=1, source_target_pairs={{0,16},{4,20},{8,24},{12,28},{16,0},{20,4},{24,8},{28,12},{1,17},{... | collective-permute-start | bytes 3538952 | tf_op jit(solution)/shard_map/ppermute | solution.py:434
  578.2 80.6 %collective-permute-start.52 = (bf16[1,2,2,384,384]{4,3,2,1,0:T(8,128)(2,1)}, bf16[1,2,2,384,384]{4,3,2,1,0:T(8,128)(2,1)S(1)}, u32[]{:S(2)}, u32[]{:S(2)}) collective-permute-start(bf16[1,2,2,384,384]{4,3,2,1,0:T(8,128)(2,1)} %get-tuple-element.255), channel_id=1, source_target_pairs={{0,8},{4,12},{8,0},{12,4},{16,24},{20,28},{24,16},{28,20},{1,9},{5... | collective-permute-start | bytes 3538952 | tf_op jit(solution)/shard_map/ppermute | solution.py:434
  585.4 73.4 %collective-permute-start.60 = (bf16[512,1536]{0,1:T(8,128)(2,1)S(1)}, bf16[512,1536]{0,1:T(8,128)(2,1)S(1)}, u32[]{:S(2)}, u32[]{:S(2)}) collective-permute-start(bf16[512,1536]{0,1:T(8,128)(2,1)S(1)} %add_convert_fusion), channel_id=1, source_target_pairs={{0,4},{4,0},{8,12},{12,8},{16,20},{20,16},{24,28},{28,24},{1,5},{5... | collective-permute-start | bytes 4718600 | tf_op jit(solution)/shard_map/ppermute | solution.py:429
  659.6 48.9 %collective-permute-start.79 = (bf16[192,384]{1,0:T(8,128)(2,1)}, bf16[192,384]{1,0:T(8,128)(2,1)}, u32[]{:S(2)}, u32[]{:S(2)}) collective-permute-start(bf16[192,384]{1,0:T(8,128)(2,1)} %fusion.88), channel_id=1, source_target_pairs={{0,3},{1,0},{2,1},{3,2},{4,7},{5,4},{6,5},{7,6},{8,11},{9,8},{10,9... | collective-permute-start | bytes 442376 | tf_op jit(solution)/shard_map/ppermute | solution.py:440
  659.8 48.9 %collective-permute-start.78 = (bf16[192,384]{1,0:T(8,128)(2,1)}, bf16[192,384]{1,0:T(8,128)(2,1)}, u32[]{:S(2)}, u32[]{:S(2)}) collective-permute-start(bf16[192,384]{1,0:T(8,128)(2,1)} %fusion.88), channel_id=1, source_target_pairs={{0,2},{1,3},{2,0},{3,1},{4,6},{5,7},{6,4},{7,5},{8,10},{9,11},{10,... | collective-permute-start | bytes 442376 | tf_op jit(solution)/shard_map/ppermute | solution.py:440
  (209 other events, 2842.6 us)

commit v3 on v2

--- a/solution.py
+++ b/solution.py
@@ -325,8 +325,8 @@
     )(hv, fl, rv, al, bc, bt, x_ext, cw, dy, states, s_recv, r_recv, seg)
 
 
-def project_body(places, at_ref, act_ref, *refs):
-    blocks, out_ref, full_ref = refs[:-2], refs[-2], refs[-1]
+def project_body(places, skip, at_ref, *refs):
+    left_ref, right_ref, blocks, out_ref, full_ref = refs[0], refs[1], refs[2:-2], refs[-2], refs[-1]
 
     @pl.when(pl.program_id(0) == 0)
     def _():
@@ -335,64 +335,491 @@
             row = pl.multiple_of(at_ref[k], rows)
             column = pl.multiple_of(at_ref[4 + d], columns)
             full_ref[pl.ds(row, rows), pl.ds(column, columns)] = ref[0]
-
-    out_ref[...] = mm(act_ref[...], full_ref[...])
-
-
-def project(act, at, items, weight, channels):
-    rows, features = act.shape
-    tile = rows // 3 if rows % 48 == 0 else rows // 4
+        out_ref[...] = mm(left_ref[skip:, :], full_ref[...])
+
+    @pl.when(pl.program_id(0) == 1)
+    def _():
+        out_ref[...] = mm(right_ref[skip:, :], full_ref[...])
+
+
+def project(acts, skip, at, items, weight, channels):
+    rows, features = acts[0].shape
+    rows = rows - skip
     blocks = [item[0] for item in items]
     places = [item[1:] for item in items]
     return pl.pallas_call(
-        lambda *refs: project_body(places, *refs),
+        lambda *refs: project_body(places, skip, *refs),
         grid_spec=pltpu.PrefetchScalarGridSpec(
             num_scalar_prefetch=1,
-            grid=(rows // tile,),
-            in_specs=[pl.BlockSpec((tile, features), lambda i, at: (i, 0))]
+            grid=(2,),
+            in_specs=[pl.BlockSpec(v.shape, lambda i, at: (0, 0), pipeline_mode=pl.Buffered(1)) for v in acts]
             + [
                 pl.BlockSpec((1,) + b.shape[1:], lambda i, at: (weight, 0, 0), pipeline_mode=pl.Buffered(1))
                 for b in blocks
             ],
             out_specs=[
-                pl.BlockSpec((tile, channels), lambda i, at: (i, 0)),
+                pl.BlockSpec((rows, channels), lambda i, at: (i, 0)),
                 pl.BlockSpec((features, channels), lambda i, at: (0, 0), pipeline_mode=pl.Buffered(1)),
             ],
         ),
         out_shape=[
-            jax.ShapeDtypeStruct((rows, channels), f32),
+            jax.ShapeDtypeStruct((2 * rows, channels), f32),
             jax.ShapeDtypeStruct((features, channels), bf16),
         ],
         cost_estimate=pl.CostEstimate(
-            flops=2 * rows * features * channels,
+            flops=4 * rows * features * channels,
             transcendentals=0,
-            bytes_accessed=rows * features * 2 + rows * channels * 4 + features * channels * 4,
+            bytes_accessed=rows * features * 4 + rows * channels * 8 + features * channels * 4,
         ),
         name="project",
-    )(at, act, *blocks)
+    )(at, *acts, *blocks)
+
+
+def turn_body(x_ref, out_ref):
+    out_ref[...] = x_ref[...].T
+
+
+def turn(x):
+    rows, columns = x.shape
+    return pl.pallas_call(
+        turn_body, out_shape=jax.ShapeDtypeStruct((columns, rows), x.dtype), name="turn", cost_estimate=pl.CostEstimate(flops=1, transcendentals=0, bytes_accessed=1)
+    )(x)
+
+
+def norm_body(x_ref, halo_ref, gain_ref, out_ref, turned_ref):
+    def normed(ref, at):
+        x = ref[at, :].astype(f32)
+        inv = lax.rsqrt(jnp.mean(x * x, axis=-1, keepdims=True) + epsilon)
+        return (x * inv * gain_ref[...]).astype(bf16)
+
+    out_ref[:HALO, :] = normed(halo_ref, slice(0, HALO))
+    for r in range(x_ref.shape[0] // 128):
+        rows = normed(x_ref, slice(128 * r, 128 * r + 128))
+        out_ref[HALO + 128 * r : HALO + 128 * r + 128, :] = rows
+        turned_ref[:, 128 * r : 128 * r + 128] = rows.T
+
+
+def norm(x, halo, gain):
+    rows, features = x.shape
+    return pl.pallas_call(
+        norm_body,
+        out_shape=[
+            jax.ShapeDtypeStruct((HALO + rows, features), bf16),
+            jax.ShapeDtypeStruct((features, rows), bf16),
+        ],
+        cost_estimate=pl.CostEstimate(flops=1, transcendentals=0, bytes_accessed=1),
+        name="norm",
+    )(x, halo, gain)
+
+
+def prepare_body(
+    own_ref, other_ref, thin_ref, pick_ref, lanes_ref, cbc_ref, ids_ref, row_ref,
+    bcx_ref, pre_ref, act_ref, turned_ref, low_ref, dt_ref, log_ref, hv_ref, rv_ref, al_ref, since_ref, flags_ref,
+    scr_ref,
+):
+    length = act_ref.shape[1]
+    n_chunks = length // CH
+    width = pre_ref.shape[2]
+    channels = al_ref.shape[2]
+    picked = mm(thin_ref[:, width:], pick_ref[...]).astype(bf16)
+    weights = jnp.concatenate([thin_ref[:, :width], picked], axis=1)
+
+    @pl.when(pl.program_id(0) == 0)
+    def _():
+        scr_ref[...] = mm(own_ref[...], weights)
+
+    @pl.when(pl.program_id(0) == 1)
+    def _():
+        scr_ref[...] = mm(other_ref[...], weights)
+
+    columns = ids_ref[0].T
+    at = slice(HALO, HALO + length)
+    ids = columns[at, :1]
+    before = columns[HALO - 1 : HALO, :1]
+    eight = lax.broadcasted_iota(jnp.int32, (length, 8), 1)
+    flags = jnp.where(eight == 3, ids, 0.0)
+    near = {}
+    for j, k in enumerate((-1, -2, -3, 0, 1, 2, 3)):
+        if k != 0:
+            near[k] = (columns[HALO + k : HALO + k + length, :1] == ids).astype(f32)
+            flags = jnp.where(eight == j, near[k], flags)
+    flags_ref[0] = flags
+
+    bcx_ref[0] = scr_ref[:, :width]
+    pre = cbc_ref[4:5, :] + cbc_ref[0:1, :] * scr_ref[at, :width]
+    for k in range(1, 4):
+        pre = pre + cbc_ref[k : k + 1, :] * scr_ref[HALO - k : HALO - k + length, :width] * near[-k]
+    act = pre * jax.nn.sigmoid(pre)
+    pre_ref[0] = pre
+    act_ref[0] = act
+    turned_ref[0] = act.T.astype(bf16)
+    low_ref[0] = act[:, width // 2 :].astype(bf16)
+
+    dt_in = scr_ref[at, width:] + lanes_ref[0:1, :]
+    dt_ref[0] = dt_in
+    step = jnp.maximum(dt_in, 0.0) + jnp.log1p(jnp.exp(-jnp.abs(dt_in)))
+    log_step = step * lanes_ref[1:2, :]
+    log_ref[0] = log_step
+    tri = (
+        lax.broadcasted_iota(jnp.int32, (CH, CH), 0) >= lax.broadcasted_iota(jnp.int32, (CH, CH), 1)
+    ).astype(f32)
+    quarter = lax.broadcasted_iota(jnp.int32, (CH, 128), 1) // 32
+    low_lanes = lax.broadcasted_iota(jnp.int32, (CH, 128), 1) < 32
+    row_at = lax.broadcasted_iota(jnp.int32, (32, CH), 0)
+    to_wide = (
+        lax.broadcasted_iota(jnp.int32, (128, channels), 1) // 64 == lax.broadcasted_iota(jnp.int32, (128, channels), 0)
+    ).astype(f32)
+    eight_rows = lax.broadcasted_iota(jnp.int32, (8, 128), 0)
+    alphas = jnp.zeros((8, 128), f32)
+    lead = jnp.zeros((1, 128), f32)
+    chunk_before = before
+    for c in range(n_chunks):
+        rows = slice(c * CH, (c + 1) * CH)
+        running = exact(tri, log_step[rows])
+        last = running[CH - 1 : CH, :]
+        ids_c = ids[rows]
+        chunk_end = ids_c[CH - 1 : CH, :]
+        still = (chunk_end == chunk_before).astype(f32)
+        alphas = jnp.where(eight_rows == c, still * jnp.exp(last), alphas)
+        since = (ids_c == before).astype(f32) * jnp.exp(running + lead)
+        since = jnp.where(low_lanes, since, 0.0).astype(bf16)
+        since_ref[0, rows, :] = mm(since, to_wide.astype(bf16)).astype(bf16)
+        hv = jnp.where(
+            quarter == 0,
+            running * LOG2E,
+            jnp.where(
+                quarter == 1,
+                step[rows],
+                jnp.where(
+                    quarter == 2,
+                    (ids_c == chunk_before).astype(f32) * jnp.exp(running),
+                    (ids_c == chunk_end).astype(f32) * jnp.exp(last - running),
+                ),
+            ),
+        )
+        hv_ref[0, rows, :] = hv
+        turned = hv.T[:32, :]
+        rv_ref[0, :, rows] = jnp.where(
+            row_at < 24, turned, jnp.where(row_at == 24, row_ref[0, 0:1, rows], 0.0)
+        )
+        lead = lead + last
+        chunk_before = chunk_end
+    first = lax.broadcasted_iota(jnp.int32, (8, 128), 1) < 32
+    al_ref[0] = exact(jnp.where(first, alphas, 0.0), to_wide)
+
+
+def prepare(own, other, thin, pick, lanes, cbc, ids_all, ids_rows, channels):
+    length = own.shape[0] - HALO
+    width = cbc.shape[1]
+    whole = lambda v: pl.BlockSpec(v.shape, lambda s: (0,) * len(v.shape), pipeline_mode=pl.Buffered(1))
+    piece = lambda shape: pl.BlockSpec((1,) + shape, lambda s: (s, 0, 0))
+    outs = [
+        ((HALO + length, width), f32), ((length, width), f32), ((length, width), f32), ((width, length), bf16),
+        ((length, width // 2), bf16), ((length, 128), f32), ((length, 128), f32), ((length, 128), f32),
+        ((32, length), f32), ((8, channels), f32), ((length, channels), bf16), ((length, 8), f32),
+    ]
+    return pl.pallas_call(
+        prepare_body,
+        grid=(2,),
+        in_specs=[whole(v) for v in (own, other, thin, pick, lanes, cbc)]
+        + [piece(ids_all.shape[1:]), piece(ids_rows.shape[1:])],
+        out_specs=[piece(shape) for shape, _ in outs],
+        out_shape=[jax.ShapeDtypeStruct((2,) + shape, kind) for shape, kind in outs],
+        scratch_shapes=[pltpu.VMEM((HALO + length, width + 128), f32)],
+        cost_estimate=pl.CostEstimate(flops=1, transcendentals=0, bytes_accessed=1),
+        name="prepare",
+    )(own, other, thin, pick, lanes, cbc, ids_all, ids_rows)
+
+
+def gate_sums_body(here_ref, since_ref, low_ref, state_ref, gate_ref, grad_ref, gain_ref, y_ref, sums_ref):
+    y = here_ref[...] + since_ref[...].astype(f32) * mm(low_ref[...], state_ref[0])
+    y_ref[...] = y
+    gate = gate_ref[...]
+    gated = y * (gate * jax.nn.sigmoid(gate))
+    scaled = grad_ref[...] * gain_ref[...]
+    lane = lax.broadcasted_iota(jnp.int32, sums_ref.shape, 1)
+    sums_ref[...] = jnp.where(
+        lane == 0,
+        jnp.sum(gated * gated, axis=1, keepdims=True),
+        jnp.where(lane == 1, jnp.sum(scaled * gated, axis=1, keepdims=True), 0.0),
+    )
+
+
+def gate_sums(here, since, low, state, gate, grad, gain):
+    tokens, channels = here.shape
+    tile = 128
+    per = tokens // tile // 2
+    token = lambda width: pl.BlockSpec((tile, width), lambda i: (i, 0))
+    return pl.pallas_call(
+        gate_sums_body,
+        grid=(tokens // tile,),
+        in_specs=[
+            token(channels), token(channels), token(low.shape[1]),
+            pl.BlockSpec((1,) + state.shape[1:], lambda i: (i // per, 0, 0)),
+            token(channels), token(channels), pl.BlockSpec((1, channels), lambda i: (0, 0)),
+        ],
+        out_specs=[token(channels), token(128)],
+        out_shape=[jax.ShapeDtypeStruct((tokens, channels), f32), jax.ShapeDtypeStruct((tokens, 128), f32)],
+        cost_estimate=pl.CostEstimate(flops=1, transcendentals=0, bytes_accessed=1),
+        name="gate_sums",
+    )(here, since, low, state, gate, grad, gain)
+
+
+def gate_grads_body(
+    all_channels, per, y_ref, since_ref, low_ref, gate_ref, grad_ref, gain_ref, sums_ref, came_ref,
+    mixed_ref, gate_grad_ref, y_grad_ref, gain_grad_ref, state_ref,
+):
+    at = pl.program_id(0)
+    y = y_ref[...]
+    gate = gate_ref[...]
+    grad = grad_ref[...]
+    sums = sums_ref[...] + came_ref[...]
+    gate_rms = lax.rsqrt(sums[:, 0:1] / all_channels + epsilon)
+    inner = gate_rms * gate_rms * gate_rms * (sums[:, 1:2] / all_channels)
+    sig = jax.nn.sigmoid(gate)
+    act = gate * sig
+    gated = y * act
+    hat = gated * gate_rms
+    mixed_ref[...] = (hat * gain_ref[...]).astype(bf16)
+    gated_grad = gate_rms * (grad * gain_ref[...]) - gated * inner
+    y_grad = gated_grad * act
+    y_grad_ref[...] = y_grad
+    gate_grad_ref[...] = (gated_grad * y * sig * (1.0 + gate * (1.0 - sig))).astype(bf16)
+    part = jnp.sum((grad * hat).reshape((y.shape[0] // 8, 8, y.shape[1])), axis=0)
+    pushed = tmm(low_ref[...], (y_grad * since_ref[...].astype(f32)).astype(bf16))
+
+    @pl.when(at == 0)
+    def _():
+        gain_grad_ref[...] = part
+
+    @pl.when(at > 0)
+    def _():
+        gain_grad_ref[...] += part
+
+    @pl.when(lax.rem(at, per) == 0)
+    def _():
+        state_ref[0] = pushed
+
+    @pl.when(lax.rem(at, per) > 0)
+    def _():
+        state_ref[0] += pushed
+
+
+def gate_grads(y, since, low, gate, grad, gain, sums, came, all_channels):
+    tokens, channels = y.shape
+    tile = 128
+    count = tokens // tile
+    per = count // 2
+    token = lambda width: pl.BlockSpec((tile, width), lambda i: (i, 0))
+    turned = pl.BlockSpec((tile, 128), lambda i: (lax.rem(i + per, count), 0))
+    return pl.pallas_call(
+        lambda *refs: gate_grads_body(all_channels, per, *refs),
+        grid=(count,),
+        in_specs=[
+            token(channels), token(channels), token(low.shape[1]), token(channels), token(channels),
+            pl.BlockSpec((1, channels), lambda i: (0, 0)), token(128), turned,
+        ],
+        out_specs=[
+            token(channels), token(channels), token(channels), pl.BlockSpec((8, channels), lambda i: (0, 0)),
+            pl.BlockSpec((1, low.shape[1], channels), lambda i: (i // per, 0, 0)),
+        ],
+        out_shape=[
+            jax.ShapeDtypeStruct((tokens, channels), bf16),
+            jax.ShapeDtypeStruct((tokens, channels), bf16),
+            jax.ShapeDtypeStruct((tokens, channels), f32),
+            jax.ShapeDtypeStruct((8, channels), f32),
+            jax.ShapeDtypeStruct((2, low.shape[1], channels), f32),
+        ],
+        cost_estimate=pl.CostEstimate(flops=1, transcendentals=0, bytes_accessed=1),
+        name="gate_grads",
+    )(y, since, low, gate, grad, gain, sums, came)
+
+
+def small_grads_body(
+    dbc_ref, came_ref, pre_ref, bcx_ref, flags_ref, own_col_ref, other_col_ref, own_row_ref, other_row_ref,
+    log_ref, dt_ref, lanes_ref, back_ref, own_sums_ref, other_sums_ref, gain_ref, dpre_ref, dt_low_ref, taps_ref,
+    packed_ref,
+):
+    length = dpre_ref.shape[0]
+    width = dpre_ref.shape[1]
+    channels = packed_ref.shape[1]
+    pre = pre_ref[0]
+    sig = jax.nn.sigmoid(pre)
+    dpre = (dbc_ref[0] + came_ref[...]) * (sig * (1.0 + pre * (1.0 - sig)))
+    dpre_ref[...] = dpre
+    sums = [jnp.sum(dpre * bcx_ref[0, HALO:, :], axis=0, keepdims=True)]
+    for k in range(1, 4):
+        shifted = bcx_ref[0, HALO - k : HALO - k + length, :]
+        sums.append(jnp.sum(dpre * shifted * flags_ref[0, :, k - 1 : k], axis=0, keepdims=True))
+    sums.append(jnp.sum(dpre, axis=0, keepdims=True))
+    taps_ref[...] = jnp.concatenate(sums + [jnp.zeros((11, width), f32)], axis=0)
+
+    tri = (
+        lax.broadcasted_iota(jnp.int32, (CH, CH), 1) >= lax.broadcasted_iota(jnp.int32, (CH, CH), 0)
+    ).astype(f32)
+    raw_sum = jnp.zeros((1, 128), f32)
+    rate_sum = jnp.zeros((1, 128), f32)
+    for p, (col_ref, row_ref) in enumerate(((own_col_ref, own_row_ref), (other_col_ref, other_row_ref))):
+        for c in range(length // CH):
+            rows = slice(c * CH, (c + 1) * CH)
+            by_row = jnp.concatenate([row_ref[0, :, rows], jnp.zeros((96, CH), f32)], axis=0).T
+            dlog = exact(tri, col_ref[0, rows, :128] - by_row)
+            dstep = col_ref[0, rows, 128:] + dlog * lanes_ref[1:2, :]
+            raw = dstep * jax.nn.sigmoid(dt_ref[p, rows, :])
+            rate_sum += jnp.sum(dlog * log_ref[p, rows, :], axis=0, keepdims=True)
+            raw_sum += jnp.sum(raw, axis=0, keepdims=True)
+            dt_low_ref[p, rows, :] = mm(raw.astype(bf16), back_ref[...]).astype(bf16)
+    to_wide = (
+        lax.broadcasted_iota(jnp.int32, (128, channels), 1) // 64 == lax.broadcasted_iota(jnp.int32, (128, channels), 0)
+    ).astype(f32)
+    both = jnp.concatenate([raw_sum, rate_sum, jnp.zeros((6, 128), f32)], axis=0)
+    first = lax.broadcasted_iota(jnp.int32, (8, 128), 1) < 32
+    wide = exact(jnp.where(first, both, 0.0), to_wide)
+    sums = own_sums_ref[0] + other_sums_ref[0]
+    gain = jnp.sum(gain_ref[...], axis=0, keepdims=True)
+    packed_ref[...] = jnp.concatenate(
+        [sums[:5], gain, sums[5:6], wide[:2], jnp.zeros((7, channels), f32)], axis=0
+    )
+
+
+def small_grads(dbc, came, pre, *rest):
+    length, width = came.shape
+    channels = rest[-1].shape[1]
+    return pl.pallas_call(
+        small_grads_body,
+        out_shape=[
+            jax.ShapeDtypeStruct((length, width), f32),
+            jax.ShapeDtypeStruct((2, length, 128), bf16),
+            jax.ShapeDtypeStruct((16, width), f32),
+            jax.ShapeDtypeStruct((16, channels), f32),
+        ],
+        cost_estimate=pl.CostEstimate(flops=1, transcendentals=0, bytes_accessed=1),
+        name="small_grads",
+    )(dbc, came, pre, *rest)
+
+
+def normed_grads_body(
+    dpre_ref, head_ref, flags_ref, cbc_ref, dt_low_ref, own_turned_ref, other_turned_ref, own_ref, other_ref, gate_ref,
+    wx_ref, wz_ref, thin_ref, own_out_ref, other_out_ref, part_ref, low_ref, scr_ref,
+):
+    length, width = dpre_ref.shape
+
+    @pl.when((pl.program_id(0) == 0) & (pl.program_id(1) == 0))
+    def _():
+        scr_ref[:length, :] = dpre_ref[...]
+        scr_ref[length:, :] = head_ref[...]
+        raw = cbc_ref[0:1, :] * dpre_ref[...]
+        for k in range(1, 4):
+            raw = raw + cbc_ref[k : k + 1, :] * scr_ref[k : k + length, :] * flags_ref[0, :, 3 + k : 4 + k]
+        own = jnp.concatenate([raw.astype(bf16), dt_low_ref[0]], axis=1)
+        other = jnp.concatenate([jnp.zeros((length, width), bf16), dt_low_ref[1]], axis=1)
+        low_ref[:length, :] = own
+        low_ref[length:, :] = other
+        part_ref[...] = (mm(own_turned_ref[...], own) + mm(other_turned_ref[...], other)).astype(bf16)
+
+    def total(ref, rows):
+        return (
+            mmt(ref[...], wx_ref[...]) + mmt(gate_ref[rows, :], wz_ref[...]) + mmt(low_ref[rows, :], thin_ref[...])
+        )
+
+    @pl.when(pl.program_id(0) == 0)
+    def _():
+        other_out_ref[...] = total(other_ref, slice(length, 2 * length)).astype(bf16)
+
+    @pl.when(pl.program_id(0) == 1)
+    def _():
+        own_out_ref[...] = total(own_ref, slice(0, length))
+
+
+def normed_grads(dpre, head, flags, cbc, dt_low, turned, x_low, gate_grad, wx, wz, thin):
+    length, width = dpre.shape
+    features = wx.shape[0]
+    tile = features // 3
+    last = features // tile - 1
+    whole = lambda v: pl.BlockSpec(v.shape, lambda p, j: (0,) * len(v.shape), pipeline_mode=pl.Buffered(1))
+    weight = lambda v: pl.BlockSpec((tile, v.shape[1]), lambda p, j: (j, 0))
+    return pl.pallas_call(
+        normed_grads_body,
+        grid=(2, features // tile),
+        in_specs=[whole(v) for v in (dpre, head, flags, cbc, dt_low, *turned, *x_low, gate_grad)]
+        + [weight(v) for v in (wx, wz, thin)],
+        out_specs=[
+            pl.BlockSpec((length, tile), lambda p, j: (0, j * p)),
+            pl.BlockSpec((length, tile), lambda p, j: (0, j * (1 - p) + last * p)),
+            pl.BlockSpec((features, width + 128), lambda p, j: (0, 0), pipeline_mode=pl.Buffered(1)),
+        ],
+        out_shape=[
+            jax.ShapeDtypeStruct((length, features), f32),
+            jax.ShapeDtypeStruct((length, features), bf16),
+            jax.ShapeDtypeStruct((features, width + 128), bf16),
+        ],
+        scratch_shapes=[pltpu.VMEM((2 * length, width + 128), bf16), pltpu.VMEM((length + 8, width), f32)],
+        cost_estimate=pl.CostEstimate(
+            flops=8 * length * features * features, transcendentals=0, bytes_accessed=8 * features * features
+        ),
+        name="normed_grads",
+    )(dpre, head, flags, cbc, dt_low, *turned, *x_low, gate_grad, wx, wz, thin)
+
+
+def x_grads_body(own_ref, came_ref, x_ref, cot_ref, gain_ref, out_ref, gain_grad_ref):
+    grad = own_ref[...] + came_ref[...].astype(f32)
+    x = x_ref[...].astype(f32)
+    inv = lax.rsqrt(jnp.mean(x * x, axis=-1, keepdims=True) + epsilon)
+    hat = x * inv
+    part = jnp.sum((grad * hat).reshape((x.shape[0] // 8, 8, x.shape[1])), axis=0)
+    pushed = grad * gain_ref[...]
+    inner = jnp.mean(pushed * x, axis=-1, keepdims=True)
+    out_ref[...] = cot_ref[...].astype(f32) + inv * pushed - hat * (inv * inv * inner)
+
+    @pl.when(pl.program_id(0) == 0)
+    def _():
+        gain_grad_ref[...] = part
+
+    @pl.when(pl.program_id(0) > 0)
+    def _():
+        gain_grad_ref[...] += part
+
+
+def x_grads(own, came, x, cot, gain):
+    tokens, features = own.shape
+    tile = 128
+    token = pl.BlockSpec((tile, features), lambda i: (i, 0))
+    return pl.pallas_call(
+        x_grads_body,
+        grid=(tokens // tile,),
+        in_specs=[token] * 4 + [pl.BlockSpec((1, features), lambda i: (0, 0))],
+        out_specs=[token, pl.BlockSpec((8, features), lambda i: (0, 0))],
+        out_shape=[jax.ShapeDtypeStruct((tokens, features), f32), jax.ShapeDtypeStruct((8, features), f32)],
+        cost_estimate=pl.CostEstimate(flops=1, transcendentals=0, bytes_accessed=1),
+        name="x_grads",
+    )(own, came, x, cot, gain)
 
 
 def weight_parts_body(count, group, flip, at_ref, *refs):
     keep_ref, give_ref = refs[-2:]
     rows, columns = keep_ref.shape[3:]
-    per = (len(refs) - 2 - count) // count
+    rights_per = (len(refs) - 2) // count - 2
     for w in range(count):
-        left_ref, right_refs = refs[w], refs[count + w * per : count + (w + 1) * per]
+        lefts = refs[2 * w : 2 * w + 2]
+        rights = refs[2 * count + w * rights_per : 2 * count + (w + 1) * rights_per]
+        tokens = lefts[0].shape[1]
 
         @pl.when(pl.program_id(0) == w)
         def _():
-            rights = [
-                jnp.concatenate(
-                    [ref[:, pl.ds(pl.multiple_of(at_ref[4 + d], columns), columns)] for d in group], axis=1
+            def right(i):
+                ref, start = (rights[0], i * tokens) if rights_per == 1 else (rights[i], 0)
+                return jnp.concatenate(
+                    [
+                        ref[start : start + tokens, pl.ds(pl.multiple_of(at_ref[4 + d], columns), columns)]
+                        for d in group
+                    ],
+                    axis=1,
                 )
-                for ref in right_refs
-            ]
-            tokens = right_refs[0].shape[0]
+
+            values = [right(0), right(1)]
             for k in range(4):
                 left = pl.ds(pl.multiple_of(at_ref[k], rows), rows)
-                part = mm(left_ref[left, :tokens], rights[0])
-                for i in range(1, per):
-                    part = part + mm(left_ref[left, i * tokens : (i + 1) * tokens], rights[i])
+                part = mm(lefts[0][left, :], values[0]) + mm(lefts[1][left, :], values[1])
                 part = part.astype(bf16)
                 away, place = (k // 2, k % 2) if flip == 0 else (k % 2, k // 2)
                 target = give_ref if away else keep_ref
@@ -401,11 +828,12 @@
 
 
 def weight_parts(at, lefts, rights, group, own_rows, columns, flip):
+    count = len(lefts)
+    tokens = 2 * lefts[0][0].shape[1]
+    lefts = [piece for left in lefts for piece in left]
     rights = [piece for right in rights for piece in right]
-    count = len(lefts)
     shape = (count, len(group), 2, 2 * own_rows, columns)
     whole = lambda v: pl.BlockSpec(v.shape, lambda w, at: (0, 0), pipeline_mode=pl.Buffered(1))
-    tokens = lefts[0].shape[1]
     return pl.pallas_call(
         lambda *refs: weight_parts_body(count, group, flip, *refs),
         grid_spec=pltpu.PrefetchScalarGridSpec(
@@ -509,6 +937,14 @@
             now = (keep.astype(f32) + across(give, bit).astype(f32)).astype(whole.dtype)
         return now
 
+    def half_rows(self, whole, bit):
+        keep = lax.dynamic_index_in_dim(whole, self.side[bit], whole.ndim - 3, keepdims=False)
+        give = lax.dynamic_index_in_dim(whole, 1 - self.side[bit], whole.ndim - 3, keepdims=False)
+        return (keep.astype(f32) + across(give, bit).astype(f32)).astype(whole.dtype)
+
+    def ordered_sum(self, part):
+        return self.half_rows(part.reshape((2, 2, 2, -1, part.shape[1])), 0)
+
     def gather_weight(self, mine, other):
         both = self.ordered(0, mine, other, 0).reshape((-1, mine.shape[1]))
         blocks = self.gather_slots(both)
@@ -535,7 +971,7 @@
         return out.reshape((rows // 2, -1))
 
     def fast(self, half_channels):
-        return len(self.bits) == 2 and half_channels % 128 == 0
+        return len(self.bits) == 2 and self.slots == 4 and half_channels % 128 == 0
 
     def offsets(self, own_rows, half_channels):
         chip = lax.axis_index("dp") // 2
@@ -563,12 +999,16 @@
     def second_exchange(self, at, term):
         return across(term, self.bits[at])
 
-    def slot_sum(self, keeps, cames, lasts, groups):
+    def slot_parts(self, keeps, cames, lasts, groups):
         own = {}
         for group, keep, came, last in zip(groups, keeps, cames, lasts):
             total = keep[:, :, 0].astype(f32) + came[:, :, 0].astype(f32) + last.astype(f32)
             for i, d in enumerate(group):
                 own[d] = total[:, i]
+        return own
+
+    def slot_sum(self, keeps, cames, lasts, groups):
+        own = self.slot_parts(keeps, cames, lasts, groups)
         return own[0], [around(own[d].astype(bf16), -d) for d in range(1, self.slots)]
 
     def to_owner(self, own, others):
@@ -950,17 +1390,13 @@
     mine = lax.dynamic_index_in_dim(stacked, core, 2, keepdims=False)
     other = swap(lax.dynamic_index_in_dim(stacked, 1 - core, 2, keepdims=False))
     both = place.ordered(0, mine, other, 1).reshape((3, 2 * own_rows, half_channels))
-    (
-        both, x_in, segment_ids, norm_gain, w_bc, w_dt, conv_x, conv_x_bias, dt_bias, a_log, d_skip, gate_gain, cotangent,
-    ) = tie(both, x_in, segment_ids, norm_gain, w_bc, w_dt, conv_x, conv_x_bias, dt_bias, a_log, d_skip, gate_gain, cotangent)
-
-    wx_here = [both[:1]] + [around(both[:1], d) for d in range(1, slots)]
-    wx_items = []
-    for d in range(slots):
-        one, two = place.unit(d, wx_here[d])
-        wx_items += place.items(d, wx_here[d], one, two, place.forward(d, one))
-    pair, _ = tie(both[1:], wx_here[1:])
-    pair_here = [pair] + [around(pair, d) for d in range(1, slots)]
+    padded = jnp.pad(segment_ids, ((0, 0), (HALO, HALO)), constant_values=-1)
+    ids_own = lax.dynamic_slice(
+        padded, (slot // pieces, (slot % pieces) * length), (1, length + 2 * HALO)
+    )
+    ids_all = jnp.concatenate([ids_own, swap(ids_own)], axis=0).astype(f32)
+    both, ids_all, conv_x, conv_x_bias, gate_gain, dt_bias, a_log, d_skip, w_dt, w_bc, norm_gain, x_in, cotangent = tie(
+        both, ids_all, conv_x, conv_x_bias, gate_gain, dt_bias, a_log, d_skip, w_dt, w_bc, norm_gain, x_in, cotangent)
 
     rows = jnp.concatenate(
         [
@@ -976,11 +1412,43 @@
         axis=0,
     )
     rows = place.gather_slots(rows)
+    halo = along_sequence(x_in[-HALO:], pieces, True)
+    wx_here = [both[:1]] + [around(both[:1], d) for d in range(1, slots)]
+    wx_one, wx_two = {}, {}
+    wx_one[0], wx_two[0] = place.unit(0, wx_here[0])
+    cot_turned_own = turn(cotangent)
+    rows, halo, wx_here[slots - 1], wx_one, wx_two, cot_turned_own, w_bc, norm_gain = tie(
+        rows, halo, wx_here[slots - 1], wx_one, wx_two, cot_turned_own, w_bc, norm_gain)
     dt_slots = rows[8:, :, :own_rows].transpose(2, 1, 0).reshape((own_rows, all_heads)).astype(bf16)
     thin = jnp.concatenate([w_bc, dt_slots, norm_gain[:, None]], axis=1)
     thin = jnp.pad(thin, ((0, 0), (0, bc_width + 128 - thin.shape[1])))
-    thin = place.ordered(0, thin, swap(thin), 0).reshape((2 * own_rows, -1))
-    thin = place.gather_rows(thin, True)
+    thin = place.ordered(0, thin, swap(thin), 0)
+    low, high = place.bits
+    thin = place.ordered(low, thin, across(thin, low), 0)
+    odd = slots - 1
+    wx_one[odd] = across(wx_here[odd], high)
+    thin, wx_here[odd], wx_here[1], wx_one, cot_turned_own, cotangent = tie(
+        thin, wx_here[odd], wx_here[1], wx_one, cot_turned_own, cotangent)
+    thin = place.ordered(high, thin, across(thin, high), 0).reshape((features, -1))
+    wx_two[odd] = across(wx_here[odd], low)
+    gain = thin[:, bc_width + all_heads].astype(f32)[None, :]
+    thin, gain, wx_here, wx_two, both, cot_turned_own, cotangent = tie(
+        thin, gain, wx_here, wx_two, both, cot_turned_own, cotangent)
+    pair_here = {0: both[1:], 1: around(both[1:], 1)}
+    normed_own, normed_turned_own = norm(x_in, halo, gain)
+    normed_both = [normed_own, swap(normed_own)]
+    for d in range(1, slots - 1):
+        wx_one[d], wx_two[d] = place.unit(d, wx_here[d])
+
+    thin, gain, normed_both, normed_turned_own, pair_here, rows, ids_all, wx_here, wx_one, wx_two = tie(
+        thin, gain, normed_both, normed_turned_own, pair_here, rows, ids_all, wx_here, wx_one, wx_two)
+    normed_turned = [normed_turned_own, swap(normed_turned_own)]
+    cot = [cotangent, swap(cotangent)]
+    cot_turned = [cot_turned_own, swap(cot_turned_own)]
+
+    pair_here[2] = around(pair_here[0], 2)
+    one, two, both_k = {}, {}, {}
+    one[0], two[0] = place.unit(0, pair_here[0])
     own = lax.dynamic_index_in_dim(
         rows[:8].reshape((8, slots, 2, half_channels)), core, 2, keepdims=False
     ).reshape((8, channels))
@@ -989,98 +1457,27 @@
     head_at = lane % 32
     global_head = (head_at // half_heads) * slot_heads + core * half_heads + head_at % half_heads
     pick = ((lane[:, None] == global_head[None, :]) & (head_at < heads)[None, :]).astype(f32)
+    first_lanes = (lane < 32).astype(f32)
     small = rows[6, :, : 3 * slot_heads].reshape((slots, 3, slot_heads)).transpose(1, 0, 2)
     small = jnp.pad(small.reshape((3, all_heads)), ((0, 5), (0, 128 - all_heads)))
     small = exact(small, pick)
     bias_lanes = small[0]
     rate_lanes = jnp.where(head_at < heads, -jnp.exp(small[1]), 0.0)
     to_heads = head_map(channels, f32)
-    skip_row = exact(small[2:3] * (lane < 32), to_heads.T)
+    skip_row = exact(small[2:3] * first_lanes, to_heads.T)
     cw = jnp.concatenate([own[:5], skip_row, jnp.zeros((2, channels), f32)], axis=0)
-
-    padded = jnp.pad(segment_ids, ((0, 0), (HALO, HALO)), constant_values=-1)
-    ids_own = lax.dynamic_slice(
-        padded, (slot // pieces, (slot % pieces) * length), (1, length + 2 * HALO)
-    )
-    ids_all = jnp.concatenate([ids_own, swap(ids_own)], axis=0)
-    ids = ids_all[:, HALO : HALO + length]
-    before = ids_all[:, HALO - 1]
-
-    def near(k):
-        return ids_all[:, HALO + k : HALO + k + length] == ids
-
-    flags = [near(-1), near(-2), near(-3), ids, near(1), near(2), near(3), jnp.zeros_like(ids)]
-    flags = jnp.stack([v.astype(f32) for v in flags], axis=-1)
-
-    x_rows = jnp.concatenate([along_sequence(x_in[-HALO:], pieces, True), x_in], axis=0)
-    tokens_ext = x_rows.astype(f32)
-    inv_ext = lax.rsqrt(jnp.mean(tokens_ext * tokens_ext, axis=-1, keepdims=True) + epsilon)
-    gain = thin[:, bc_width + all_heads].astype(f32)[None, :]
-    normed_own = (tokens_ext * inv_ext * gain).astype(bf16)
-    normed_other = swap(normed_own)
-    normed_ext = jnp.concatenate([normed_own, normed_other], axis=0)
-    normed = jnp.concatenate([normed_own[HALO:], normed_other[HALO:]], axis=0)
-    tokens, inv_rms = tokens_ext[HALO:], inv_ext[HALO:]
-    cot = jnp.concatenate([cotangent, swap(cotangent)], axis=0)
-    normed_turned, cot_turned = normed.T, cot.T
-
-    dt_pick = jnp.dot(thin[:, bc_width:], pick.astype(bf16), preferred_element_type=f32).astype(bf16)
-    thin_proj = mm(normed_ext, jnp.concatenate([thin[:, :bc_width], dt_pick], axis=1))
-    thin_proj = thin_proj.reshape((2, HALO + length, -1))
-    bc_ext = thin_proj[:, :, :bc_width]
-    dt_in = thin_proj[:, HALO:, bc_width:] + bias_lanes
-
-    bc_pre = conv_bc_bias + conv_bc[0] * bc_ext[:, HALO:]
-    for k in range(1, conv_bc.shape[0]):
-        shifted = bc_ext[:, HALO - k : HALO - k + length]
-        bc_pre = bc_pre + conv_bc[k] * shifted * flags[:, :, k - 1 : k]
-    bc_act = jax.nn.silu(bc_pre)
-    bc_turned = bc_act.astype(bf16).transpose(0, 2, 1)
-    c_low = bc_act[:, :, bc_width // 2 :].astype(bf16)
-
-    step = jax.nn.softplus(dt_in)
-    log_step = (step * rate_lanes).reshape((2 * n_chunks, CH, 128))
+    lanes = jnp.concatenate([bias_lanes[None], rate_lanes[None], jnp.zeros((6, 128), f32)], axis=0)
+    cbc = jnp.concatenate([conv_bc, conv_bc_bias[None], jnp.zeros((3, bc_width), f32)], axis=0)
+    wide_ids = jnp.pad(ids_all, ((0, 0), (0, -ids_all.shape[1] % 128)))
+    wide_ids = jnp.broadcast_to(wide_ids[:, None, :], (2, 8, wide_ids.shape[1]))
+    ids_rows = jnp.broadcast_to(ids_all[:, None, HALO : HALO + length], (2, 8, length))
     tri = (jnp.arange(CH)[:, None] >= jnp.arange(CH)[None, :]).astype(f32)
-    running = jnp.einsum("ts,csh->cth", tri, log_step, precision=highest)
-    running = running.reshape((2, n_chunks, CH, 128))
-    last = running[:, :, -1:, :]
-    ids_chunks = ids.reshape((2, n_chunks, CH, 1))
-    chunk_end = ids_chunks[:, :, -1:, :]
-    chunk_before = jnp.concatenate([before[:, None, None, None], chunk_end[:, :-1]], axis=1)
-    still = (chunk_end == chunk_before).astype(f32)
-    alpha = still * jnp.exp(last)
-    lead = jnp.cumsum(last, axis=1) - last
-    since_piece = (ids_chunks == before[:, None, None, None]).astype(f32) * jnp.exp(running + lead)
-    since_piece = since_piece.reshape((2 * length, 128))
-    group_lane = lane // 32
-    hv = jnp.where(
-        group_lane == 0,
-        running * LOG2E,
-        jnp.where(
-            group_lane == 1,
-            step.reshape((2, n_chunks, CH, 128)),
-            jnp.where(
-                group_lane == 2,
-                (ids_chunks == chunk_before).astype(f32) * jnp.exp(running),
-                (ids_chunks == chunk_end).astype(f32) * jnp.exp(last - running),
-            ),
-        ),
-    ).reshape((2, length, 128))
-    rv = jnp.concatenate(
-        [
-            hv[:, :, :24].transpose(0, 2, 1),
-            ids.astype(f32)[:, None, :],
-            jnp.zeros((2, 7, length), f32),
-        ],
-        axis=1,
-    )
-    first_lanes = (lane < 32).astype(f32)
-    al = exact((alpha * first_lanes).reshape((2 * n_chunks, 128)), to_heads.T)
-    al = al.reshape((2, n_chunks, channels))
-    whole_alpha = jnp.prod(al, axis=1, keepdims=True)
-    al = jnp.pad(al, ((0, 0), (0, 8 - n_chunks), (0, 0)))
-    wide_since = mm((since_piece * first_lanes).astype(bf16), to_heads.T.astype(bf16))
-    wide_since = wide_since.reshape((2, length, channels))
+
+    bc_ext, bc_pre, bc_act, bc_turned, c_low, dt_in, log_step, hv, rv, al, wide_since, flags = prepare(
+        normed_both[0], normed_both[1], thin, pick.astype(bf16), lanes, cbc, wide_ids, ids_rows, channels)
+    whole_alpha = jnp.prod(al[:, :n_chunks], axis=1, keepdims=True)
+    log_step = log_step.reshape((2 * n_chunks, CH, 128))
+    wx_both = {d: place.forward(d, wx_one[d]) for d in range(slots)}
 
     def hand_on(local, forward):
         low = local.astype(bf16)
@@ -1089,66 +1486,53 @@
             low = (local + whole_alpha * came.astype(f32)).astype(bf16)
         return along_sequence(low, pieces, forward)
 
-    (wx_blocks, pair_here[0], pair_here[1], normed_ext, hv, rv, al, bc_act, bc_turned, cw, wide_since, c_low, normed,
-     normed_turned, cot, cot_turned) = tie(
-        [item[0] for item in wx_items], pair_here[0], pair_here[1], normed_ext, hv, rv, al, bc_act, bc_turned, cw,
-        wide_since, c_low, normed, normed_turned, cot, cot_turned)
-    wx_items = [(block,) + item[1:] for block, item in zip(wx_blocks, wx_items)]
-    one, two, both_k = {}, {}, {}
-    one[0], two[0] = place.unit(0, pair_here[0])
+    (one, two, pair_here, wx_here, wx_one, wx_two, wx_both, normed_both, hv, rv, al, bc_act, bc_turned, cw, wide_since, c_low, flags, bc_ext, bc_pre,
+     dt_in, log_step) = tie(
+        one, two, pair_here, wx_here, wx_one, wx_two, wx_both, normed_both, hv, rv, al, bc_act, bc_turned, cw, wide_since, c_low, flags,
+        bc_ext, bc_pre, dt_in, log_step)
+    wx_items = []
+    for d in range(slots):
+        wx_items += place.items(d, wx_here[d], wx_one[d], wx_two[d], wx_both[d])
+
+    pair_here[3] = around(pair_here[0], 3)
+    both_k[0] = place.forward(0, one[0])
     one[1], two[1] = place.unit(1, pair_here[1])
-    x_ext, wx = project(normed_ext, at, wx_items, 0, channels)
+    one[2] = across(pair_here[2], place.bits[0])
+    x_ext, wx = project(normed_both, 0, at, wx_items, 0, channels)
     x_ext = x_ext.reshape((2, HALO + length, channels))
 
-    x_ext, one[0], two[0], one[1], two[1], pair_here[2], pair_here[3] = tie(
-        x_ext, one[0], two[0], one[1], two[1], pair_here[2], pair_here[3])
-    both_k[0], both_k[1] = place.forward(0, one[0]), place.forward(1, one[1])
-    one[2], one[3] = across(pair_here[2], place.bits[0]), across(pair_here[3], place.bits[1])
+    x_ext, one, two, both_k, pair_here = tie(x_ext, one, two, both_k, pair_here)
+    one[3], two[3] = place.unit(3, pair_here[3])
+    two[2] = across(pair_here[2], place.bits[1])
+    both_k[1] = place.forward(1, one[1])
     y_here, states = scan_fwd(hv, flags, rv, al, bc_act, bc_turned, x_ext, cw, CH)
 
-    y_here, states, both_k[0], both_k[1], one[2], one[3] = tie(y_here, states, both_k[0], both_k[1], one[2], one[3])
-    two[2], two[3] = across(pair_here[2], place.bits[1]), across(pair_here[3], place.bits[0])
+    y_here, states, one, two, both_k = tie(y_here, states, one, two, both_k)
+    state_in = hand_on(states[:, -1], True)
     both_k[2], both_k[3] = place.forward(2, one[2]), place.forward(3, one[3])
     pair_items = []
     for d in range(slots):
         pair_items += place.items(d, pair_here[d], one[d], two[d], both_k[d])
-    state_in = hand_on(states[:, -1], True)
-    y = y_here + wide_since * lax.dot_general(
-        c_low, state_in, (((2,), (1,)), ((0,), (0,))), preferred_element_type=f32
-    )
-
-    gate_in, wz = project(normed, at, pair_items, 0, channels)
-    mixed_grad, wo = project(cot, at, pair_items, 1, channels)
-    y = y.reshape((2 * length, channels))
-    sig = jax.nn.sigmoid(gate_in)
-    act = gate_in * sig
-    gated = y * act
-    scaled = mixed_grad * gain_row
-    sums = jnp.stack([jnp.sum(gated * gated, axis=1), jnp.sum(scaled * gated, axis=1)])
-    sums = sums.reshape((2, 2, length))
-    sums = (sums + swap(sums)[:, ::-1]).reshape((2, 2 * length))
-    gate_rms = lax.rsqrt(sums[0] / all_channels + epsilon)[:, None]
-    mixed = (gated * gate_rms * gain_row).astype(bf16)
-    gate_gain_part = jnp.sum(mixed_grad * gated * gate_rms, axis=0)
-    gated_grad = gate_rms * scaled - gated * gate_rms**3 * (sums[1] / all_channels)[:, None]
-    y_grad = (gated_grad * act).reshape((2, length, channels))
-    gate_grad = (gated_grad * y * sig * (1.0 + gate_in * (1.0 - sig))).astype(bf16)
-    state_grad = lax.dot_general(
-        c_low, (y_grad * wide_since).astype(bf16), (((1,), (1,)), ((0,), (0,))), preferred_element_type=f32
-    )
+    tokens = x_in.astype(f32)
+
+    gate_in, wz = project(normed_both, HALO, at, pair_items, 0, channels)
+    mixed_grad, wo = project(cot, 0, at, pair_items, 1, channels)
+    flat = lambda v: v.reshape((2 * length, -1))
+    y, sums = gate_sums(flat(y_here), flat(wide_since), flat(c_low), state_in, gate_in, mixed_grad, gain_row)
+    mixed, gate_grad, y_grad, gain_grad, state_grad = gate_grads(
+        y, flat(wide_since), flat(c_low), gate_in, mixed_grad, gain_row, sums, swap(sums), all_channels)
+    y_grad = y_grad.reshape((2, length, channels))
     state_grad = hand_on(state_grad, False)
     parts = [
         weight_parts(at, [normed_turned, cot_turned], [[gate_grad], [mixed]], group, own_rows, half_channels, flip)
         for flip, group in enumerate(groups)
     ]
-    parts, y_grad, mixed, gate_grad = tie(parts, y_grad, mixed, gate_grad)
+    parts, y_grad, mixed, gate_grad, state_grad = tie(parts, y_grad, mixed, gate_grad, state_grad)
     pair_came = [place.first_exchange(i, parts[i][1]) for i in range(2)]
 
     branch_other = swap(mmt(mixed[length:], wo).astype(bf16))
     branch = mmt(mixed[:length], wo)
     block_out = (tokens + branch + branch_other.astype(f32)).astype(bf16)
-    normed_grad_other = mmt(gate_grad[length:], wz)
-    normed_grad = mmt(gate_grad[:length], wz)
 
     def backward(piece):
         return scan_bwd(
@@ -1156,17 +1540,21 @@
         )
 
     back_other = backward(1)
-    pair_came, back_other, y_grad, block_out, normed_grad, normed_grad_other = tie(
-        pair_came, back_other, y_grad, block_out, normed_grad, normed_grad_other)
+    pair_came, back_other, y_grad, block_out = tie(pair_came, back_other, y_grad, block_out)
     terms = [place.second_term(parts[i][0], pair_came[i]) for i in range(2)]
     pair_last = [place.second_exchange(i, terms[i]) for i in range(2)]
     back_own = backward(0)
     dbc_other = swap(back_other[3][0])
-    pair_last, back_own, dbc_other, normed_grad, normed_grad_other = tie(
-        pair_last, back_own, dbc_other, normed_grad, normed_grad_other)
-    pair_own, pair_others = place.slot_sum([p[0] for p in parts], pair_came, pair_last, groups)
-
-    head = along_sequence(jnp.concatenate([back_own[2], back_other[2]]), pieces, False)
+    head_other = along_sequence(back_other[2], pieces, False)
+    pair_last, back_own, dbc_other, head_other = tie(pair_last, back_own, dbc_other, head_other)
+
+    head = jnp.concatenate([along_sequence(back_own[2], pieces, False), head_other])
+    pair_sums = place.slot_parts([p[0] for p in parts], pair_came, pair_last, groups)
+    pair_others = {1: around(pair_sums[1].astype(bf16), -1)}
+    place_back = (pick * first_lanes).T.astype(bf16)
+    bc_dpre, dt_low, bc_small, packed = small_grads(
+        back_own[3], dbc_other, bc_pre, bc_ext, flags, back_own[4], back_other[4], back_own[5], back_other[5],
+        log_step.reshape((2, length, 128)), dt_in, lanes, place_back, back_own[6], back_other[6], gain_grad)
 
     def past_end(begin, taps):
         total = jnp.zeros((begin.shape[0], HALO, begin.shape[2]), f32)
@@ -1180,59 +1568,43 @@
         lax.dynamic_update_slice(back[0][0], (back[1][0] + fix[i]).astype(bf16), (length - HALO, 0))
         for i, back in enumerate((back_own, back_other))
     ]
+    x_low, bc_dpre, dt_low, bc_small, packed = tie(x_low, bc_dpre, dt_low, bc_small, packed)
+    bc_head = along_sequence(bc_dpre[:8], pieces, False)
     x_parts = [
         weight_parts(at, [normed_turned], [x_low], group, own_rows, half_channels, flip)
         for flip, group in enumerate(groups)
     ]
+    x_parts, x_low, pair_others, pair_sums, bc_head, bc_dpre, dt_low = tie(
+        x_parts, x_low, pair_others, pair_sums, bc_head, bc_dpre, dt_low)
     x_came = [place.first_exchange(i, x_parts[i][1]) for i in range(2)]
-
-    bc_grad = back_own[3][0] + dbc_other
-    pre = bc_pre[0]
-    sig_bc = jax.nn.sigmoid(pre)
-    bc_dpre = bc_grad * (sig_bc * (1.0 + pre * (1.0 - sig_bc)))
-    bc_head = along_sequence(bc_dpre[:8], pieces, False)
-    bc_raw = conv_bc[0] * bc_dpre
-    bc_taps = [jnp.sum(bc_dpre * bc_ext[0, HALO:], axis=0)]
-    longer = jnp.concatenate([bc_dpre, bc_head], axis=0)
-    for k in range(1, conv_bc.shape[0]):
-        bc_raw = bc_raw + conv_bc[k] * longer[k : k + length] * flags[0, :, 3 + k : 4 + k]
-        shifted = bc_ext[0, HALO - k : HALO - k + length]
-        bc_taps.append(jnp.sum(bc_dpre * shifted * flags[0, :, k - 1 : k], axis=0))
-    bc_low = bc_raw.astype(bf16)
-    bc_small = jnp.stack(bc_taps + [jnp.sum(bc_dpre, axis=0)] + [jnp.zeros((bc_width,), f32)] * 11)
-    bc_small = bc_small + swap(bc_small)
-
-    dcol = jnp.concatenate([back_own[4], back_other[4]])
-    drow = jnp.concatenate([back_own[5], back_other[5]])
-    dcum = dcol[:, :, :128] - jnp.pad(drow.transpose(0, 2, 1), ((0, 0), (0, 0), (0, 96)))
-    dlog = jnp.einsum("ts,csh->cth", tri.T, dcum.reshape((2 * n_chunks, CH, 128)), precision=highest)
-    dstep = dcol[:, :, 128:] + dlog.reshape((2, length, 128)) * rate_lanes
-    dt_raw = (dstep * jax.nn.sigmoid(dt_in)).reshape((2 * length, 128))
-    rate_part = jnp.sum(dlog * log_step, axis=(0, 1))
-    place_back = (pick * first_lanes).T.astype(bf16)
-    dt_low = mm(dt_raw.astype(bf16), place_back).astype(bf16)
-    thin_low = jnp.concatenate(
-        [jnp.concatenate([bc_low, jnp.zeros_like(bc_low)], axis=0), dt_low], axis=1
-    )
-    thin_part = mm(normed_turned, thin_low).astype(bf16)
-
-    dcw = back_own[6][0] + back_other[6][0]
-    head_rows = jnp.stack([jnp.sum(dt_raw, axis=0), rate_part]) * first_lanes
-    head_rows = exact(head_rows, to_heads.T)
-    packed = jnp.concatenate(
-        [dcw[:5], gate_gain_part[None], dcw[5:6], head_rows, jnp.zeros((7, channels), f32)], axis=0
-    )
-    packed = place.sum_chips(jnp.concatenate([packed, bc_small], axis=1))
-
-    normed_grad_other = normed_grad_other + mmt(x_low[1], wx) + mmt(thin_low[length:], thin)
-    normed_grad_other = swap(normed_grad_other.astype(bf16))
-    normed_grad = normed_grad + mmt(x_low[0], wx) + mmt(thin_low[:length], thin)
-    thin_grad = place.scatter_rows(thin_part, True, low_bit=0)
-
-    x_came, packed, thin_grad, normed_grad_other, normed_grad, pair_own, pair_others = tie(
-        x_came, packed, thin_grad, normed_grad_other, normed_grad, pair_own, pair_others)
+    for d in range(2, slots - 1):
+        pair_others[d] = around(pair_sums[d].astype(bf16), -d)
+    normed_grad, normed_grad_other, thin_part = normed_grads(
+        bc_dpre, bc_head, flags, cbc, dt_low, normed_turned, x_low, gate_grad, wx, wz, thin)
+
+    x_came, thin_part, pair_others, pair_sums, normed_grad, normed_grad_other, packed, bc_small = tie(
+        x_came, thin_part, pair_others, pair_sums, normed_grad, normed_grad_other, packed, bc_small)
     x_terms = [place.second_term(x_parts[i][0], x_came[i]) for i in range(2)]
     x_last = [place.second_exchange(i, x_terms[i]) for i in range(2)]
+    pair_others[slots - 1] = around(pair_sums[slots - 1].astype(bf16), 1)
+    thin_part = place.ordered_sum(thin_part)
+    x_grad, gain_part = x_grads(normed_grad, swap(normed_grad_other), x_in, cotangent, gain)
+    gain_part = jnp.sum(gain_part, axis=0).reshape((-1, bc_width))
+    gain_rows = gain_part.shape[0]
+    bc_small = jnp.concatenate([bc_small[:5], gain_part, jnp.zeros((11 - gain_rows, bc_width), f32)], axis=0)
+    bc_small = bc_small + swap(bc_small)
+    packed = jnp.concatenate([packed, bc_small], axis=1)
+    low, high = place.bits
+    packed = packed + across(packed, low)
+    thin_part = place.half_rows(thin_part, low)
+
+    x_last, packed, thin_part, x_grad, pair_sums, pair_others = tie(
+        x_last, packed, thin_part, x_grad, pair_sums, pair_others)
+    x_sums = place.slot_parts([p[0] for p in x_parts], x_came, x_last, groups)
+    x_others = [around(x_sums[1].astype(bf16), -1)]
+    packed = packed + across(packed, high)
+    thin_grad = place.half_rows(thin_part, high)
+    packed, thin_grad, x_others, x_sums = tie(packed, thin_grad, x_others, x_sums)
 
     bc_small = packed[:, channels:]
     packed = packed[:, :channels].reshape((16, slots, half_channels))
@@ -1243,30 +1615,19 @@
     own_sums = jnp.concatenate([block(slot), bc_small], axis=1)
     for d in range(1, slots):
         own_sums = own_sums + around(jnp.concatenate([block(slot + d), bc_small], axis=1), d)
+    thin_grad = place.sum_slots(thin_grad)
+    own_sums, thin_grad, x_sums, x_others = tie(own_sums, thin_grad, x_sums, x_others)
+    x_others += [around(x_sums[d].astype(bf16), -d) for d in range(2, slots)]
     packed = own_sums[:, :half_channels]
     bc_small = own_sums[:, half_channels:]
     packed = place.ordered(0, packed, swap(packed), 1).reshape((16, slot_channels))
     by_head = packed[6:9].reshape((3, slot_heads, 64))
-
-    normed_grad = normed_grad + normed_grad_other.astype(f32)
-    gain_part = jnp.sum(normed_grad * tokens * inv_rms, axis=0)
-    pushed = normed_grad * gain
-    x_grad = (
-        cotangent.astype(f32)
-        + inv_rms * pushed
-        - tokens * inv_rms**3 * jnp.mean(pushed * tokens, axis=-1, keepdims=True)
-    )
-    gain_rows = gain_part.reshape((features // own_rows * 2, own_rows // 2))
-    gain_rows = place.scatter_rows(gain_rows, True, low_bit=0)
-    w_z_grad, w_out_grad = place.to_owner(pair_own, pair_others)
-
-    x_last, gain_rows, x_grad = tie(x_last, gain_rows, x_grad)
-    x_own, x_others = place.slot_sum([p[0] for p in x_parts], x_came, x_last, groups)
-    thin_grad = place.sum_slots(thin_grad)
+    norm_gain_grad = lax.dynamic_slice_in_dim(
+        bc_small[5 : 5 + gain_rows].reshape((features,)), lax.axis_index("dp") * own_rows, own_rows, 0)
+    w_z_grad, w_out_grad = place.to_owner(pair_sums[0], list(pair_others.values()))
     w_bc_grad = thin_grad[:, :bc_width]
     w_dt_grad = lax.dynamic_slice_in_dim(thin_grad, bc_width + slot * slot_heads, slot_heads, 1)
-    norm_gain_grad = place.sum_slots(gain_rows).reshape((own_rows,))
-    w_x_grad = place.to_owner(x_own, x_others)[0]
+    w_x_grad = place.to_owner(x_sums[0], x_others)[0]
     return (
         block_out,
         x_grad,

time: 762 us -> 565 us (0.74)
  local copies, waits for them, and re-layouts: 143 us -> 46 us
  Pallas kernels: 165 us -> 253 us
  other arithmetic: 120 us -> 32.3 us
  matrix products: 62.3 us -> 14.4 us
  starting transfers between devices: 119 us -> 91 us
  waiting for transfers between devices: 136 us -> 118 us
    pallas_call x3 -> x11, Pallas kernels: 34.8 us -> 123 us  [the longest x3 38.7 us: project(): pl.pallas_call(lambda *refs: project_body(places, skip, *refs), grid_spec...]
    ppermute x24 -> x21, waiting for transfers between devices: 69.4 us -> 31.2 us  [around(): lax.ppermute(value, 'tensor', [(i, (i + by) % size) for i in range(size)])]
    ppermute x42 -> x39, waiting for transfers between devices: 55 us -> 80.8 us  [across(): return lax.ppermute(value, 'dp', [(i, i ^ 1 << bit) for i in range(size)])]
    optimization_barrier x14 -> x2, local copies, waits for them, and re-layouts: 28.1 us -> 4.13 us  [tie(): return lax.optimization_barrier(values)]
    dot_general x9 -> x0, matrix products: 21.9 us -> none  [the longest x4 9.75 us: mm(): lax.dot_general(a, b, (((1,), (0,)), ((), ())), preferred_element_type=f32)]
    dot_general x8 -> x2, matrix products: 35.3 us -> 13.7 us  [mmt(): lax.dot_general(a, b, (((1,), (1,)), ((), ())), preferred_element_type=f32)]
    unnamed x328 -> x156, local copies, waits for them, and re-layouts: 33.4 us -> 12.6 us
    mul x3 -> x0, other arithmetic: 16 us -> none  [the longest x1 15.6 us: on_device_fast(): y_grad = (gated_grad * act).reshape((2, length, channels))]
  transfers between devices with their start and end apart: 84 -> 81, of which waited for: 17 -> 23; matrix products, arithmetic and copies ran while one was open for 34% -> 10% of each run, Pallas kernels for 19% -> 45%
where the time goes in v3:
time: 565 us; the launch traced here: 558 us
  Pallas kernels  253 us (45%)
  waiting for transfers between devices  118 us (21%)
  starting transfers between devices  91 us (16%)
  local copies, waits for them, and re-layouts  46 us (8%)
  other arithmetic  32.3 us (6%)
  matrix products  14.4 us (3%)
    ppermute x39, waiting for transfers between devices, across(): return lax.ppermute(value, 'dp', [(i, i ^ 1 << bit) for i in range(size)])  80.8 us
    pallas_call x2, Pallas kernels, scan_bwd(): pl.pallas_call(lambda *refs: scan_bwd_body(n_chunks, rows, *refs), grid=(...  64.2 us
    ppermute x21, starting transfers between devices, around(): lax.ppermute(value, 'tensor', [(i, (i + by) % size) for i in range(size)])  40.6 us
    ppermute x39, starting transfers between devices, across(): return lax.ppermute(value, 'dp', [(i, i ^ 1 << bit) for i in range(size)])  39.2 us
    pallas_call x4, Pallas kernels, weight_parts(): pl.pallas_call(lambda *refs: weight_parts_body(count, group, flip, *refs)...  38.8 us
    pallas_call x3, Pallas kernels, project(): pl.pallas_call(lambda *refs: project_body(places, skip, *refs), grid_spec...  38.7 us
    ppermute x21, waiting for transfers between devices, around(): lax.ppermute(value, 'tensor', [(i, (i + by) % size) for i in range(size)])  31.2 us
    pallas_call x1, Pallas kernels, scan_fwd(): pl.pallas_call(lambda *refs: scan_fwd_body(n_chunks, rows, *refs), grid=(...  26.9 us
  transfers between devices with their start and end apart: 81, of which 23 were waited for; matrix products, arithmetic and copies ran while one was open for 10% of the time, Pallas kernels for 45%

profile of v3, /device:TPU:0, one launch (start us, length us, event | category | flops | bytes accessed | tf_op | source)
XLA Modules:
  0.0 557.8 jit_solution(16386841885191238928)
XLA Ops:
  46.2 11.5 %collective-permute-done.13 = bf16[2,2,192,384]{3,2,1,0:T(8,128)(2,1)S(1)} collective-permute-done((bf16[2,2,192,384]{3,2,1,0:T(8,128)(2,1)S(1)}, bf16[2,2,192,384]{3,2,1,0:T(8,128)(2,1)S(1)}, u32[]{:S(2)}, u32[]{:S(2)}) %collective-permute-start.13) | collective-permute-done | bytes 589856 | tf_op jit(solution)/shard_map/ppermute | solution.py:862
  74.4 6.3 %collective-permute-done.19.refs_12_ = bf16[1,384,384]{2,1,0:T(8,128)(2,1)S(1)} collective-permute-done((bf16[1,384,384]{2,1,0:T(8,128)(2,1)}, bf16[1,384,384]{2,1,0:T(8,128)(2,1)S(1)}, u32[]{:S(2)}, u32[]{:S(2)}) %collective-permute-start.19) | collective-permute-done | bytes 294944 | tf_op jit(solution)/shard_map/ppermute | solution.py:862
  90.8 12.5 %prepare.1 = (f32[2,528,256]{2,1,0:T(8,128)}, f32[2,512,256]{2,1,0:T(8,128)}, f32[2,512,256]{2,1,0:T(8,128)}, bf16[2,256,512]{2,1,0:T(8,128)(2,1)}, bf16[2,512,1...) custom-call(bf16[528,1536]{1,0:T(8,128)(2,1)} %get-tuple-element.354, ...), custom_call_target="tpu_custom_call" | custom-call | flops 1 | bytes 1 | tf_op jit(solution)/shard_map/prepare/pallas_call | solution.py:521
  119.5 13.1 %project.3 = (f32[1056,1536]{1,0:T(8,128)}, bf16[1536,1536]{1,0:T(8,128)(2,1)}) custom-call(s32[8]{0:T(128)} %stack.38.refs_0_, bf16[528,1536]{1,0:T(8,128)(2,1)} %get-tuple-element.354.own_ref.refs_1_, bf16[528,1536]{1,0:T(8,128)(2,1)} %collective-permute-done.16.other_ref.refs_2_, bf16[1,384,384]{2,1,0:T(8,128)(2,1)} %slice.237.refs_3_, ...), custom_call_target="tpu_custom_call" | custom-call | flops 4982833152 | bytes 19169280 | tf_op jit(solution)/shard_map/project/pallas_call | solution.py:350
  132.6 7.4 %collective-permute-done.32.refs_12_ = bf16[2,384,384]{2,1,0:T(8,128)(2,1)} collective-permute-done((bf16[2,384,384]{2,1,0:T(8,128)(2,1)}, bf16[2,384,384]{2,1,0:T(8,128)(2,1)}, u32[]{:S(2)}, u32[]{:S(2)}) %collective-permute-start.32) | collective-permute-done | bytes 589856 | tf_op jit(solution)/shard_map/ppermute | solution.py:862
  144.2 26.9 %scan_fwd.1 = (f32[2,512,1536]{2,1,0:T(8,128)}, f32[2,2,128,1536]{3,2,1,0:T(8,128)}) custom-call(f32[2,512,128]{2,1,0:T(8,128)} %get-tuple-element.348.refs_0_, f32[2,512,8]{2,1,0:T(8,128)} %get-tuple-element.349.refs_1_.flags_ref, f32[2,32,512]{2,1,0:T(8,128)} %get-tuple-element.350.refs_2_, f32[2,8,1536]{2,1,0:T(8,128)} %get-tuple-element.351.refs_3_, ...), custom_call_target="tpu_custom_call" | custom-call | flops 3221225472 | bytes 12582912 | tf_op jit(solution)/shard_map/scan_fwd/pallas_call | solution.py:116
  176.6 11.0 %collective-permute-done.41.refs_14_ = bf16[2,384,384]{2,1,0:T(8,128)(2,1)S(1)} collective-permute-done((bf16[2,384,384]{2,1,0:T(8,128)(2,1)}, bf16[2,384,384]{2,1,0:T(8,128)(2,1)S(1)}, u32[]{:S(2)}, u32[]{:S(2)}) %collective-permute-start.41) | collective-permute-done | bytes 589856 | tf_op jit(solution)/shard_map/ppermute | solution.py:862
  190.0 12.7 %project.4 = (f32[1024,1536]{1,0:T(8,128)}, bf16[1536,1536]{1,0:T(8,128)(2,1)}) custom-call(s32[8]{0:T(128)} %stack.38.refs_0_, bf16[528,1536]{1,0:T(8,128)(2,1)} %get-tuple-element.354.own_ref.refs_1_, bf16[528,1536]{1,0:T(8,128)(2,1)} %collective-permute-done.16.other_ref.refs_2_, bf16[2,384,384]{2,1,0:T(8,128)(2,1)} %copy-done.18, ...), custom_call_target="tpu_custom_call" | custom-call | flops 4831838208 | bytes 18874368 | tf_op jit(solution)/shard_map/project/pallas_call | solution.py:350
  202.7 12.8 %project.5 = (f32[1024,1536]{1,0:T(8,128)}, bf16[1536,1536]{1,0:T(8,128)(2,1)}) custom-call(s32[8]{0:T(128)} %stack.38.refs_0_, bf16[512,1536]{1,0:T(8,128)(2,1)} %cot_ref, bf16[512,1536]{1,0:T(8,128)(2,1)} %collective-permute-done.43.refs_2_, bf16[2,384,384]{2,1,0:T(8,128)(2,1)} %copy-done.18, bf16[2,384,384]{2,1,0:T(8,128)(2,1)} %copy-done.51, ...), custom_call_target="tpu_custom_call" | custom-call | flops 4831838208 | bytes 18874368 | tf_op jit(solution)/shard_map/project/pallas_call | solution.py:350
  216.5 12.9 %gate_sums.1 = (f32[1024,1536]{1,0:T(8,128)}, f32[1024,128]{1,0:T(8,128)}) custom-call(f32[1024,1536]{1,0:T(8,128)} %bitcast.174, bf16[1024,1536]{1,0:T(8,128)(2,1)} %bitcast.169, bf16[1024,128]{1,0:T(8,128)(2,1)} %bitcast.186, bf16[2,128,1536]{2,1,0:T(8,128)(2,1)} %copy-done, f32[1024,1536]{1,0:T(8,128)} %get-tuple-element.406.gate_ref.refs_3_, ...), custom_call_target="tpu_custom_call" | custom-call | flops 1 | bytes 1 | tf_op jit(solution)/shard_map/gate_sums/pallas_call | solution.py:553
  232.2 17.3 %gate_grads.1 = (bf16[1024,1536]{1,0:T(8,128)(2,1)}, bf16[1024,1536]{1,0:T(8,128)(2,1)}, f32[1024,1536]{1,0:T(8,128)}, f32[8,1536]{1,0:T(8,128)}, f32[2,128,1536]{2,1,0:T(8,128)}) custom-call(f32[1024,1536]{1,0:T(8,128)} %get-tuple-element.409.refs_0_, bf16[1024,1536]{1,0:T(8,128)(2,1)} %bitcast.170, bf16[1024,128]{1,0:T(8,128)(2,1)} %bitcast.187, ...), custom_call_target="tpu_custom_call" | custom-call | flops 1 | bytes 1 | tf_op jit(solution)/shard_map/gate_grads/pallas_call | solution.py:615
  252.9 12.2 %weight_parts.5 = (bf16[2,2,2,384,384]{4,3,2,1,0:T(8,128)(2,1)}, bf16[2,2,2,384,384]{4,3,2,1,0:T(8,128)(2,1)}) custom-call(s32[8]{0:T(128)} %stack.38.refs_0_, bf16[1536,512]{1,0:T(8,128)(2,1)} %get-tuple-element.315.refs_1_.own_turned_ref, bf16[1536,512]{1,0:T(8,128)(2,1)} %collective-permute-done.22.refs_2_.other_turned_ref, ...), custom_call_target="tpu_custom_call" | custom-call | flops 4831838208 | bytes 9437184 | tf_op jit(solution)/shard_map/weight_parts/pallas_call | solution.py:837
  265.0 12.2 %weight_parts.4 = (bf16[2,2,2,384,384]{4,3,2,1,0:T(8,128)(2,1)}, bf16[2,2,2,384,384]{4,3,2,1,0:T(8,128)(2,1)}) custom-call(s32[8]{0:T(128)} %stack.38.refs_0_, bf16[1536,512]{1,0:T(8,128)(2,1)} %get-tuple-element.315.refs_1_.own_turned_ref, bf16[1536,512]{1,0:T(8,128)(2,1)} %collective-permute-done.22.refs_2_.other_turned_ref, ...), custom_call_target="tpu_custom_call" | custom-call | flops 4831838208 | bytes 9437184 | tf_op jit(solution)/shard_map/weight_parts/pallas_call | solution.py:837
  277.2 6.9 %convolution_convert_fusion = bf16[512,1536]{1,0:T(8,128)(2,1)} fusion(bf16[1536,1536]{1,0:T(8,128)(2,1)} %get-tuple-element.431, bf16[1024,1536]{1,0:T(8,128)(2,1)} %get-tuple-element.430.refs_6_), kind=kOutput, calls=%fused_computation.3 | convolution fusion | flops 2416705536 | bytes 7864320 | tf_op jit(solution)/shard_map/dot_general | solution.py:23
  289.7 32.1 %scan_bwd.2 = (bf16[1,512,1536]{2,1,0:T(8,128)(2,1)}, f32[1,16,1536]{2,1,0:T(8,128)}, f32[1,8,1536]{2,1,0:T(8,128)}, f32[1,512,256]{2,1,0:T(8,128)}, f32[1,512,2...) custom-call(f32[2,512,128]{2,1,0:T(8,128)} %get-tuple-element.348.refs_0_, ...), custom_call_target="tpu_custom_call" | custom-call | flops 4831838208 | bytes 9437184 | tf_op jit(solution)/shard_map/scan_bwd/pallas_call | solution.py:278
  321.9 6.8 %fusion.1 = bf16[512,1536]{1,0:T(8,128)(2,1)} fusion(bf16[512,1536]{1,0:T(8,128)(2,1)S(1)} %collective-permute-done.48, bf16[1536,1536]{1,0:T(8,128)(2,1)} %get-tuple-element.431, bf16[512,1536]{1,0:T(8,128)(2,1)S(1)} %copy-done.1, bf16[1024,1536]{1,0:T(8,128)(2,1)} %get-tuple-element.430.refs_6_), kind=kOutput, calls=%fused_computation.2 | convolution fusion | flops 2419851264 | bytes 11010048 | tf_op jit(solution)/shard_map/dot_general | solution.py:23
  328.7 11.1 %collective-permute-done.46 = bf16[2,2,2,384,384]{4,3,0,1,2:T(8,128)(2,1)} collective-permute-done((bf16[2,2,2,384,384]{4,3,0,1,2:T(8,128)(2,1)}, bf16[2,2,2,384,384]{4,3,0,1,2:T(8,128)(2,1)}, u32[]{:S(2)}, u32[]{:S(2)}) %collective-permute-start.46) | collective-permute-done | bytes 2359328 | tf_op jit(solution)/shard_map/ppermute | solution.py:862
  353.1 32.1 %scan_bwd.3 = (bf16[1,512,1536]{2,1,0:T(8,128)(2,1)}, f32[1,16,1536]{2,1,0:T(8,128)}, f32[1,8,1536]{2,1,0:T(8,128)}, f32[1,512,256]{2,1,0:T(8,128)}, f32[1,512,2...) custom-call(f32[2,512,128]{2,1,0:T(8,128)} %get-tuple-element.348.refs_0_, ...), custom_call_target="tpu_custom_call" | custom-call | flops 4831838208 | bytes 9437184 | tf_op jit(solution)/shard_map/scan_bwd/pallas_call | solution.py:278
  393.4 6.2 %collective-permute-start.54 = (bf16[2,384,384]{2,1,0:T(8,128)(2,1)S(1)}, bf16[2,384,384]{2,1,0:T(8,128)(2,1)S(1)}, u32[]{:S(2)}, u32[]{:S(2)}) collective-permute-start(bf16[2,384,384]{2,1,0:T(8,128)(2,1)S(1)} %get-tuple-element.616), channel_id=1, source_target_pairs={{0,3},{1,0},{2,1},{3,2},{4,7},{5,4},{6,5},{7,6},{8,11},{9,8},{10,9... | collective-permute-start | bytes 1769480 | tf_op jit(solution)/shard_map/ppermute | solution.py:868
  409.7 7.2 %weight_parts.7 = (bf16[1,2,2,384,384]{4,3,2,1,0:T(8,128)(2,1)}, bf16[1,2,2,384,384]{4,3,2,1,0:T(8,128)(2,1)}) custom-call(s32[8]{0:T(128)} %stack.38.refs_0_, bf16[1536,512]{1,0:T(8,128)(2,1)} %get-tuple-element.315.refs_1_.own_turned_ref, bf16[1536,512]{1,0:T(8,128)(2,1)} %collective-permute-done.22.refs_2_.other_turned_ref, ...), custom_call_target="tpu_custom_call" | custom-call | flops 2415919104 | bytes 4718592 | tf_op jit(solution)/shard_map/weight_parts/pallas_call | solution.py:837
  416.9 7.2 %weight_parts.6 = (bf16[1,2,2,384,384]{4,3,2,1,0:T(8,128)(2,1)}, bf16[1,2,2,384,384]{4,3,2,1,0:T(8,128)(2,1)}) custom-call(s32[8]{0:T(128)} %stack.38.refs_0_, bf16[1536,512]{1,0:T(8,128)(2,1)} %get-tuple-element.315.refs_1_.own_turned_ref, bf16[1536,512]{1,0:T(8,128)(2,1)} %collective-permute-done.22.refs_2_.other_turned_ref, ...), custom_call_target="tpu_custom_call" | custom-call | flops 2415919104 | bytes 4718592 | tf_op jit(solution)/shard_map/weight_parts/pallas_call | solution.py:837
  428.7 22.7 %normed_grads.1 = (f32[512,1536]{1,0:T(8,128)}, bf16[512,1536]{1,0:T(8,128)(2,1)}, bf16[1536,384]{1,0:T(8,128)(2,1)}) custom-call(f32[512,256]{1,0:T(8,128)} %get-tuple-element.483.dpre_ref, f32[8,256]{1,0:T(8,128)} %copy-done.70, f32[2,512,8]{2,1,0:T(8,128)} %get-tuple-element.349.refs_1_.flags_ref, f32[8,256]{1,0:T(8,128)} %maximum_maximum_fusion.2.cbc_ref, ...), custom_call_target="tpu_custom_call" | custom-call | flops 9663676416 | bytes 18874368 | tf_op jit(solution)/shard_map/normed_grads/pallas_call | solution.py:741
  479.6 9.0 %collective-permute-done.65 = bf16[2,192,384]{2,1,0:T(8,128)(2,1)S(1)} collective-permute-done((bf16[2,192,384]{2,1,0:T(8,128)(2,1)S(1)}, bf16[2,192,384]{2,1,0:T(8,128)(2,1)S(1)}, u32[]{:S(2)}, u32[]{:S(2)}) %collective-permute-start.65) | collective-permute-done | bytes 294944 | tf_op jit(solution)/shard_map/ppermute | solution.py:862
  537.5 12.4 %collective-permute-done.76 = bf16[1,384,384]{2,1,0:T(8,128)(2,1)} collective-permute-done((bf16[1,384,384]{2,1,0:T(8,128)(2,1)S(1)}, bf16[1,384,384]{2,1,0:T(8,128)(2,1)}, u32[]{:S(2)}, u32[]{:S(2)}) %collective-permute-start.76) | collective-permute-done | bytes 294944 | tf_op jit(solution)/shard_map/ppermute | solution.py:868
  (464 shorter events, 232.5 us)
Async XLA Ops:
  82.8 29.4 %collective-permute-start.24 = (bf16[2,384,384]{2,1,0:T(8,128)(2,1)S(1)}, bf16[2,384,384]{2,1,0:T(8,128)(2,1)S(1)}, u32[]{:S(2)}, u32[]{:S(2)}) collective-permute-start(bf16[2,384,384]{2,1,0:T(8,128)(2,1)S(1)} %slice.240.refs_3_), channel_id=1, source_target_pairs={{0,8},{4,12},{8,0},{12,4},{16,24},{20,28},{24,16},{28,20},{1,9},{5... | collective-permute-start | bytes 1769480 | tf_op jit(solution)/shard_map/ppermute | solution.py:862
  82.9 29.3 %collective-permute-start.25 = (bf16[2,384,384]{2,1,0:T(8,128)(2,1)S(1)}, bf16[2,384,384]{2,1,0:T(8,128)(2,1)S(1)}, u32[]{:S(2)}, u32[]{:S(2)}) collective-permute-start(bf16[2,384,384]{2,1,0:T(8,128)(2,1)S(1)} %slice.240.refs_3_), channel_id=1, source_target_pairs={{0,16},{4,20},{8,24},{12,28},{16,0},{20,4},{24,8},{28,12},{1,17},{... | collective-permute-start | bytes 1769480 | tf_op jit(solution)/shard_map/ppermute | solution.py:862
  84.5 27.6 %collective-permute-start.26 = (bf16[2,384,384]{2,1,0:T(8,128)(2,1)S(1)}, bf16[2,384,384]{2,1,0:T(8,128)(2,1)}, u32[]{:S(2)}, u32[]{:S(2)}) collective-permute-start(bf16[2,384,384]{2,1,0:T(8,128)(2,1)S(1)} %slice.240.refs_3_), channel_id=1, source_target_pairs={{0,2},{1,3},{2,0},{3,1},{4,6},{5,7},{6,4},{7,5},{8,10},{9,11},{10,... | collective-permute-start | bytes 1769480 | tf_op jit(solution)/shard_map/ppermute | solution.py:868
  112.9 27.2 %collective-permute-start.33 = (bf16[2,384,384]{2,1,0:T(8,128)(2,1)}, bf16[2,384,384]{2,1,0:T(8,128)(2,1)}, u32[]{:S(2)}, u32[]{:S(2)}) collective-permute-start(bf16[2,384,384]{2,1,0:T(8,128)(2,1)} %collective-permute-done.17.refs_7_), channel_id=1, source_target_pairs={{0,8},{4,12},{8,0},{12,4},{16,24},{20,28},{24,16},{28,20},{1,9},{5... | collective-permute-start | bytes 1769480 | tf_op jit(solution)/shard_map/ppermute | solution.py:862
  140.1 31.0 %collective-permute-start.36 = (bf16[2,384,384]{2,1,0:T(8,128)(2,1)}, bf16[2,384,384]{2,1,0:T(8,128)(2,1)}, u32[]{:S(2)}, u32[]{:S(2)}) collective-permute-start(bf16[2,384,384]{2,1,0:T(8,128)(2,1)} %collective-permute-done.35.refs_15_), channel_id=1, source_target_pairs={{0,16},{4,20},{8,24},{12,28},{16,0},{20,4},{24,8},{28,12},{1,17},{... | collective-permute-start | bytes 1769480 | tf_op jit(solution)/shard_map/ppermute | solution.py:862
  141.7 29.9 %collective-permute-start.37 = (bf16[2,384,384]{2,1,0:T(8,128)(2,1)}, bf16[2,384,384]{2,1,0:T(8,128)(2,1)S(1)}, u32[]{:S(2)}, u32[]{:S(2)}) collective-permute-start(bf16[2,384,384]{2,1,0:T(8,128)(2,1)} %collective-permute-done.26.refs_11_), channel_id=1, source_target_pairs={{0,16},{4,20},{8,24},{12,28},{16,0},{20,4},{24,8},{28,12},{1,17},{... | collective-permute-start | bytes 1769480 | tf_op jit(solution)/shard_map/ppermute | solution.py:862
  142.1 29.6 %collective-permute-start.38 = (bf16[2,384,384]{2,1,0:T(8,128)(2,1)}, bf16[2,384,384]{2,1,0:T(8,128)(2,1)S(1)}, u32[]{:S(2)}, u32[]{:S(2)}) collective-permute-start(bf16[2,384,384]{2,1,0:T(8,128)(2,1)} %collective-permute-done.35.refs_15_), channel_id=1, source_target_pairs={{0,8},{4,12},{8,0},{12,4},{16,24},{20,28},{24,16},{28,20},{1,9},{5... | collective-permute-start | bytes 1769480 | tf_op jit(solution)/shard_map/ppermute | solution.py:862
  143.8 27.9 %collective-permute-start.39 = (bf16[2,384,384]{2,1,0:T(8,128)(2,1)}, bf16[2,384,384]{2,1,0:T(8,128)(2,1)S(1)}, u32[]{:S(2)}, u32[]{:S(2)}) collective-permute-start(bf16[2,384,384]{2,1,0:T(8,128)(2,1)} %collective-permute-done.31.refs_9_), channel_id=1, source_target_pairs={{0,8},{4,12},{8,0},{12,4},{16,24},{20,28},{24,16},{28,20},{1,9},{5... | collective-permute-start | bytes 1769480 | tf_op jit(solution)/shard_map/ppermute | solution.py:862
  144.2 58.5 %collective-permute-start.43 = (bf16[512,1536]{1,0:T(8,128)(2,1)S(1)}, bf16[512,1536]{1,0:T(8,128)(2,1)}, u32[]{:S(2)}, u32[]{:S(2)}) collective-permute-start(bf16[512,1536]{1,0:T(8,128)(2,1)S(1)} %copy-done.3), channel_id=1, source_target_pairs={{0,4},{4,0},{8,12},{12,8},{16,20},{20,16},{24,28},{28,24},{1,5},{5... | collective-permute-start | bytes 4718600 | tf_op jit(solution)/shard_map/ppermute | solution.py:857
  171.1 81.8 %collective-permute-start.23 = (bf16[1536,512]{1,0:T(8,128)(2,1)}, bf16[1536,512]{1,0:T(8,128)(2,1)}, u32[]{:S(2)}, u32[]{:S(2)}) collective-permute-start(bf16[1536,512]{1,0:T(8,128)(2,1)} %turn.1.refs_3_), channel_id=1, source_target_pairs={{0,4},{4,0},{8,12},{12,8},{16,20},{20,16},{24,28},{28,24},{1,5},{5... | collective-permute-start | bytes 4718600 | tf_op jit(solution)/shard_map/ppermute | solution.py:857
  171.6 81.2 %collective-permute-start.22 = (bf16[1536,512]{1,0:T(8,128)(2,1)}, bf16[1536,512]{1,0:T(8,128)(2,1)}, u32[]{:S(2)}, u32[]{:S(2)}) collective-permute-start(bf16[1536,512]{1,0:T(8,128)(2,1)} %get-tuple-element.315.refs_1_.own_turned_ref), channel_id=1, source_target_pairs={{0,4},{4,0},{8,12},{12,8},{16,20},{20,16},{24,28},{28,24},{1,5},{5... | collective-permute-start | bytes 4718600 | tf_op jit(solution)/shard_map/ppermute | solution.py:857
  187.7 27.9 %collective-permute-start.40 = (bf16[2,128,1536]{2,1,0:T(8,128)(2,1)S(1)}, bf16[2,128,1536]{2,1,0:T(8,128)(2,1)S(1)}, u32[]{:S(2)}, u32[]{:S(2)}) collective-permute-start(bf16[2,128,1536]{2,1,0:T(8,128)(2,1)S(1)} %fusion.7), channel_id=1, source_target_pairs={{0,1},{2,3},{4,5},{6,7},{8,9},{10,11},{12,13},{14,15},{16,17},{18,... | collective-permute-start | bytes 2359304 | tf_op jit(solution)/shard_map/ppermute | solution.py:876
  284.2 37.7 %collective-permute-start.48 = (bf16[512,1536]{1,0:T(8,128)(2,1)}, bf16[512,1536]{1,0:T(8,128)(2,1)S(1)}, u32[]{:S(2)}, u32[]{:S(2)}) collective-permute-start(bf16[512,1536]{1,0:T(8,128)(2,1)} %convolution_convert_fusion), channel_id=1, source_target_pairs={{0,4},{4,0},{8,12},{12,8},{16,20},{20,16},{24,28},{28,24},{1,5},{5... | collective-permute-start | bytes 4718600 | tf_op jit(solution)/shard_map/ppermute | solution.py:857
  286.0 53.8 %collective-permute-start.46 = (bf16[2,2,2,384,384]{4,3,0,1,2:T(8,128)(2,1)}, bf16[2,2,2,384,384]{4,3,0,1,2:T(8,128)(2,1)}, u32[]{:S(2)}, u32[]{:S(2)}) collective-permute-start(bf16[2,2,2,384,384]{4,3,0,1,2:T(8,128)(2,1)} %copy.100), channel_id=1, source_target_pairs={{0,16},{4,20},{8,24},{12,28},{16,0},{20,4},{24,8},{28,12},{1,17},{... | collective-permute-start | bytes 7077896 | tf_op jit(solution)/shard_map/ppermute | solution.py:862
  287.1 53.6 %collective-permute-start.47 = (bf16[2,2,2,384,384]{4,3,2,1,0:T(8,128)(2,1)}, bf16[2,2,2,384,384]{4,3,2,1,0:T(8,128)(2,1)}, u32[]{:S(2)}, u32[]{:S(2)}) collective-permute-start(bf16[2,2,2,384,384]{4,3,2,1,0:T(8,128)(2,1)} %get-tuple-element.420), channel_id=1, source_target_pairs={{0,8},{4,12},{8,0},{12,4},{16,24},{20,28},{24,16},{28,20},{1,9},{5... | collective-permute-start | bytes 7077896 | tf_op jit(solution)/shard_map/ppermute | solution.py:862
  342.4 42.8 %collective-permute-start.50 = (bf16[2,2,384,384]{3,2,1,0:T(8,128)(2,1)S(1)}, bf16[2,2,384,384]{3,2,1,0:T(8,128)(2,1)}, u32[]{:S(2)}, u32[]{:S(2)}) collective-permute-start(bf16[2,2,384,384]{3,2,1,0:T(8,128)(2,1)S(1)} %fusion.5), channel_id=1, source_target_pairs={{0,16},{4,20},{8,24},{12,28},{16,0},{20,4},{24,8},{28,12},{1,17},{... | collective-permute-start | bytes 3538952 | tf_op jit(solution)/shard_map/ppermute | solution.py:862
  346.0 39.2 %collective-permute-start.49 = (bf16[2,2,384,384]{3,2,0,1:T(8,128)(2,1)}, bf16[2,2,384,384]{3,2,0,1:T(8,128)(2,1)}, u32[]{:S(2)}, u32[]{:S(2)}) collective-permute-start(bf16[2,2,384,384]{3,2,0,1:T(8,128)(2,1)} %fusion.4), channel_id=1, source_target_pairs={{0,8},{4,12},{8,0},{12,4},{16,24},{20,28},{24,16},{28,20},{1,9},{5... | collective-permute-start | bytes 3538952 | tf_op jit(solution)/shard_map/ppermute | solution.py:862
  350.2 35.0 %collective-permute-start.51 = (f32[512,256]{1,0:T(8,128)}, f32[512,256]{1,0:T(8,128)}, u32[]{:S(2)}, u32[]{:S(2)}) collective-permute-start(f32[512,256]{1,0:T(8,128)} %bitcast.215), channel_id=1, source_target_pairs={{0,4},{4,0},{8,12},{12,8},{16,20},{20,16},{24,28},{28,24},{1,5},{5... | collective-permute-start | bytes 1572872 | tf_op jit(solution)/shard_map/ppermute | solution.py:857
  351.8 33.4 %collective-permute-start.52 = (f32[1,8,1536]{2,1,0:T(8,128)}, f32[1,8,1536]{2,1,0:T(8,128)}, u32[]{:S(2)}, u32[]{:S(2)}) collective-permute-start(f32[1,8,1536]{2,1,0:T(8,128)} %get-tuple-element.446), channel_id=1, source_target_pairs={{1,0},{3,2},{5,4},{7,6},{9,8},{11,10},{13,12},{15,14},{17,16},{19,... | collective-permute-start | bytes 147464 | tf_op jit(solution)/shard_map/ppermute | solution.py:876
  393.4 30.6 %collective-permute-start.54 = (bf16[2,384,384]{2,1,0:T(8,128)(2,1)S(1)}, bf16[2,384,384]{2,1,0:T(8,128)(2,1)S(1)}, u32[]{:S(2)}, u32[]{:S(2)}) collective-permute-start(bf16[2,384,384]{2,1,0:T(8,128)(2,1)S(1)} %get-tuple-element.616), channel_id=1, source_target_pairs={{0,3},{1,0},{2,1},{3,2},{4,7},{5,4},{6,5},{7,6},{8,11},{9,8},{10,9... | collective-permute-start | bytes 1769480 | tf_op jit(solution)/shard_map/ppermute | solution.py:868
  427.1 30.3 %collective-permute-start.56 = (bf16[1,2,2,384,384]{4,3,1,2,0:T(8,128)(2,1)}, bf16[1,2,2,384,384]{4,3,1,2,0:T(8,128)(2,1)S(1)}, u32[]{:S(2)}, u32[]{:S(2)}) collective-permute-start(bf16[1,2,2,384,384]{4,3,1,2,0:T(8,128)(2,1)} %copy.107), channel_id=1, source_target_pairs={{0,16},{4,20},{8,24},{12,28},{16,0},{20,4},{24,8},{28,12},{1,17},{... | collective-permute-start | bytes 3538952 | tf_op jit(solution)/shard_map/ppermute | solution.py:862
  428.1 29.3 %collective-permute-start.57 = (bf16[1,2,2,384,384]{4,3,2,1,0:T(8,128)(2,1)}, bf16[1,2,2,384,384]{4,3,2,1,0:T(8,128)(2,1)S(1)}, u32[]{:S(2)}, u32[]{:S(2)}) collective-permute-start(bf16[1,2,2,384,384]{4,3,2,1,0:T(8,128)(2,1)} %get-tuple-element.482), channel_id=1, source_target_pairs={{0,8},{4,12},{8,0},{12,4},{16,24},{20,28},{24,16},{28,20},{1,9},{5... | collective-permute-start | bytes 3538952 | tf_op jit(solution)/shard_map/ppermute | solution.py:862
  428.7 28.8 %collective-permute-start.58 = (bf16[2,384,384]{2,1,0:T(8,128)(2,1)}, bf16[2,384,384]{2,1,0:T(8,128)(2,1)}, u32[]{:S(2)}, u32[]{:S(2)}) collective-permute-start(bf16[2,384,384]{2,1,0:T(8,128)(2,1)} %slice_bitcast_fusion.1), channel_id=1, source_target_pairs={{0,2},{1,3},{2,0},{3,1},{4,6},{5,7},{6,4},{7,5},{8,10},{9,11},{10,... | collective-permute-start | bytes 1769480 | tf_op jit(solution)/shard_map/ppermute | solution.py:868
  463.0 27.1 %collective-permute-start.60 = (bf16[1,2,384,384]{3,2,1,0:T(8,128)(2,1)}, bf16[1,2,384,384]{3,2,1,0:T(8,128)(2,1)}, u32[]{:S(2)}, u32[]{:S(2)}) collective-permute-start(bf16[1,2,384,384]{3,2,1,0:T(8,128)(2,1)} %fusion.11), channel_id=1, source_target_pairs={{0,16},{4,20},{8,24},{12,28},{16,0},{20,4},{24,8},{28,12},{1,17},{... | collective-permute-start | bytes 1769480 | tf_op jit(solution)/shard_map/ppermute | solution.py:862
  (128 other events, 1391.3 us)

commit v4 on v3

--- a/solution.py
+++ b/solution.py
@@ -761,6 +761,41 @@
     )(dpre, head, flags, cbc, dt_low, *turned, *x_low, gate_grad, wx, wz, thin)
 
 
+def branch_body(mixed_ref, weight_ref, own_ref, other_ref):
+    part = mmt(mixed_ref[...], weight_ref[...])
+
+    @pl.when(pl.program_id(0) == 0)
+    def _():
+        other_ref[...] = part.astype(bf16)
+
+    @pl.when(pl.program_id(0) == 1)
+    def _():
+        own_ref[...] = part
+
+
+def branch_parts(mixed, weight):
+    tokens, channels = mixed.shape
+    features = weight.shape[0]
+    half = pl.BlockSpec((tokens // 2, features), lambda p: (0, 0))
+    return pl.pallas_call(
+        branch_body,
+        grid=(2,),
+        in_specs=[
+            pl.BlockSpec((tokens // 2, channels), lambda p: (1 - p, 0)),
+            pl.BlockSpec(weight.shape, lambda p: (0, 0), pipeline_mode=pl.Buffered(1)),
+        ],
+        out_specs=[half, half],
+        out_shape=[
+            jax.ShapeDtypeStruct((tokens // 2, features), f32),
+            jax.ShapeDtypeStruct((tokens // 2, features), bf16),
+        ],
+        cost_estimate=pl.CostEstimate(
+            flops=2 * tokens * channels * features, transcendentals=0, bytes_accessed=4 * features * channels
+        ),
+        name="branch_parts",
+    )(mixed, weight)
+
+
 def x_grads_body(own_ref, came_ref, x_ref, cot_ref, gain_ref, out_ref, gain_grad_ref):
     grad = own_ref[...] + came_ref[...].astype(f32)
     x = x_ref[...].astype(f32)
@@ -1530,9 +1565,6 @@
     parts, y_grad, mixed, gate_grad, state_grad = tie(parts, y_grad, mixed, gate_grad, state_grad)
     pair_came = [place.first_exchange(i, parts[i][1]) for i in range(2)]
 
-    branch_other = swap(mmt(mixed[length:], wo).astype(bf16))
-    branch = mmt(mixed[:length], wo)
-    block_out = (tokens + branch + branch_other.astype(f32)).astype(bf16)
 
     def backward(piece):
         return scan_bwd(
@@ -1540,17 +1572,15 @@
         )
 
     back_other = backward(1)
-    pair_came, back_other, y_grad, block_out = tie(pair_came, back_other, y_grad, block_out)
+    dbc_other = swap(back_other[3][0])
+    head_other = along_sequence(back_other[2], pieces, False)
+    back_other, y_grad = tie(back_other, y_grad)
+    back_own = backward(0)
+    pair_came, back_own, dbc_other, head_other = tie(pair_came, back_own, dbc_other, head_other)
     terms = [place.second_term(parts[i][0], pair_came[i]) for i in range(2)]
     pair_last = [place.second_exchange(i, terms[i]) for i in range(2)]
-    back_own = backward(0)
-    dbc_other = swap(back_other[3][0])
-    head_other = along_sequence(back_other[2], pieces, False)
-    pair_last, back_own, dbc_other, head_other = tie(pair_last, back_own, dbc_other, head_other)
 
     head = jnp.concatenate([along_sequence(back_own[2], pieces, False), head_other])
-    pair_sums = place.slot_parts([p[0] for p in parts], pair_came, pair_last, groups)
-    pair_others = {1: around(pair_sums[1].astype(bf16), -1)}
     place_back = (pick * first_lanes).T.astype(bf16)
     bc_dpre, dt_low, bc_small, packed = small_grads(
         back_own[3], dbc_other, bc_pre, bc_ext, flags, back_own[4], back_other[4], back_own[5], back_other[5],
@@ -1574,11 +1604,10 @@
         weight_parts(at, [normed_turned], [x_low], group, own_rows, half_channels, flip)
         for flip, group in enumerate(groups)
     ]
-    x_parts, x_low, pair_others, pair_sums, bc_head, bc_dpre, dt_low = tie(
-        x_parts, x_low, pair_others, pair_sums, bc_head, bc_dpre, dt_low)
+    x_parts, x_low, pair_last, bc_head, bc_dpre, dt_low = tie(x_parts, x_low, pair_last, bc_head, bc_dpre, dt_low)
     x_came = [place.first_exchange(i, x_parts[i][1]) for i in range(2)]
-    for d in range(2, slots - 1):
-        pair_others[d] = around(pair_sums[d].astype(bf16), -d)
+    pair_sums = place.slot_parts([p[0] for p in parts], pair_came, pair_last, groups)
+    pair_others = {d: around(pair_sums[d].astype(bf16), -d) for d in range(1, slots - 1)}
     normed_grad, normed_grad_other, thin_part = normed_grads(
         bc_dpre, bc_head, flags, cbc, dt_low, normed_turned, x_low, gate_grad, wx, wz, thin)
 
@@ -1604,7 +1633,8 @@
     x_others = [around(x_sums[1].astype(bf16), -1)]
     packed = packed + across(packed, high)
     thin_grad = place.half_rows(thin_part, high)
-    packed, thin_grad, x_others, x_sums = tie(packed, thin_grad, x_others, x_sums)
+    packed, thin_grad, x_others, x_sums, pair_sums, pair_others, mixed = tie(
+        packed, thin_grad, x_others, x_sums, pair_sums, pair_others, mixed)
 
     bc_small = packed[:, channels:]
     packed = packed[:, :channels].reshape((16, slots, half_channels))
@@ -1615,16 +1645,19 @@
     own_sums = jnp.concatenate([block(slot), bc_small], axis=1)
     for d in range(1, slots):
         own_sums = own_sums + around(jnp.concatenate([block(slot + d), bc_small], axis=1), d)
+    branch, branch_other = branch_parts(mixed, wo)
+    x_others += [around(x_sums[d].astype(bf16), -d) for d in range(2, slots)]
+    branch, branch_other, x_others, own_sums, thin_grad = tie(branch, branch_other, x_others, own_sums, thin_grad)
     thin_grad = place.sum_slots(thin_grad)
-    own_sums, thin_grad, x_sums, x_others = tie(own_sums, thin_grad, x_sums, x_others)
-    x_others += [around(x_sums[d].astype(bf16), -d) for d in range(2, slots)]
+    pair_grads = place.to_owner(pair_sums[0], list(pair_others.values()))
+    block_out = (tokens + branch + swap(branch_other).astype(f32)).astype(bf16)
     packed = own_sums[:, :half_channels]
     bc_small = own_sums[:, half_channels:]
     packed = place.ordered(0, packed, swap(packed), 1).reshape((16, slot_channels))
     by_head = packed[6:9].reshape((3, slot_heads, 64))
     norm_gain_grad = lax.dynamic_slice_in_dim(
         bc_small[5 : 5 + gain_rows].reshape((features,)), lax.axis_index("dp") * own_rows, own_rows, 0)
-    w_z_grad, w_out_grad = place.to_owner(pair_sums[0], list(pair_others.values()))
+    w_z_grad, w_out_grad = pair_grads
     w_bc_grad = thin_grad[:, :bc_width]
     w_dt_grad = lax.dynamic_slice_in_dim(thin_grad, bc_width + slot * slot_heads, slot_heads, 1)
     w_x_grad = place.to_owner(x_sums[0], x_others)[0]

time: 565 us -> 541 us (0.958)
  waiting for transfers between devices: 118 us -> 91.5 us
  matrix products: 14.4 us -> 0.71 us
  Pallas kernels: 253 us -> 264 us
    ppermute x21, waiting for transfers between devices: 31.2 us -> 11.5 us  [around(): lax.ppermute(value, 'tensor', [(i, (i + by) % size) for i in range(size)])]
    dot_general x2 -> x0, matrix products: 13.7 us -> none  [mmt(): lax.dot_general(a, b, (((1,), (1,)), ((), ())), preferred_element_type=f32)]
    pallas_call x0 -> x1, Pallas kernels: none -> 10.6 us  [branch_parts(): pl.pallas_call(branch_body, grid=(2,), in_specs=[pl.BlockSpec((tokens //...]
    ppermute x39, waiting for transfers between devices: 80.8 us -> 73.8 us  [across(): return lax.ppermute(value, 'dp', [(i, i ^ 1 << bit) for i in range(size)])]
    unnamed x156 -> x144, local copies, waits for them, and re-layouts: 12.6 us -> 11.6 us
  transfers between devices with their start and end apart: 81 -> 81, of which waited for: 23 -> 23; matrix products, arithmetic and copies ran while one was open for 10% -> 11% of each run, Pallas kernels for 45% -> 49%
where the time goes in v4:
time: 541 us; the launch traced here: 534 us
  Pallas kernels  264 us (49%)
  starting transfers between devices  93.3 us (17%)
  waiting for transfers between devices  91.5 us (17%)
  local copies, waits for them, and re-layouts  45.4 us (8%)
  other arithmetic  37.2 us (7%)
    ppermute x39, waiting for transfers between devices, across(): return lax.ppermute(value, 'dp', [(i, i ^ 1 << bit) for i in range(size)])  73.8 us
    pallas_call x2, Pallas kernels, scan_bwd(): pl.pallas_call(lambda *refs: scan_bwd_body(n_chunks, rows, *refs), grid=(...  64 us
    ppermute x21, starting transfers between devices, around(): lax.ppermute(value, 'tensor', [(i, (i + by) % size) for i in range(size)])  42.4 us
    ppermute x39, starting transfers between devices, across(): return lax.ppermute(value, 'dp', [(i, i ^ 1 << bit) for i in range(size)])  38.8 us
    pallas_call x3, Pallas kernels, project(): pl.pallas_call(lambda *refs: project_body(places, skip, *refs), grid_spec...  38.8 us
    pallas_call x4, Pallas kernels, weight_parts(): pl.pallas_call(lambda *refs: weight_parts_body(count, group, flip, *refs)...  38.7 us
    pallas_call x1, Pallas kernels, scan_fwd(): pl.pallas_call(lambda *refs: scan_fwd_body(n_chunks, rows, *refs), grid=(...  26.9 us
    pallas_call x1, Pallas kernels, normed_grads(): pl.pallas_call(normed_grads_body, grid=(2, features // tile), in_specs=[w...  22.7 us
  transfers between devices with their start and end apart: 81, of which 23 were waited for; matrix products, arithmetic and copies ran while one was open for 11% of the time, Pallas kernels for 49%

profile of v4, /device:TPU:0, one launch (start us, length us, event | category | flops | bytes accessed | tf_op | source)
XLA Modules:
  0.0 533.9 jit_solution(15140675608125832872)
XLA Ops:
  45.5 11.5 %collective-permute-done.13 = bf16[2,2,192,384]{3,2,1,0:T(8,128)(2,1)S(1)} collective-permute-done((bf16[2,2,192,384]{3,2,1,0:T(8,128)(2,1)S(1)}, bf16[2,2,192,384]{3,2,1,0:T(8,128)(2,1)S(1)}, u32[]{:S(2)}, u32[]{:S(2)}) %collective-permute-start.13) | collective-permute-done | bytes 589856 | tf_op jit(solution)/shard_map/ppermute | solution.py:897
  66.3 6.0 %collective-permute-done.18.refs_9_ = bf16[1,384,384]{2,1,0:T(8,128)(2,1)S(1)} collective-permute-done((bf16[1,384,384]{2,1,0:T(8,128)(2,1)}, bf16[1,384,384]{2,1,0:T(8,128)(2,1)S(1)}, u32[]{:S(2)}, u32[]{:S(2)}) %collective-permute-start.18) | collective-permute-done | bytes 294944 | tf_op jit(solution)/shard_map/ppermute | solution.py:897
  73.7 6.3 %collective-permute-done.19.refs_12_ = bf16[1,384,384]{2,1,0:T(8,128)(2,1)S(1)} collective-permute-done((bf16[1,384,384]{2,1,0:T(8,128)(2,1)}, bf16[1,384,384]{2,1,0:T(8,128)(2,1)S(1)}, u32[]{:S(2)}, u32[]{:S(2)}) %collective-permute-start.19) | collective-permute-done | bytes 294944 | tf_op jit(solution)/shard_map/ppermute | solution.py:897
  90.1 12.5 %prepare.1 = (f32[2,528,256]{2,1,0:T(8,128)}, f32[2,512,256]{2,1,0:T(8,128)}, f32[2,512,256]{2,1,0:T(8,128)}, bf16[2,256,512]{2,1,0:T(8,128)(2,1)}, bf16[2,512,1...) custom-call(bf16[528,1536]{1,0:T(8,128)(2,1)} %get-tuple-element.355, ...), custom_call_target="tpu_custom_call" | custom-call | flops 1 | bytes 1 | tf_op jit(solution)/shard_map/prepare/pallas_call | solution.py:521
  118.7 13.1 %project.3 = (f32[1056,1536]{1,0:T(8,128)}, bf16[1536,1536]{1,0:T(8,128)(2,1)}) custom-call(s32[8]{0:T(128)} %stack.39.refs_0_, bf16[528,1536]{1,0:T(8,128)(2,1)} %get-tuple-element.355.own_ref.refs_1_, bf16[528,1536]{1,0:T(8,128)(2,1)} %collective-permute-done.16.other_ref.refs_2_, bf16[1,384,384]{2,1,0:T(8,128)(2,1)} %slice.231.refs_3_, ...), custom_call_target="tpu_custom_call" | custom-call | flops 4982833152 | bytes 19169280 | tf_op jit(solution)/shard_map/project/pallas_call | solution.py:350
  131.8 7.5 %collective-permute-done.32.refs_12_ = bf16[2,384,384]{2,1,0:T(8,128)(2,1)} collective-permute-done((bf16[2,384,384]{2,1,0:T(8,128)(2,1)}, bf16[2,384,384]{2,1,0:T(8,128)(2,1)}, u32[]{:S(2)}, u32[]{:S(2)}) %collective-permute-start.32) | collective-permute-done | bytes 589856 | tf_op jit(solution)/shard_map/ppermute | solution.py:897
  143.4 26.9 %scan_fwd.1 = (f32[2,512,1536]{2,1,0:T(8,128)}, f32[2,2,128,1536]{3,2,1,0:T(8,128)}) custom-call(f32[2,512,128]{2,1,0:T(8,128)} %get-tuple-element.349.refs_0_, f32[2,512,8]{2,1,0:T(8,128)} %get-tuple-element.350.refs_1_.flags_ref, f32[2,32,512]{2,1,0:T(8,128)} %get-tuple-element.351.refs_2_, f32[2,8,1536]{2,1,0:T(8,128)} %get-tuple-element.352.refs_3_, ...), custom_call_target="tpu_custom_call" | custom-call | flops 3221225472 | bytes 12582912 | tf_op jit(solution)/shard_map/scan_fwd/pallas_call | solution.py:116
  175.7 11.2 %collective-permute-done.41.refs_14_ = bf16[2,384,384]{2,1,0:T(8,128)(2,1)S(1)} collective-permute-done((bf16[2,384,384]{2,1,0:T(8,128)(2,1)}, bf16[2,384,384]{2,1,0:T(8,128)(2,1)S(1)}, u32[]{:S(2)}, u32[]{:S(2)}) %collective-permute-start.41) | collective-permute-done | bytes 589856 | tf_op jit(solution)/shard_map/ppermute | solution.py:897
  189.3 12.9 %project.4 = (f32[1024,1536]{1,0:T(8,128)}, bf16[1536,1536]{1,0:T(8,128)(2,1)}) custom-call(s32[8]{0:T(128)} %stack.39.refs_0_, bf16[528,1536]{1,0:T(8,128)(2,1)} %get-tuple-element.355.own_ref.refs_1_, bf16[528,1536]{1,0:T(8,128)(2,1)} %collective-permute-done.16.other_ref.refs_2_, bf16[2,384,384]{2,1,0:T(8,128)(2,1)} %copy-done.19, ...), custom_call_target="tpu_custom_call" | custom-call | flops 4831838208 | bytes 18874368 | tf_op jit(solution)/shard_map/project/pallas_call | solution.py:350
  202.2 12.7 %project.5 = (f32[1024,1536]{1,0:T(8,128)}, bf16[1536,1536]{1,0:T(8,128)(2,1)}) custom-call(s32[8]{0:T(128)} %stack.39.refs_0_, bf16[512,1536]{1,0:T(8,128)(2,1)} %cot_ref, bf16[512,1536]{1,0:T(8,128)(2,1)} %collective-permute-done.43.refs_2_, bf16[2,384,384]{2,1,0:T(8,128)(2,1)} %copy-done.19, bf16[2,384,384]{2,1,0:T(8,128)(2,1)} %copy-done.46, ...), custom_call_target="tpu_custom_call" | custom-call | flops 4831838208 | bytes 18874368 | tf_op jit(solution)/shard_map/project/pallas_call | solution.py:350
  215.8 12.9 %gate_sums.1 = (f32[1024,1536]{1,0:T(8,128)}, f32[1024,128]{1,0:T(8,128)}) custom-call(f32[1024,1536]{1,0:T(8,128)} %bitcast.174, bf16[1024,1536]{1,0:T(8,128)(2,1)} %bitcast.169, bf16[1024,128]{1,0:T(8,128)(2,1)} %bitcast.186, bf16[2,128,1536]{2,1,0:T(8,128)(2,1)} %copy-done.1, f32[1024,1536]{1,0:T(8,128)} %get-tuple-element.407.gate_ref.refs_3_, ...), custom_call_target="tpu_custom_call" | custom-call | flops 1 | bytes 1 | tf_op jit(solution)/shard_map/gate_sums/pallas_call | solution.py:553
  231.7 17.4 %gate_grads.1 = (bf16[1024,1536]{1,0:T(8,128)(2,1)}, bf16[1024,1536]{1,0:T(8,128)(2,1)}, f32[1024,1536]{1,0:T(8,128)}, f32[8,1536]{1,0:T(8,128)}, f32[2,128,1536]{2,1,0:T(8,128)}) custom-call(f32[1024,1536]{1,0:T(8,128)} %get-tuple-element.410.refs_0_, bf16[1024,1536]{1,0:T(8,128)(2,1)} %bitcast.170, bf16[1024,128]{1,0:T(8,128)(2,1)} %bitcast.187, ...), custom_call_target="tpu_custom_call" | custom-call | flops 1 | bytes 1 | tf_op jit(solution)/shard_map/gate_grads/pallas_call | solution.py:615
  252.3 12.2 %weight_parts.5 = (bf16[2,2,2,384,384]{4,3,2,1,0:T(8,128)(2,1)}, bf16[2,2,2,384,384]{4,3,2,1,0:T(8,128)(2,1)}) custom-call(s32[8]{0:T(128)} %stack.39.refs_0_, bf16[1536,512]{1,0:T(8,128)(2,1)} %get-tuple-element.316.refs_1_.own_turned_ref, bf16[1536,512]{1,0:T(8,128)(2,1)} %collective-permute-done.22.refs_2_.other_turned_ref, ...), custom_call_target="tpu_custom_call" | custom-call | flops 4831838208 | bytes 9437184 | tf_op jit(solution)/shard_map/weight_parts/pallas_call | solution.py:872
  264.5 12.1 %weight_parts.4 = (bf16[2,2,2,384,384]{4,3,2,1,0:T(8,128)(2,1)}, bf16[2,2,2,384,384]{4,3,2,1,0:T(8,128)(2,1)}) custom-call(s32[8]{0:T(128)} %stack.39.refs_0_, bf16[1536,512]{1,0:T(8,128)(2,1)} %get-tuple-element.316.refs_1_.own_turned_ref, bf16[1536,512]{1,0:T(8,128)(2,1)} %collective-permute-done.22.refs_2_.other_turned_ref, ...), custom_call_target="tpu_custom_call" | custom-call | flops 4831838208 | bytes 9437184 | tf_op jit(solution)/shard_map/weight_parts/pallas_call | solution.py:872
  285.4 32.0 %scan_bwd.2 = (bf16[1,512,1536]{2,1,0:T(8,128)(2,1)}, f32[1,16,1536]{2,1,0:T(8,128)}, f32[1,8,1536]{2,1,0:T(8,128)}, f32[1,512,256]{2,1,0:T(8,128)}, f32[1,512,2...) custom-call(f32[2,512,128]{2,1,0:T(8,128)} %get-tuple-element.349.refs_0_, ...), custom_call_target="tpu_custom_call" | custom-call | flops 4831838208 | bytes 9437184 | tf_op jit(solution)/shard_map/scan_bwd/pallas_call | solution.py:278
  320.4 32.0 %scan_bwd.3 = (bf16[1,512,1536]{2,1,0:T(8,128)(2,1)}, f32[1,16,1536]{2,1,0:T(8,128)}, f32[1,8,1536]{2,1,0:T(8,128)}, f32[1,512,256]{2,1,0:T(8,128)}, f32[1,512,2...) custom-call(f32[2,512,128]{2,1,0:T(8,128)} %get-tuple-element.349.refs_0_, ...), custom_call_target="tpu_custom_call" | custom-call | flops 4831838208 | bytes 9437184 | tf_op jit(solution)/shard_map/scan_bwd/pallas_call | solution.py:278
  359.7 6.0 %small_grads.1 = (f32[512,256]{1,0:T(8,128)}, bf16[2,512,128]{2,1,0:T(8,128)(2,1)}, f32[16,256]{1,0:T(8,128)}, f32[16,1536]{1,0:T(8,128)}) custom-call(f32[1,512,256]{2,1,0:T(8,128)} %get-tuple-element.445.dbc_ref, f32[512,256]{1,0:T(8,128)} %copy-done.21, f32[2,512,256]{2,1,0:T(8,128)} %get-tuple-element.447.pre_ref, ...), custom_call_target="tpu_custom_call" | custom-call | flops 1 | bytes 1 | tf_op jit(solution)/shard_map/small_grads/pallas_call | solution.py:688
  371.7 7.2 %weight_parts.7 = (bf16[1,2,2,384,384]{4,3,2,1,0:T(8,128)(2,1)}, bf16[1,2,2,384,384]{4,3,2,1,0:T(8,128)(2,1)}) custom-call(s32[8]{0:T(128)} %stack.39.refs_0_, bf16[1536,512]{1,0:T(8,128)(2,1)} %get-tuple-element.316.refs_1_.own_turned_ref, bf16[1536,512]{1,0:T(8,128)(2,1)} %collective-permute-done.22.refs_2_.other_turned_ref, ...), custom_call_target="tpu_custom_call" | custom-call | flops 2415919104 | bytes 4718592 | tf_op jit(solution)/shard_map/weight_parts/pallas_call | solution.py:872
  378.9 7.2 %weight_parts.6 = (bf16[1,2,2,384,384]{4,3,2,1,0:T(8,128)(2,1)}, bf16[1,2,2,384,384]{4,3,2,1,0:T(8,128)(2,1)}) custom-call(s32[8]{0:T(128)} %stack.39.refs_0_, bf16[1536,512]{1,0:T(8,128)(2,1)} %get-tuple-element.316.refs_1_.own_turned_ref, bf16[1536,512]{1,0:T(8,128)(2,1)} %collective-permute-done.22.refs_2_.other_turned_ref, ...), custom_call_target="tpu_custom_call" | custom-call | flops 2415919104 | bytes 4718592 | tf_op jit(solution)/shard_map/weight_parts/pallas_call | solution.py:872
  404.1 22.7 %normed_grads.1 = (f32[512,1536]{1,0:T(8,128)}, bf16[512,1536]{1,0:T(8,128)(2,1)}, bf16[1536,384]{1,0:T(8,128)(2,1)}) custom-call(f32[512,256]{1,0:T(8,128)} %get-tuple-element.477.dpre_ref, f32[8,256]{1,0:T(8,128)} %copy-done.64, f32[2,512,8]{2,1,0:T(8,128)} %get-tuple-element.350.refs_1_.flags_ref, f32[8,256]{1,0:T(8,128)} %maximum_maximum_fusion.2.cbc_ref, ...), custom_call_target="tpu_custom_call" | custom-call | flops 9663676416 | bytes 18874368 | tf_op jit(solution)/shard_map/normed_grads/pallas_call | solution.py:741
  444.9 6.2 %x_grads.1 = (f32[512,1536]{1,0:T(8,128)}, f32[8,1536]{1,0:T(8,128)}) custom-call(f32[512,1536]{1,0:T(8,128)} %get-tuple-element.497.own_ref, bf16[512,1536]{1,0:T(8,128)(2,1)} %copy-done.9, bf16[512,1536]{1,0:T(8,128)(2,1)} %x_ref.2, bf16[512,1536]{1,0:T(8,128)(2,1)} %cot_ref, f32[1,1536]{1,0:T(1,128)} %reshape.507.gain_ref), custom_call_target="tpu_custom_call" | custom-call | flops 1 | bytes 1 | tf_op jit(solution)/shard_map/x_grads/pallas_call | solution.py:822
  454.4 7.7 %collective-permute-done.64 = bf16[2,192,384]{2,1,0:T(8,128)(2,1)S(1)} collective-permute-done((bf16[2,192,384]{2,1,0:T(8,128)(2,1)S(1)}, bf16[2,192,384]{2,1,0:T(8,128)(2,1)S(1)}, u32[]{:S(2)}, u32[]{:S(2)}) %collective-permute-start.64) | collective-permute-done | bytes 294944 | tf_op jit(solution)/shard_map/ppermute | solution.py:897
  485.6 10.6 %branch_parts.1 = (f32[512,1536]{1,0:T(8,128)}, bf16[512,1536]{1,0:T(8,128)(2,1)}) custom-call(bf16[1024,1536]{1,0:T(8,128)(2,1)} %get-tuple-element.516.refs_6_.mixed_ref, bf16[1536,1536]{1,0:T(8,128)(2,1)} %get-tuple-element.517.weight_ref), custom_call_target="tpu_custom_call" | custom-call | flops 4831838208 | bytes 9437184 | tf_op jit(solution)/shard_map/branch_parts/pallas_call | solution.py:780
  499.4 5.9 %collective-permute-done.69 = bf16[1,384,384]{2,1,0:T(8,128)(2,1)S(1)} collective-permute-done((bf16[1,384,384]{2,1,0:T(8,128)(2,1)S(1)}, bf16[1,384,384]{2,1,0:T(8,128)(2,1)S(1)}, u32[]{:S(2)}, u32[]{:S(2)}) %collective-permute-start.69) | collective-permute-done | bytes 294944 | tf_op jit(solution)/shard_map/ppermute | solution.py:903
  (452 shorter events, 219.0 us)
Async XLA Ops:
  82.0 29.4 %collective-permute-start.24 = (bf16[2,384,384]{2,1,0:T(8,128)(2,1)S(1)}, bf16[2,384,384]{2,1,0:T(8,128)(2,1)S(1)}, u32[]{:S(2)}, u32[]{:S(2)}) collective-permute-start(bf16[2,384,384]{2,1,0:T(8,128)(2,1)S(1)} %slice.234.refs_3_), channel_id=1, source_target_pairs={{0,8},{4,12},{8,0},{12,4},{16,24},{20,28},{24,16},{28,20},{1,9},{5... | collective-permute-start | bytes 1769480 | tf_op jit(solution)/shard_map/ppermute | solution.py:897
  82.2 29.3 %collective-permute-start.25 = (bf16[2,384,384]{2,1,0:T(8,128)(2,1)S(1)}, bf16[2,384,384]{2,1,0:T(8,128)(2,1)S(1)}, u32[]{:S(2)}, u32[]{:S(2)}) collective-permute-start(bf16[2,384,384]{2,1,0:T(8,128)(2,1)S(1)} %slice.234.refs_3_), channel_id=1, source_target_pairs={{0,16},{4,20},{8,24},{12,28},{16,0},{20,4},{24,8},{28,12},{1,17},{... | collective-permute-start | bytes 1769480 | tf_op jit(solution)/shard_map/ppermute | solution.py:897
  83.8 27.7 %collective-permute-start.26 = (bf16[2,384,384]{2,1,0:T(8,128)(2,1)S(1)}, bf16[2,384,384]{2,1,0:T(8,128)(2,1)}, u32[]{:S(2)}, u32[]{:S(2)}) collective-permute-start(bf16[2,384,384]{2,1,0:T(8,128)(2,1)S(1)} %slice.234.refs_3_), channel_id=1, source_target_pairs={{0,2},{1,3},{2,0},{3,1},{4,6},{5,7},{6,4},{7,5},{8,10},{9,11},{10,... | collective-permute-start | bytes 1769480 | tf_op jit(solution)/shard_map/ppermute | solution.py:903
  112.2 27.1 %collective-permute-start.33 = (bf16[2,384,384]{2,1,0:T(8,128)(2,1)}, bf16[2,384,384]{2,1,0:T(8,128)(2,1)}, u32[]{:S(2)}, u32[]{:S(2)}) collective-permute-start(bf16[2,384,384]{2,1,0:T(8,128)(2,1)} %collective-permute-done.17.refs_7_), channel_id=1, source_target_pairs={{0,8},{4,12},{8,0},{12,4},{16,24},{20,28},{24,16},{28,20},{1,9},{5... | collective-permute-start | bytes 1769480 | tf_op jit(solution)/shard_map/ppermute | solution.py:897
  139.3 31.0 %collective-permute-start.36 = (bf16[2,384,384]{2,1,0:T(8,128)(2,1)}, bf16[2,384,384]{2,1,0:T(8,128)(2,1)}, u32[]{:S(2)}, u32[]{:S(2)}) collective-permute-start(bf16[2,384,384]{2,1,0:T(8,128)(2,1)} %collective-permute-done.35.refs_15_), channel_id=1, source_target_pairs={{0,16},{4,20},{8,24},{12,28},{16,0},{20,4},{24,8},{28,12},{1,17},{... | collective-permute-start | bytes 1769480 | tf_op jit(solution)/shard_map/ppermute | solution.py:897
  141.0 29.9 %collective-permute-start.37 = (bf16[2,384,384]{2,1,0:T(8,128)(2,1)}, bf16[2,384,384]{2,1,0:T(8,128)(2,1)S(1)}, u32[]{:S(2)}, u32[]{:S(2)}) collective-permute-start(bf16[2,384,384]{2,1,0:T(8,128)(2,1)} %collective-permute-done.26.refs_11_), channel_id=1, source_target_pairs={{0,16},{4,20},{8,24},{12,28},{16,0},{20,4},{24,8},{28,12},{1,17},{... | collective-permute-start | bytes 1769480 | tf_op jit(solution)/shard_map/ppermute | solution.py:897
  141.4 29.6 %collective-permute-start.38 = (bf16[2,384,384]{2,1,0:T(8,128)(2,1)}, bf16[2,384,384]{2,1,0:T(8,128)(2,1)S(1)}, u32[]{:S(2)}, u32[]{:S(2)}) collective-permute-start(bf16[2,384,384]{2,1,0:T(8,128)(2,1)} %collective-permute-done.35.refs_15_), channel_id=1, source_target_pairs={{0,8},{4,12},{8,0},{12,4},{16,24},{20,28},{24,16},{28,20},{1,9},{5... | collective-permute-start | bytes 1769480 | tf_op jit(solution)/shard_map/ppermute | solution.py:897
  143.1 27.9 %collective-permute-start.39 = (bf16[2,384,384]{2,1,0:T(8,128)(2,1)}, bf16[2,384,384]{2,1,0:T(8,128)(2,1)S(1)}, u32[]{:S(2)}, u32[]{:S(2)}) collective-permute-start(bf16[2,384,384]{2,1,0:T(8,128)(2,1)} %collective-permute-done.31.refs_9_), channel_id=1, source_target_pairs={{0,8},{4,12},{8,0},{12,4},{16,24},{20,28},{24,16},{28,20},{1,9},{5... | collective-permute-start | bytes 1769480 | tf_op jit(solution)/shard_map/ppermute | solution.py:897
  143.4 58.7 %collective-permute-start.43 = (bf16[512,1536]{1,0:T(8,128)(2,1)S(1)}, bf16[512,1536]{1,0:T(8,128)(2,1)}, u32[]{:S(2)}, u32[]{:S(2)}) collective-permute-start(bf16[512,1536]{1,0:T(8,128)(2,1)S(1)} %copy-done.3), channel_id=1, source_target_pairs={{0,4},{4,0},{8,12},{12,8},{16,20},{20,16},{24,28},{28,24},{1,5},{5... | collective-permute-start | bytes 4718600 | tf_op jit(solution)/shard_map/ppermute | solution.py:892
  170.3 82.0 %collective-permute-start.23 = (bf16[1536,512]{1,0:T(8,128)(2,1)}, bf16[1536,512]{1,0:T(8,128)(2,1)}, u32[]{:S(2)}, u32[]{:S(2)}) collective-permute-start(bf16[1536,512]{1,0:T(8,128)(2,1)} %turn.1.refs_3_), channel_id=1, source_target_pairs={{0,4},{4,0},{8,12},{12,8},{16,20},{20,16},{24,28},{28,24},{1,5},{5... | collective-permute-start | bytes 4718600 | tf_op jit(solution)/shard_map/ppermute | solution.py:892
  170.9 81.4 %collective-permute-start.22 = (bf16[1536,512]{1,0:T(8,128)(2,1)}, bf16[1536,512]{1,0:T(8,128)(2,1)}, u32[]{:S(2)}, u32[]{:S(2)}) collective-permute-start(bf16[1536,512]{1,0:T(8,128)(2,1)} %get-tuple-element.316.refs_1_.own_turned_ref), channel_id=1, source_target_pairs={{0,4},{4,0},{8,12},{12,8},{16,20},{20,16},{24,28},{28,24},{1,5},{5... | collective-permute-start | bytes 4718600 | tf_op jit(solution)/shard_map/ppermute | solution.py:892
  186.9 28.0 %collective-permute-start.40 = (bf16[2,128,1536]{2,1,0:T(8,128)(2,1)S(1)}, bf16[2,128,1536]{2,1,0:T(8,128)(2,1)S(1)}, u32[]{:S(2)}, u32[]{:S(2)}) collective-permute-start(bf16[2,128,1536]{2,1,0:T(8,128)(2,1)S(1)} %fusion.3), channel_id=1, source_target_pairs={{0,1},{2,3},{4,5},{6,7},{8,9},{10,11},{12,13},{14,15},{16,17},{18,... | collective-permute-start | bytes 2359304 | tf_op jit(solution)/shard_map/ppermute | solution.py:911
  280.4 72.1 %collective-permute-start.46 = (bf16[2,2,2,384,384]{4,3,0,1,2:T(8,128)(2,1)}, bf16[2,2,2,384,384]{4,3,0,1,2:T(8,128)(2,1)}, u32[]{:S(2)}, u32[]{:S(2)}) collective-permute-start(bf16[2,2,2,384,384]{4,3,0,1,2:T(8,128)(2,1)} %copy.100), channel_id=1, source_target_pairs={{0,16},{4,20},{8,24},{12,28},{16,0},{20,4},{24,8},{28,12},{1,17},{... | collective-permute-start | bytes 7077896 | tf_op jit(solution)/shard_map/ppermute | solution.py:897
  281.4 71.1 %collective-permute-start.47 = (bf16[2,2,2,384,384]{4,3,2,1,0:T(8,128)(2,1)}, bf16[2,2,2,384,384]{4,3,2,1,0:T(8,128)(2,1)}, u32[]{:S(2)}, u32[]{:S(2)}) collective-permute-start(bf16[2,2,2,384,384]{4,3,2,1,0:T(8,128)(2,1)} %get-tuple-element.421), channel_id=1, source_target_pairs={{0,8},{4,12},{8,0},{12,4},{16,24},{20,28},{24,16},{28,20},{1,9},{5... | collective-permute-start | bytes 7077896 | tf_op jit(solution)/shard_map/ppermute | solution.py:897
  317.4 35.0 %collective-permute-start.48 = (f32[512,256]{1,0:T(8,128)}, f32[512,256]{1,0:T(8,128)S(1)}, u32[]{:S(2)}, u32[]{:S(2)}) collective-permute-start(f32[512,256]{1,0:T(8,128)} %bitcast.214), channel_id=1, source_target_pairs={{0,4},{4,0},{8,12},{12,8},{16,20},{20,16},{24,28},{28,24},{1,5},{5... | collective-permute-start | bytes 1572872 | tf_op jit(solution)/shard_map/ppermute | solution.py:892
  319.1 33.3 %collective-permute-start.49 = (f32[1,8,1536]{2,1,0:T(8,128)}, f32[1,8,1536]{2,1,0:T(8,128)S(1)}, u32[]{:S(2)}, u32[]{:S(2)}) collective-permute-start(f32[1,8,1536]{2,1,0:T(8,128)} %get-tuple-element.426), channel_id=1, source_target_pairs={{1,0},{3,2},{5,4},{7,6},{9,8},{11,10},{13,12},{15,14},{17,16},{19,... | collective-permute-start | bytes 147464 | tf_op jit(solution)/shard_map/ppermute | solution.py:911
  354.9 31.2 %collective-permute-start.52 = (bf16[2,2,384,384]{3,2,1,0:T(8,128)(2,1)S(1)}, bf16[2,2,384,384]{3,2,1,0:T(8,128)(2,1)S(1)}, u32[]{:S(2)}, u32[]{:S(2)}) collective-permute-start(bf16[2,2,384,384]{3,2,1,0:T(8,128)(2,1)S(1)} %fusion.1), channel_id=1, source_target_pairs={{0,16},{4,20},{8,24},{12,28},{16,0},{20,4},{24,8},{28,12},{1,17},{... | collective-permute-start | bytes 3538952 | tf_op jit(solution)/shard_map/ppermute | solution.py:897
  359.1 28.3 %collective-permute-start.51 = (bf16[2,2,384,384]{3,2,0,1:T(8,128)(2,1)S(1)}, bf16[2,2,384,384]{3,2,0,1:T(8,128)(2,1)}, u32[]{:S(2)}, u32[]{:S(2)}) collective-permute-start(bf16[2,2,384,384]{3,2,0,1:T(8,128)(2,1)S(1)} %fusion), channel_id=1, source_target_pairs={{0,8},{4,12},{8,0},{12,4},{16,24},{20,28},{24,16},{28,20},{1,9},{5... | collective-permute-start | bytes 3538952 | tf_op jit(solution)/shard_map/ppermute | solution.py:897
  390.7 36.2 %collective-permute-start.57 = (bf16[2,384,384]{2,1,0:T(8,128)(2,1)}, bf16[2,384,384]{2,1,0:T(8,128)(2,1)}, u32[]{:S(2)}, u32[]{:S(2)}) collective-permute-start(bf16[2,384,384]{2,1,0:T(8,128)(2,1)} %fusion.49), channel_id=1, source_target_pairs={{0,2},{1,3},{2,0},{3,1},{4,6},{5,7},{6,4},{7,5},{8,10},{9,11},{10,... | collective-permute-start | bytes 1769480 | tf_op jit(solution)/shard_map/ppermute | solution.py:903
  397.1 29.8 %collective-permute-start.56 = (bf16[2,384,384]{2,1,0:T(8,128)(2,1)}, bf16[2,384,384]{2,1,0:T(8,128)(2,1)}, u32[]{:S(2)}, u32[]{:S(2)}) collective-permute-start(bf16[2,384,384]{2,1,0:T(8,128)(2,1)} %get-tuple-element.618), channel_id=1, source_target_pairs={{0,3},{1,0},{2,1},{3,2},{4,7},{5,4},{6,5},{7,6},{8,11},{9,8},{10,9... | collective-permute-start | bytes 1769480 | tf_op jit(solution)/shard_map/ppermute | solution.py:903
  401.8 27.7 %collective-permute-start.54 = (bf16[1,2,2,384,384]{4,3,1,2,0:T(8,128)(2,1)}, bf16[1,2,2,384,384]{4,3,1,2,0:T(8,128)(2,1)}, u32[]{:S(2)}, u32[]{:S(2)}) collective-permute-start(bf16[1,2,2,384,384]{4,3,1,2,0:T(8,128)(2,1)} %copy.105), channel_id=1, source_target_pairs={{0,16},{4,20},{8,24},{12,28},{16,0},{20,4},{24,8},{28,12},{1,17},{... | collective-permute-start | bytes 3538952 | tf_op jit(solution)/shard_map/ppermute | solution.py:897
  402.8 27.4 %collective-permute-start.55 = (bf16[1,2,2,384,384]{4,3,2,1,0:T(8,128)(2,1)}, bf16[1,2,2,384,384]{4,3,2,1,0:T(8,128)(2,1)}, u32[]{:S(2)}, u32[]{:S(2)}) collective-permute-start(bf16[1,2,2,384,384]{4,3,2,1,0:T(8,128)(2,1)} %get-tuple-element.476), channel_id=1, source_target_pairs={{0,8},{4,12},{8,0},{12,4},{16,24},{20,28},{24,16},{28,20},{1,9},{5... | collective-permute-start | bytes 3538952 | tf_op jit(solution)/shard_map/ppermute | solution.py:897
  434.3 29.8 %collective-permute-start.59 = (bf16[1,2,384,384]{3,2,1,0:T(8,128)(2,1)}, bf16[1,2,384,384]{3,2,1,0:T(8,128)(2,1)}, u32[]{:S(2)}, u32[]{:S(2)}) collective-permute-start(bf16[1,2,384,384]{3,2,1,0:T(8,128)(2,1)} %fusion.7), channel_id=1, source_target_pairs={{0,16},{4,20},{8,24},{12,28},{16,0},{20,4},{24,8},{28,12},{1,17},{... | collective-permute-start | bytes 1769480 | tf_op jit(solution)/shard_map/ppermute | solution.py:897
  437.3 26.8 %collective-permute-start.58 = (bf16[1,2,384,384]{3,2,1,0:T(8,128)(2,1)}, bf16[1,2,384,384]{3,2,1,0:T(8,128)(2,1)}, u32[]{:S(2)}, u32[]{:S(2)}) collective-permute-start(bf16[1,2,384,384]{3,2,1,0:T(8,128)(2,1)} %fusion.6), channel_id=1, source_target_pairs={{0,8},{4,12},{8,0},{12,4},{16,24},{20,28},{24,16},{28,20},{1,9},{5... | collective-permute-start | bytes 1769480 | tf_op jit(solution)/shard_map/ppermute | solution.py:897
  (122 other events, 1304.2 us)

commit v5 on v4

--- a/solution.py
+++ b/solution.py
@@ -1627,14 +1627,16 @@
     packed = packed + across(packed, low)
     thin_part = place.half_rows(thin_part, low)
 
-    x_last, packed, thin_part, x_grad, pair_sums, pair_others = tie(
-        x_last, packed, thin_part, x_grad, pair_sums, pair_others)
     x_sums = place.slot_parts([p[0] for p in x_parts], x_came, x_last, groups)
     x_others = [around(x_sums[1].astype(bf16), -1)]
+    x_sums, x_others, packed, thin_part, x_grad, pair_sums, pair_others = tie(
+        x_sums, x_others, packed, thin_part, x_grad, pair_sums, pair_others)
+    x_others.append(around(x_sums[2].astype(bf16), -2))
+    pair_grads = place.to_owner(pair_sums[0], list(pair_others.values()))
     packed = packed + across(packed, high)
     thin_grad = place.half_rows(thin_part, high)
-    packed, thin_grad, x_others, x_sums, pair_sums, pair_others, mixed = tie(
-        packed, thin_grad, x_others, x_sums, pair_sums, pair_others, mixed)
+    packed, thin_grad, x_others, x_sums, pair_grads, mixed = tie(
+        packed, thin_grad, x_others, x_sums, pair_grads, mixed)
 
     bc_small = packed[:, channels:]
     packed = packed[:, :channels].reshape((16, slots, half_channels))
@@ -1646,10 +1648,9 @@
     for d in range(1, slots):
         own_sums = own_sums + around(jnp.concatenate([block(slot + d), bc_small], axis=1), d)
     branch, branch_other = branch_parts(mixed, wo)
-    x_others += [around(x_sums[d].astype(bf16), -d) for d in range(2, slots)]
+    x_others += [around(x_sums[d].astype(bf16), -d) for d in range(3, slots)]
     branch, branch_other, x_others, own_sums, thin_grad = tie(branch, branch_other, x_others, own_sums, thin_grad)
     thin_grad = place.sum_slots(thin_grad)
-    pair_grads = place.to_owner(pair_sums[0], list(pair_others.values()))
     block_out = (tokens + branch + swap(branch_other).astype(f32)).astype(bf16)
     packed = own_sums[:, :half_channels]
     bc_small = own_sums[:, half_channels:]

time: 541 us -> 545 us (level)
    unnamed x144 -> x138, local copies, waits for them, and re-layouts: 11.6 us -> 9.28 us
  transfers between devices with their start and end apart: 81 -> 81, of which waited for: 23 -> 24; matrix products, arithmetic and copies ran while one was open for 11% -> 11% of each run, Pallas kernels for 49% -> 48%
where the time goes in v5:
time: 545 us; the launch traced here: 536 us
  Pallas kernels  264 us (48%)
  starting transfers between devices  96.5 us (18%)
  waiting for transfers between devices  91.9 us (17%)
  local copies, waits for them, and re-layouts  42.7 us (8%)
  other arithmetic  38.8 us (7%)
    ppermute x39, waiting for transfers between devices, across(): return lax.ppermute(value, 'dp', [(i, i ^ 1 << bit) for i in range(size)])  73.4 us
    pallas_call x2, Pallas kernels, scan_bwd(): pl.pallas_call(lambda *refs: scan_bwd_body(n_chunks, rows, *refs), grid=(...  64 us
    ppermute x21, starting transfers between devices, around(): lax.ppermute(value, 'tensor', [(i, (i + by) % size) for i in range(size)])  44.9 us
    ppermute x39, starting transfers between devices, across(): return lax.ppermute(value, 'dp', [(i, i ^ 1 << bit) for i in range(size)])  39 us
    pallas_call x4, Pallas kernels, weight_parts(): pl.pallas_call(lambda *refs: weight_parts_body(count, group, flip, *refs)...  38.7 us
    pallas_call x3, Pallas kernels, project(): pl.pallas_call(lambda *refs: project_body(places, skip, *refs), grid_spec...  38.7 us
    pallas_call x1, Pallas kernels, scan_fwd(): pl.pallas_call(lambda *refs: scan_fwd_body(n_chunks, rows, *refs), grid=(...  26.9 us
    pallas_call x1, Pallas kernels, normed_grads(): pl.pallas_call(normed_grads_body, grid=(2, features // tile), in_specs=[w...  22.7 us
  transfers between devices with their start and end apart: 81, of which 24 were waited for; matrix products, arithmetic and copies ran while one was open for 11% of the time, Pallas kernels for 48%

profile of v5, /device:TPU:0, one launch (start us, length us, event | category | flops | bytes accessed | tf_op | source)
XLA Modules:
  0.0 536.4 jit_solution(7482474806651606093)
XLA Ops:
  45.5 11.5 %collective-permute-done.13 = bf16[2,2,192,384]{3,2,1,0:T(8,128)(2,1)S(1)} collective-permute-done((bf16[2,2,192,384]{3,2,1,0:T(8,128)(2,1)S(1)}, bf16[2,2,192,384]{3,2,1,0:T(8,128)(2,1)S(1)}, u32[]{:S(2)}, u32[]{:S(2)}) %collective-permute-start.13) | collective-permute-done | bytes 589856 | tf_op jit(solution)/shard_map/ppermute | solution.py:897
  66.3 5.9 %collective-permute-done.18.refs_9_ = bf16[1,384,384]{2,1,0:T(8,128)(2,1)S(1)} collective-permute-done((bf16[1,384,384]{2,1,0:T(8,128)(2,1)}, bf16[1,384,384]{2,1,0:T(8,128)(2,1)S(1)}, u32[]{:S(2)}, u32[]{:S(2)}) %collective-permute-start.18) | collective-permute-done | bytes 294944 | tf_op jit(solution)/shard_map/ppermute | solution.py:897
  73.7 6.3 %collective-permute-done.19.refs_12_ = bf16[1,384,384]{2,1,0:T(8,128)(2,1)S(1)} collective-permute-done((bf16[1,384,384]{2,1,0:T(8,128)(2,1)}, bf16[1,384,384]{2,1,0:T(8,128)(2,1)S(1)}, u32[]{:S(2)}, u32[]{:S(2)}) %collective-permute-start.19) | collective-permute-done | bytes 294944 | tf_op jit(solution)/shard_map/ppermute | solution.py:897
  90.1 12.5 %prepare.1 = (f32[2,528,256]{2,1,0:T(8,128)}, f32[2,512,256]{2,1,0:T(8,128)}, f32[2,512,256]{2,1,0:T(8,128)}, bf16[2,256,512]{2,1,0:T(8,128)(2,1)}, bf16[2,512,1...) custom-call(bf16[528,1536]{1,0:T(8,128)(2,1)} %get-tuple-element.354, ...), custom_call_target="tpu_custom_call" | custom-call | flops 1 | bytes 1 | tf_op jit(solution)/shard_map/prepare/pallas_call | solution.py:521
  118.8 13.1 %project.3 = (f32[1056,1536]{1,0:T(8,128)}, bf16[1536,1536]{1,0:T(8,128)(2,1)}) custom-call(s32[8]{0:T(128)} %stack.39.refs_0_, bf16[528,1536]{1,0:T(8,128)(2,1)} %get-tuple-element.354.own_ref.refs_1_, bf16[528,1536]{1,0:T(8,128)(2,1)} %collective-permute-done.16.other_ref.refs_2_, bf16[1,384,384]{2,1,0:T(8,128)(2,1)} %slice.229.refs_3_, ...), custom_call_target="tpu_custom_call" | custom-call | flops 4982833152 | bytes 19169280 | tf_op jit(solution)/shard_map/project/pallas_call | solution.py:350
  131.9 7.4 %collective-permute-done.32.refs_12_ = bf16[2,384,384]{2,1,0:T(8,128)(2,1)} collective-permute-done((bf16[2,384,384]{2,1,0:T(8,128)(2,1)}, bf16[2,384,384]{2,1,0:T(8,128)(2,1)}, u32[]{:S(2)}, u32[]{:S(2)}) %collective-permute-start.32) | collective-permute-done | bytes 589856 | tf_op jit(solution)/shard_map/ppermute | solution.py:897
  143.5 26.9 %scan_fwd.1 = (f32[2,512,1536]{2,1,0:T(8,128)}, f32[2,2,128,1536]{3,2,1,0:T(8,128)}) custom-call(f32[2,512,128]{2,1,0:T(8,128)} %get-tuple-element.348.refs_0_, f32[2,512,8]{2,1,0:T(8,128)} %get-tuple-element.349.refs_1_.flags_ref, f32[2,32,512]{2,1,0:T(8,128)} %get-tuple-element.350.refs_2_, f32[2,8,1536]{2,1,0:T(8,128)} %get-tuple-element.351.refs_3_, ...), custom_call_target="tpu_custom_call" | custom-call | flops 3221225472 | bytes 12582912 | tf_op jit(solution)/shard_map/scan_fwd/pallas_call | solution.py:116
  175.6 11.3 %collective-permute-done.41.refs_14_ = bf16[2,384,384]{2,1,0:T(8,128)(2,1)S(1)} collective-permute-done((bf16[2,384,384]{2,1,0:T(8,128)(2,1)}, bf16[2,384,384]{2,1,0:T(8,128)(2,1)S(1)}, u32[]{:S(2)}, u32[]{:S(2)}) %collective-permute-start.41) | collective-permute-done | bytes 589856 | tf_op jit(solution)/shard_map/ppermute | solution.py:897
  189.3 12.8 %project.4 = (f32[1024,1536]{1,0:T(8,128)}, bf16[1536,1536]{1,0:T(8,128)(2,1)}) custom-call(s32[8]{0:T(128)} %stack.39.refs_0_, bf16[528,1536]{1,0:T(8,128)(2,1)} %get-tuple-element.354.own_ref.refs_1_, bf16[528,1536]{1,0:T(8,128)(2,1)} %collective-permute-done.16.other_ref.refs_2_, bf16[2,384,384]{2,1,0:T(8,128)(2,1)} %copy-done.18, ...), custom_call_target="tpu_custom_call" | custom-call | flops 4831838208 | bytes 18874368 | tf_op jit(solution)/shard_map/project/pallas_call | solution.py:350
  202.1 12.8 %project.5 = (f32[1024,1536]{1,0:T(8,128)}, bf16[1536,1536]{1,0:T(8,128)(2,1)}) custom-call(s32[8]{0:T(128)} %stack.39.refs_0_, bf16[512,1536]{1,0:T(8,128)(2,1)} %cot_ref, bf16[512,1536]{1,0:T(8,128)(2,1)} %collective-permute-done.43.refs_2_, bf16[2,384,384]{2,1,0:T(8,128)(2,1)} %copy-done.18, bf16[2,384,384]{2,1,0:T(8,128)(2,1)} %copy-done.44, ...), custom_call_target="tpu_custom_call" | custom-call | flops 4831838208 | bytes 18874368 | tf_op jit(solution)/shard_map/project/pallas_call | solution.py:350
  215.8 12.9 %gate_sums.1 = (f32[1024,1536]{1,0:T(8,128)}, f32[1024,128]{1,0:T(8,128)}) custom-call(f32[1024,1536]{1,0:T(8,128)} %bitcast.172, bf16[1024,1536]{1,0:T(8,128)(2,1)} %bitcast.167, bf16[1024,128]{1,0:T(8,128)(2,1)} %bitcast.182, bf16[2,128,1536]{2,1,0:T(8,128)(2,1)} %copy-done.1, f32[1024,1536]{1,0:T(8,128)} %get-tuple-element.406.gate_ref.refs_3_, ...), custom_call_target="tpu_custom_call" | custom-call | flops 1 | bytes 1 | tf_op jit(solution)/shard_map/gate_sums/pallas_call | solution.py:553
  231.6 17.4 %gate_grads.1 = (bf16[1024,1536]{1,0:T(8,128)(2,1)}, bf16[1024,1536]{1,0:T(8,128)(2,1)}, f32[1024,1536]{1,0:T(8,128)}, f32[8,1536]{1,0:T(8,128)}, f32[2,128,1536]{2,1,0:T(8,128)}) custom-call(f32[1024,1536]{1,0:T(8,128)} %get-tuple-element.409.refs_0_, bf16[1024,1536]{1,0:T(8,128)(2,1)} %bitcast.168, bf16[1024,128]{1,0:T(8,128)(2,1)} %bitcast.183, ...), custom_call_target="tpu_custom_call" | custom-call | flops 1 | bytes 1 | tf_op jit(solution)/shard_map/gate_grads/pallas_call | solution.py:615
  252.3 12.2 %weight_parts.5 = (bf16[2,2,2,384,384]{4,3,2,1,0:T(8,128)(2,1)}, bf16[2,2,2,384,384]{4,3,2,1,0:T(8,128)(2,1)}) custom-call(s32[8]{0:T(128)} %stack.39.refs_0_, bf16[1536,512]{1,0:T(8,128)(2,1)} %get-tuple-element.315.refs_1_.own_turned_ref, bf16[1536,512]{1,0:T(8,128)(2,1)} %collective-permute-done.22.refs_2_.other_turned_ref, ...), custom_call_target="tpu_custom_call" | custom-call | flops 4831838208 | bytes 9437184 | tf_op jit(solution)/shard_map/weight_parts/pallas_call | solution.py:872
  264.5 12.1 %weight_parts.4 = (bf16[2,2,2,384,384]{4,3,2,1,0:T(8,128)(2,1)}, bf16[2,2,2,384,384]{4,3,2,1,0:T(8,128)(2,1)}) custom-call(s32[8]{0:T(128)} %stack.39.refs_0_, bf16[1536,512]{1,0:T(8,128)(2,1)} %get-tuple-element.315.refs_1_.own_turned_ref, bf16[1536,512]{1,0:T(8,128)(2,1)} %collective-permute-done.22.refs_2_.other_turned_ref, ...), custom_call_target="tpu_custom_call" | custom-call | flops 4831838208 | bytes 9437184 | tf_op jit(solution)/shard_map/weight_parts/pallas_call | solution.py:872
  285.4 32.0 %scan_bwd.2 = (bf16[1,512,1536]{2,1,0:T(8,128)(2,1)}, f32[1,16,1536]{2,1,0:T(8,128)}, f32[1,8,1536]{2,1,0:T(8,128)}, f32[1,512,256]{2,1,0:T(8,128)}, f32[1,512,2...) custom-call(f32[2,512,128]{2,1,0:T(8,128)} %get-tuple-element.348.refs_0_, ...), custom_call_target="tpu_custom_call" | custom-call | flops 4831838208 | bytes 9437184 | tf_op jit(solution)/shard_map/scan_bwd/pallas_call | solution.py:278
  320.4 32.0 %scan_bwd.3 = (bf16[1,512,1536]{2,1,0:T(8,128)(2,1)}, f32[1,16,1536]{2,1,0:T(8,128)}, f32[1,8,1536]{2,1,0:T(8,128)}, f32[1,512,256]{2,1,0:T(8,128)}, f32[1,512,2...) custom-call(f32[2,512,128]{2,1,0:T(8,128)} %get-tuple-element.348.refs_0_, ...), custom_call_target="tpu_custom_call" | custom-call | flops 4831838208 | bytes 9437184 | tf_op jit(solution)/shard_map/scan_bwd/pallas_call | solution.py:278
  359.7 6.0 %small_grads.1 = (f32[512,256]{1,0:T(8,128)}, bf16[2,512,128]{2,1,0:T(8,128)(2,1)}, f32[16,256]{1,0:T(8,128)}, f32[16,1536]{1,0:T(8,128)}) custom-call(f32[1,512,256]{2,1,0:T(8,128)} %get-tuple-element.444.dbc_ref, f32[512,256]{1,0:T(8,128)} %copy-done.20, f32[2,512,256]{2,1,0:T(8,128)} %get-tuple-element.446.pre_ref, ...), custom_call_target="tpu_custom_call" | custom-call | flops 1 | bytes 1 | tf_op jit(solution)/shard_map/small_grads/pallas_call | solution.py:688
  371.8 7.2 %weight_parts.7 = (bf16[1,2,2,384,384]{4,3,2,1,0:T(8,128)(2,1)}, bf16[1,2,2,384,384]{4,3,2,1,0:T(8,128)(2,1)}) custom-call(s32[8]{0:T(128)} %stack.39.refs_0_, bf16[1536,512]{1,0:T(8,128)(2,1)} %get-tuple-element.315.refs_1_.own_turned_ref, bf16[1536,512]{1,0:T(8,128)(2,1)} %collective-permute-done.22.refs_2_.other_turned_ref, ...), custom_call_target="tpu_custom_call" | custom-call | flops 2415919104 | bytes 4718592 | tf_op jit(solution)/shard_map/weight_parts/pallas_call | solution.py:872
  379.0 7.2 %weight_parts.6 = (bf16[1,2,2,384,384]{4,3,2,1,0:T(8,128)(2,1)}, bf16[1,2,2,384,384]{4,3,2,1,0:T(8,128)(2,1)}) custom-call(s32[8]{0:T(128)} %stack.39.refs_0_, bf16[1536,512]{1,0:T(8,128)(2,1)} %get-tuple-element.315.refs_1_.own_turned_ref, bf16[1536,512]{1,0:T(8,128)(2,1)} %collective-permute-done.22.refs_2_.other_turned_ref, ...), custom_call_target="tpu_custom_call" | custom-call | flops 2415919104 | bytes 4718592 | tf_op jit(solution)/shard_map/weight_parts/pallas_call | solution.py:872
  404.3 22.7 %normed_grads.1 = (f32[512,1536]{1,0:T(8,128)}, bf16[512,1536]{1,0:T(8,128)(2,1)}, bf16[1536,384]{1,0:T(8,128)(2,1)}) custom-call(f32[512,256]{1,0:T(8,128)} %get-tuple-element.476.dpre_ref, f32[8,256]{1,0:T(8,128)} %copy-done.62, f32[2,512,8]{2,1,0:T(8,128)} %get-tuple-element.349.refs_1_.flags_ref, f32[8,256]{1,0:T(8,128)} %maximum_maximum_fusion.2.cbc_ref, ...), custom_call_target="tpu_custom_call" | custom-call | flops 9663676416 | bytes 18874368 | tf_op jit(solution)/shard_map/normed_grads/pallas_call | solution.py:741
  443.0 6.4 %collective-permute-done.58 = bf16[1,2,384,384]{3,2,1,0:T(8,128)(2,1)S(1)} collective-permute-done((bf16[1,2,384,384]{3,2,1,0:T(8,128)(2,1)S(1)}, bf16[1,2,384,384]{3,2,1,0:T(8,128)(2,1)S(1)}, u32[]{:S(2)}, u32[]{:S(2)}) %collective-permute-start.58) | collective-permute-done | bytes 589856 | tf_op jit(solution)/shard_map/ppermute | solution.py:897
  453.2 6.2 %x_grads.1 = (f32[512,1536]{1,0:T(8,128)}, f32[8,1536]{1,0:T(8,128)}) custom-call(f32[512,1536]{1,0:T(8,128)} %get-tuple-element.496.own_ref, bf16[512,1536]{1,0:T(8,128)(2,1)} %collective-permute-done.61.came_ref, bf16[512,1536]{1,0:T(8,128)(2,1)} %x_ref.2, bf16[512,1536]{1,0:T(8,128)(2,1)} %cot_ref, f32[1,1536]{1,0:T(1,128)} %reshape.507.gain_ref), custom_call_target="tpu_custom_call" | custom-call | flops 1 | bytes 1 | tf_op jit(solution)/shard_map/x_grads/pallas_call | solution.py:822
  461.2 6.2 %collective-permute-start.60 = (bf16[1,384,384]{2,1,0:T(8,128)(2,1)S(1)}, bf16[1,384,384]{2,1,0:T(8,128)(2,1)S(1)}, u32[]{:S(2)}, u32[]{:S(2)}) collective-permute-start(bf16[1,384,384]{2,1,0:T(8,128)(2,1)S(1)} %get-tuple-element.621), channel_id=1, source_target_pairs={{0,3},{1,0},{2,1},{3,2},{4,7},{5,4},{6,5},{7,6},{8,11},{9,8},{10,9... | collective-permute-start | bytes 884744 | tf_op jit(solution)/shard_map/ppermute | solution.py:903
  500.8 10.6 %branch_parts.1 = (f32[512,1536]{1,0:T(8,128)}, bf16[512,1536]{1,0:T(8,128)(2,1)}) custom-call(bf16[1024,1536]{1,0:T(8,128)(2,1)} %get-tuple-element.517.refs_6_.mixed_ref, bf16[1536,1536]{1,0:T(8,128)(2,1)} %get-tuple-element.518.weight_ref), custom_call_target="tpu_custom_call" | custom-call | flops 4831838208 | bytes 9437184 | tf_op jit(solution)/shard_map/branch_parts/pallas_call | solution.py:780
  (447 shorter events, 222.4 us)
Async XLA Ops:
  81.9 29.5 %collective-permute-start.24 = (bf16[2,384,384]{2,1,0:T(8,128)(2,1)S(1)}, bf16[2,384,384]{2,1,0:T(8,128)(2,1)S(1)}, u32[]{:S(2)}, u32[]{:S(2)}) collective-permute-start(bf16[2,384,384]{2,1,0:T(8,128)(2,1)S(1)} %slice.232.refs_3_), channel_id=1, source_target_pairs={{0,8},{4,12},{8,0},{12,4},{16,24},{20,28},{24,16},{28,20},{1,9},{5... | collective-permute-start | bytes 1769480 | tf_op jit(solution)/shard_map/ppermute | solution.py:897
  82.2 29.3 %collective-permute-start.25 = (bf16[2,384,384]{2,1,0:T(8,128)(2,1)S(1)}, bf16[2,384,384]{2,1,0:T(8,128)(2,1)S(1)}, u32[]{:S(2)}, u32[]{:S(2)}) collective-permute-start(bf16[2,384,384]{2,1,0:T(8,128)(2,1)S(1)} %slice.232.refs_3_), channel_id=1, source_target_pairs={{0,16},{4,20},{8,24},{12,28},{16,0},{20,4},{24,8},{28,12},{1,17},{... | collective-permute-start | bytes 1769480 | tf_op jit(solution)/shard_map/ppermute | solution.py:897
  83.8 27.6 %collective-permute-start.26 = (bf16[2,384,384]{2,1,0:T(8,128)(2,1)S(1)}, bf16[2,384,384]{2,1,0:T(8,128)(2,1)}, u32[]{:S(2)}, u32[]{:S(2)}) collective-permute-start(bf16[2,384,384]{2,1,0:T(8,128)(2,1)S(1)} %slice.232.refs_3_), channel_id=1, source_target_pairs={{0,2},{1,3},{2,0},{3,1},{4,6},{5,7},{6,4},{7,5},{8,10},{9,11},{10,... | collective-permute-start | bytes 1769480 | tf_op jit(solution)/shard_map/ppermute | solution.py:903
  112.2 27.2 %collective-permute-start.33 = (bf16[2,384,384]{2,1,0:T(8,128)(2,1)}, bf16[2,384,384]{2,1,0:T(8,128)(2,1)}, u32[]{:S(2)}, u32[]{:S(2)}) collective-permute-start(bf16[2,384,384]{2,1,0:T(8,128)(2,1)} %collective-permute-done.17.refs_7_), channel_id=1, source_target_pairs={{0,8},{4,12},{8,0},{12,4},{16,24},{20,28},{24,16},{28,20},{1,9},{5... | collective-permute-start | bytes 1769480 | tf_op jit(solution)/shard_map/ppermute | solution.py:897
  139.3 31.0 %collective-permute-start.36 = (bf16[2,384,384]{2,1,0:T(8,128)(2,1)}, bf16[2,384,384]{2,1,0:T(8,128)(2,1)}, u32[]{:S(2)}, u32[]{:S(2)}) collective-permute-start(bf16[2,384,384]{2,1,0:T(8,128)(2,1)} %collective-permute-done.35.refs_15_), channel_id=1, source_target_pairs={{0,16},{4,20},{8,24},{12,28},{16,0},{20,4},{24,8},{28,12},{1,17},{... | collective-permute-start | bytes 1769480 | tf_op jit(solution)/shard_map/ppermute | solution.py:897
  141.0 29.9 %collective-permute-start.37 = (bf16[2,384,384]{2,1,0:T(8,128)(2,1)}, bf16[2,384,384]{2,1,0:T(8,128)(2,1)S(1)}, u32[]{:S(2)}, u32[]{:S(2)}) collective-permute-start(bf16[2,384,384]{2,1,0:T(8,128)(2,1)} %collective-permute-done.26.refs_11_), channel_id=1, source_target_pairs={{0,16},{4,20},{8,24},{12,28},{16,0},{20,4},{24,8},{28,12},{1,17},{... | collective-permute-start | bytes 1769480 | tf_op jit(solution)/shard_map/ppermute | solution.py:897
  141.4 29.6 %collective-permute-start.38 = (bf16[2,384,384]{2,1,0:T(8,128)(2,1)}, bf16[2,384,384]{2,1,0:T(8,128)(2,1)S(1)}, u32[]{:S(2)}, u32[]{:S(2)}) collective-permute-start(bf16[2,384,384]{2,1,0:T(8,128)(2,1)} %collective-permute-done.35.refs_15_), channel_id=1, source_target_pairs={{0,8},{4,12},{8,0},{12,4},{16,24},{20,28},{24,16},{28,20},{1,9},{5... | collective-permute-start | bytes 1769480 | tf_op jit(solution)/shard_map/ppermute | solution.py:897
  143.0 28.1 %collective-permute-start.39 = (bf16[2,384,384]{2,1,0:T(8,128)(2,1)}, bf16[2,384,384]{2,1,0:T(8,128)(2,1)S(1)}, u32[]{:S(2)}, u32[]{:S(2)}) collective-permute-start(bf16[2,384,384]{2,1,0:T(8,128)(2,1)} %collective-permute-done.31.refs_9_), channel_id=1, source_target_pairs={{0,8},{4,12},{8,0},{12,4},{16,24},{20,28},{24,16},{28,20},{1,9},{5... | collective-permute-start | bytes 1769480 | tf_op jit(solution)/shard_map/ppermute | solution.py:897
  143.5 58.6 %collective-permute-start.43 = (bf16[512,1536]{1,0:T(8,128)(2,1)S(1)}, bf16[512,1536]{1,0:T(8,128)(2,1)}, u32[]{:S(2)}, u32[]{:S(2)}) collective-permute-start(bf16[512,1536]{1,0:T(8,128)(2,1)S(1)} %copy-done.3), channel_id=1, source_target_pairs={{0,4},{4,0},{8,12},{12,8},{16,20},{20,16},{24,28},{28,24},{1,5},{5... | collective-permute-start | bytes 4718600 | tf_op jit(solution)/shard_map/ppermute | solution.py:892
  170.3 81.9 %collective-permute-start.23 = (bf16[1536,512]{1,0:T(8,128)(2,1)}, bf16[1536,512]{1,0:T(8,128)(2,1)}, u32[]{:S(2)}, u32[]{:S(2)}) collective-permute-start(bf16[1536,512]{1,0:T(8,128)(2,1)} %turn.1.refs_3_), channel_id=1, source_target_pairs={{0,4},{4,0},{8,12},{12,8},{16,20},{20,16},{24,28},{28,24},{1,5},{5... | collective-permute-start | bytes 4718600 | tf_op jit(solution)/shard_map/ppermute | solution.py:892
  170.9 81.4 %collective-permute-start.22 = (bf16[1536,512]{1,0:T(8,128)(2,1)}, bf16[1536,512]{1,0:T(8,128)(2,1)}, u32[]{:S(2)}, u32[]{:S(2)}) collective-permute-start(bf16[1536,512]{1,0:T(8,128)(2,1)} %get-tuple-element.315.refs_1_.own_turned_ref), channel_id=1, source_target_pairs={{0,4},{4,0},{8,12},{12,8},{16,20},{20,16},{24,28},{28,24},{1,5},{5... | collective-permute-start | bytes 4718600 | tf_op jit(solution)/shard_map/ppermute | solution.py:892
  187.0 27.9 %collective-permute-start.40 = (bf16[2,128,1536]{2,1,0:T(8,128)(2,1)S(1)}, bf16[2,128,1536]{2,1,0:T(8,128)(2,1)S(1)}, u32[]{:S(2)}, u32[]{:S(2)}) collective-permute-start(bf16[2,128,1536]{2,1,0:T(8,128)(2,1)S(1)} %fusion.3), channel_id=1, source_target_pairs={{0,1},{2,3},{4,5},{6,7},{8,9},{10,11},{12,13},{14,15},{16,17},{18,... | collective-permute-start | bytes 2359304 | tf_op jit(solution)/shard_map/ppermute | solution.py:911
  280.3 72.1 %collective-permute-start.46 = (bf16[2,2,2,384,384]{4,3,0,1,2:T(8,128)(2,1)}, bf16[2,2,2,384,384]{4,3,0,1,2:T(8,128)(2,1)}, u32[]{:S(2)}, u32[]{:S(2)}) collective-permute-start(bf16[2,2,2,384,384]{4,3,0,1,2:T(8,128)(2,1)} %copy.100), channel_id=1, source_target_pairs={{0,16},{4,20},{8,24},{12,28},{16,0},{20,4},{24,8},{28,12},{1,17},{... | collective-permute-start | bytes 7077896 | tf_op jit(solution)/shard_map/ppermute | solution.py:897
  281.4 71.1 %collective-permute-start.47 = (bf16[2,2,2,384,384]{4,3,2,1,0:T(8,128)(2,1)}, bf16[2,2,2,384,384]{4,3,2,1,0:T(8,128)(2,1)}, u32[]{:S(2)}, u32[]{:S(2)}) collective-permute-start(bf16[2,2,2,384,384]{4,3,2,1,0:T(8,128)(2,1)} %get-tuple-element.420), channel_id=1, source_target_pairs={{0,8},{4,12},{8,0},{12,4},{16,24},{20,28},{24,16},{28,20},{1,9},{5... | collective-permute-start | bytes 7077896 | tf_op jit(solution)/shard_map/ppermute | solution.py:897
  317.4 35.0 %collective-permute-start.48 = (f32[512,256]{1,0:T(8,128)}, f32[512,256]{1,0:T(8,128)S(1)}, u32[]{:S(2)}, u32[]{:S(2)}) collective-permute-start(f32[512,256]{1,0:T(8,128)} %bitcast.208), channel_id=1, source_target_pairs={{0,4},{4,0},{8,12},{12,8},{16,20},{20,16},{24,28},{28,24},{1,5},{5... | collective-permute-start | bytes 1572872 | tf_op jit(solution)/shard_map/ppermute | solution.py:892
  319.1 33.3 %collective-permute-start.49 = (f32[1,8,1536]{2,1,0:T(8,128)}, f32[1,8,1536]{2,1,0:T(8,128)S(1)}, u32[]{:S(2)}, u32[]{:S(2)}) collective-permute-start(f32[1,8,1536]{2,1,0:T(8,128)} %get-tuple-element.425), channel_id=1, source_target_pairs={{1,0},{3,2},{5,4},{7,6},{9,8},{11,10},{13,12},{15,14},{17,16},{19,... | collective-permute-start | bytes 147464 | tf_op jit(solution)/shard_map/ppermute | solution.py:911
  355.0 31.2 %collective-permute-start.52 = (bf16[2,2,384,384]{3,2,1,0:T(8,128)(2,1)S(1)}, bf16[2,2,384,384]{3,2,1,0:T(8,128)(2,1)S(1)}, u32[]{:S(2)}, u32[]{:S(2)}) collective-permute-start(bf16[2,2,384,384]{3,2,1,0:T(8,128)(2,1)S(1)} %fusion.1), channel_id=1, source_target_pairs={{0,16},{4,20},{8,24},{12,28},{16,0},{20,4},{24,8},{28,12},{1,17},{... | collective-permute-start | bytes 3538952 | tf_op jit(solution)/shard_map/ppermute | solution.py:897
  359.1 28.3 %collective-permute-start.51 = (bf16[2,2,384,384]{3,2,0,1:T(8,128)(2,1)S(1)}, bf16[2,2,384,384]{3,2,0,1:T(8,128)(2,1)}, u32[]{:S(2)}, u32[]{:S(2)}) collective-permute-start(bf16[2,2,384,384]{3,2,0,1:T(8,128)(2,1)S(1)} %fusion), channel_id=1, source_target_pairs={{0,8},{4,12},{8,0},{12,4},{16,24},{20,28},{24,16},{28,20},{1,9},{5... | collective-permute-start | bytes 3538952 | tf_op jit(solution)/shard_map/ppermute | solution.py:897
  390.8 36.3 %collective-permute-start.57 = (bf16[2,384,384]{2,1,0:T(8,128)(2,1)}, bf16[2,384,384]{2,1,0:T(8,128)(2,1)}, u32[]{:S(2)}, u32[]{:S(2)}) collective-permute-start(bf16[2,384,384]{2,1,0:T(8,128)(2,1)} %fusion.49), channel_id=1, source_target_pairs={{0,2},{1,3},{2,0},{3,1},{4,6},{5,7},{6,4},{7,5},{8,10},{9,11},{10,... | collective-permute-start | bytes 1769480 | tf_op jit(solution)/shard_map/ppermute | solution.py:903
  397.1 30.0 %collective-permute-start.56 = (bf16[2,384,384]{2,1,0:T(8,128)(2,1)}, bf16[2,384,384]{2,1,0:T(8,128)(2,1)}, u32[]{:S(2)}, u32[]{:S(2)}) collective-permute-start(bf16[2,384,384]{2,1,0:T(8,128)(2,1)} %get-tuple-element.616), channel_id=1, source_target_pairs={{0,3},{1,0},{2,1},{3,2},{4,7},{5,4},{6,5},{7,6},{8,11},{9,8},{10,9... | collective-permute-start | bytes 1769480 | tf_op jit(solution)/shard_map/ppermute | solution.py:903
  402.0 27.7 %collective-permute-start.54 = (bf16[1,2,2,384,384]{4,3,1,2,0:T(8,128)(2,1)}, bf16[1,2,2,384,384]{4,3,1,2,0:T(8,128)(2,1)}, u32[]{:S(2)}, u32[]{:S(2)}) collective-permute-start(bf16[1,2,2,384,384]{4,3,1,2,0:T(8,128)(2,1)} %copy.105), channel_id=1, source_target_pairs={{0,16},{4,20},{8,24},{12,28},{16,0},{20,4},{24,8},{28,12},{1,17},{... | collective-permute-start | bytes 3538952 | tf_op jit(solution)/shard_map/ppermute | solution.py:897
  403.0 27.4 %collective-permute-start.55 = (bf16[1,2,2,384,384]{4,3,2,1,0:T(8,128)(2,1)}, bf16[1,2,2,384,384]{4,3,2,1,0:T(8,128)(2,1)}, u32[]{:S(2)}, u32[]{:S(2)}) collective-permute-start(bf16[1,2,2,384,384]{4,3,2,1,0:T(8,128)(2,1)} %get-tuple-element.475), channel_id=1, source_target_pairs={{0,8},{4,12},{8,0},{12,4},{16,24},{20,28},{24,16},{28,20},{1,9},{5... | collective-permute-start | bytes 3538952 | tf_op jit(solution)/shard_map/ppermute | solution.py:897
  437.0 35.8 %collective-permute-start.66 = (bf16[2,384,384]{2,1,0:T(8,128)(2,1)}, bf16[2,384,384]{2,1,0:T(8,128)(2,1)}, u32[]{:S(2)}, u32[]{:S(2)}) collective-permute-start(bf16[2,384,384]{2,1,0:T(8,128)(2,1)} %get-tuple-element.503), channel_id=1, source_target_pairs={{0,1},{1,2},{2,3},{3,0},{4,5},{5,6},{6,7},{7,4},{8,9},{9,10},{10,1... | collective-permute-start | bytes 1769480 | tf_op jit(solution)/shard_map/ppermute | solution.py:903
  442.4 26.6 %collective-permute-start.65 = (bf16[2,192,384]{2,1,0:T(8,128)(2,1)}, bf16[2,192,384]{2,1,0:T(8,128)(2,1)}, u32[]{:S(2)}, u32[]{:S(2)}) collective-permute-start(bf16[2,192,384]{2,1,0:T(8,128)(2,1)} %dynamic-slice_bitcast_fusion.2), channel_id=1, source_target_pairs={{0,8},{4,12},{8,0},{12,4},{16,24},{20,28},{24,16},{28,20},{1,9},{5... | collective-permute-start | bytes 884744 | tf_op jit(solution)/shard_map/ppermute | solution.py:897
  (120 other events, 1244.9 us)
